TPU v7x, 128 devices: a whole 4x4x4 slice. The times are simulated.
128 devices in a mesh: rows: 64 (over y, z, x), cols: 2 (over core).
Axes of the slice: x: 4, y: 4, z: 4, core: 2. Of those that a mesh axis runs over, the one named last changes fastest.
Arguments:
- video: bfloat16 [512, 256, 256], P('rows', 'cols'), may hold values from -12 to 12
- foreground: float32 [512, 256, 256], P('rows', 'cols'), may hold values from -4 to 4
- scaled_dual: float32 [512, 256, 256], P('rows', 'cols'), may hold values from -2.5 to 2.5
Outputs:
- background: float32 [512, 256, 256], P('rows', 'cols')
- new_foreground: float32 [512, 256, 256], P('rows', 'cols')
- new_dual: float32 [512, 256, 256], P('rows', 'cols')
All inputs are finite; a program needn't handle non-finite values.
Results may differ from a plain program's by a relative error of at most 0.00035.
Values sent between devices are 32-bit elements; how exact they have to be, the bound alone decides.
A program may use at most 64 MiB of HBM per device.

v0:
```python
import jax
import jax.numpy as jnp
from jax import lax
from jax.sharding import PartitionSpec as P

K_ROOT = 8
K_SIGN = 6
K_TV = 8


threshold_ratio = 1.0
dual_step = 0.25
tv_weight = 1.0


def shifted(x, axis, by):
    length = lax.axis_size(axis)
    pairs = [(i, i + by) for i in range(length) if 0 <= i + by < length]
    return lax.ppermute(x, axis, pairs)


def matmul(left, right):
    return jnp.dot(left, right, precision=lax.Precision.HIGHEST, preferred_element_type=jnp.float32)


def shrink_matrix(gram):
    size = gram.shape[0]
    identity = jnp.eye(size, dtype=jnp.float32)
    scale = jnp.sqrt(jnp.sum(gram * gram))
    root = gram / scale
    inverse = identity
    for sweep in range(K_ROOT):
        factor = 1.5 * identity - 0.5 * matmul(inverse, root)
        root = matmul(root, factor)
        inverse = matmul(factor, inverse)
    cutoff = threshold_ratio * jnp.trace(root) / size
    signed = root - cutoff * identity
    for sweep in range(K_SIGN):
        signed = 1.5 * signed - 0.5 * matmul(signed, matmul(signed, signed))
    return 0.5 * matmul(identity - cutoff * inverse, identity + signed)


def per_device(video, foreground, scaled_dual):
    rows_here, cols_here, frames = foreground.shape
    observed = video.astype(jnp.float32)
    mixed = observed - foreground + scaled_dual
    flat = mixed.reshape(-1, frames)
    gram = lax.psum(matmul(flat.T, flat), ("rows", "cols"))
    shrink = shrink_matrix(gram)
    background = matmul(flat, shrink).reshape(foreground.shape)
    target = observed - background + scaled_dual
    last_row = lax.axis_index("rows") == lax.axis_size("rows") - 1
    last_col = lax.axis_index("cols") == lax.axis_size("cols") - 1
    row_iota = lax.broadcasted_iota(jnp.int32, (rows_here, 1, 1), 0)
    col_iota = lax.broadcasted_iota(jnp.int32, (1, cols_here, 1), 1)
    row_keep = jnp.where(last_row & (row_iota == rows_here - 1), 0.0, 1.0).astype(jnp.float32)
    col_keep = jnp.where(last_col & (col_iota == cols_here - 1), 0.0, 1.0).astype(jnp.float32)
    dual_x = jnp.zeros_like(target)
    dual_y = jnp.zeros_like(target)

    def current_of(px, py):
        prev_x = shifted(px[-1:], "rows", 1)
        prev_y = shifted(py[:, -1:], "cols", 1)
        before_x = jnp.concatenate([prev_x, px[:-1]], axis=0)
        before_y = jnp.concatenate([prev_y, py[:, :-1]], axis=1)
        return target - (before_x - px + before_y - py)

    for sweep in range(K_TV):
        current = current_of(dual_x, dual_y)
        below = shifted(current[:1], "rows", -1)
        beside = shifted(current[:, :1], "cols", -1)
        down = (jnp.concatenate([current[1:], below], axis=0) - current) * row_keep
        across = (jnp.concatenate([current[:, 1:], beside], axis=1) - current) * col_keep
        dual_x = jnp.clip(dual_x + dual_step * down, -tv_weight, tv_weight)
        dual_y = jnp.clip(dual_y + dual_step * across, -tv_weight, tv_weight)
    new_foreground = current_of(dual_x, dual_y)
    new_dual = scaled_dual + observed - background - new_foreground
    return (background, new_foreground, new_dual)


def solution(mesh):
    return jax.shard_map(
        per_device,
        mesh=mesh,
        in_specs=(P("rows", "cols", None), P("rows", "cols", None), P("rows", "cols", None)),
        out_specs=(P("rows", "cols", None), P("rows", "cols", None), P("rows", "cols", None)),
        check_vma=False,
    )
```

profile of v0, /device:TPU:8, one launch (start us, length us, event | category | flops | bytes accessed | tf_op | source)
XLA Modules:
  0.0 340.7 jit_solution(16229040897291042421)
XLA Ops:
  7.2 5.1 %convolution_bitcast_fusion = f32[256,256]{1,0:T(8,128)} fusion(f32[8,128,256]{2,1,0:T(8,128)} %param.5, f32[8,128,256]{2,1,0:T(8,128)} %param.4, bf16[8,128,256]{2,1,0:T(8,128)(2,1)} %param.3), kind=kOutput, calls=%fused_computation.36 | convolution fusion | flops 806092800 | bytes 2883584 | tf_op jit(solution)/shard_map/dot_general | solution.py:23
  12.4 1.7 collective-permute-start.1
  14.1 3.4 collective-permute-start
  17.5 140.5 %all-reduce.4.cloned.1.call-done = f32[256,256]{1,0:T(8,128)} async-done(((f32[256,256]{1,0:T(8,128)}), f32[256,256]{1,0:T(8,128)}) %all-reduce.4.cloned.1.call-update) | async-done | bytes 262160 | tf_op jit(solution)/shard_map/psum | solution.py:48
  158.1 1.7 multiply_reduce_fusion
  168.8 1.0 select_reduce_fusion
  176.9 2.0 add_subtract_fusion
  178.9 5.3 %collective-permute-start.2 = (f32[1,128,256]{2,1,0:T(8,128)S(1)}, f32[1,128,256]{2,1,0:T(8,128)S(1)}, u32[]{:S(2)}, u32[]{:S(2)}) collective-permute-start(f32[1,128,256]{2,1,0:T(8,128)S(1)} %slice.267), channel_id=1, source_target_pairs={{2,0},{4,2},{6,4},{8,6},{10,8},{12,10},{14,12},{16,14},{18,16},{20... | collective-permute-start | bytes 393224 | tf_op jit(solution)/shard_map/ppermute | solution.py:19
  184.2 1.3 collective-permute-start.4
  185.7 1.6 collective-permute-done.4
  187.7 2.1 collective-permute-start.3
  189.9 1.9 collective-permute-start.5
  191.8 0.7 collective-permute-done.5
  192.6 6.8 %collective-permute-done.3 = f32[1,128,256]{2,1,0:T(8,128)S(1)} collective-permute-done((f32[1,128,256]{2,1,0:T(8,128)S(1)}, f32[1,128,256]{2,1,0:T(8,128)S(1)}, u32[]{:S(2)}, u32[]{:S(2)}) %collective-permute-start.3) | collective-permute-done | bytes 131104 | tf_op jit(solution)/shard_map/ppermute | solution.py:19
  199.8 3.5 %collective-permute-start.6 = (f32[1,128,256]{2,1,0:T(8,128)S(1)}, f32[1,128,256]{2,1,0:T(8,128)S(1)}, u32[]{:S(2)}, u32[]{:S(2)}) collective-permute-start(f32[1,128,256]{2,1,0:T(8,128)S(1)} %slice.275), channel_id=1, source_target_pairs={{2,0},{4,2},{6,4},{8,6},{10,8},{12,10},{14,12},{16,14},{18,16},{20... | collective-permute-start | bytes 393224 | tf_op jit(solution)/shard_map/ppermute | solution.py:19
  203.4 1.3 collective-permute-start.8
  204.9 1.6 collective-permute-done.8
  207.2 2.1 collective-permute-start.7
  209.3 1.8 collective-permute-start.9
  211.2 0.7 collective-permute-done.9
  211.9 6.7 %collective-permute-done.7 = f32[1,128,256]{2,1,0:T(8,128)S(1)} collective-permute-done((f32[1,128,256]{2,1,0:T(8,128)S(1)}, f32[1,128,256]{2,1,0:T(8,128)S(1)}, u32[]{:S(2)}, u32[]{:S(2)}) %collective-permute-start.7) | collective-permute-done | bytes 131104 | tf_op jit(solution)/shard_map/ppermute | solution.py:19
  219.0 3.2 collective-permute-start.10
  222.2 1.3 collective-permute-start.12
  223.7 1.6 collective-permute-done.12
  226.4 2.1 collective-permute-start.11
  228.5 1.8 collective-permute-start.13
  230.4 0.7 collective-permute-done.13
  231.1 6.4 %collective-permute-done.11 = f32[1,128,256]{2,1,0:T(8,128)S(1)} collective-permute-done((f32[1,128,256]{2,1,0:T(8,128)S(1)}, f32[1,128,256]{2,1,0:T(8,128)S(1)}, u32[]{:S(2)}, u32[]{:S(2)}) %collective-permute-start.11) | collective-permute-done | bytes 131104 | tf_op jit(solution)/shard_map/ppermute | solution.py:19
  237.9 3.2 collective-permute-start.14
  241.1 1.3 collective-permute-start.16
  242.6 1.6 collective-permute-done.16
  245.3 2.1 collective-permute-start.15
  247.4 1.8 collective-permute-start.17
  249.3 0.7 collective-permute-done.17
  250.0 6.4 %collective-permute-done.15 = f32[1,128,256]{2,1,0:T(8,128)S(1)} collective-permute-done((f32[1,128,256]{2,1,0:T(8,128)S(1)}, f32[1,128,256]{2,1,0:T(8,128)S(1)}, u32[]{:S(2)}, u32[]{:S(2)}) %collective-permute-start.15) | collective-permute-done | bytes 131104 | tf_op jit(solution)/shard_map/ppermute | solution.py:19
  256.7 3.2 collective-permute-start.18
  259.9 1.3 collective-permute-start.20
  261.4 1.6 collective-permute-done.20
  264.1 2.1 collective-permute-start.19
  266.2 1.8 collective-permute-start.21
  268.1 0.7 collective-permute-done.21
  268.8 6.4 %collective-permute-done.19 = f32[1,128,256]{2,1,0:T(8,128)S(1)} collective-permute-done((f32[1,128,256]{2,1,0:T(8,128)S(1)}, f32[1,128,256]{2,1,0:T(8,128)S(1)}, u32[]{:S(2)}, u32[]{:S(2)}) %collective-permute-start.19) | collective-permute-done | bytes 131104 | tf_op jit(solution)/shard_map/ppermute | solution.py:19
  275.6 3.2 collective-permute-start.22
  278.8 1.3 collective-permute-start.24
  280.3 1.6 collective-permute-done.24
  283.0 2.1 collective-permute-start.23
  285.1 1.8 collective-permute-start.25
  287.0 0.7 collective-permute-done.25
  287.7 6.4 %collective-permute-done.23 = f32[1,128,256]{2,1,0:T(8,128)S(1)} collective-permute-done((f32[1,128,256]{2,1,0:T(8,128)S(1)}, f32[1,128,256]{2,1,0:T(8,128)S(1)}, u32[]{:S(2)}, u32[]{:S(2)}) %collective-permute-start.23) | collective-permute-done | bytes 131104 | tf_op jit(solution)/shard_map/ppermute | solution.py:19
  294.4 3.2 collective-permute-start.26
  297.6 1.3 collective-permute-start.28
  299.1 1.6 collective-permute-done.28
  301.8 2.1 collective-permute-start.27
  303.9 1.8 collective-permute-start.29
  305.8 0.7 collective-permute-done.29
  306.5 6.4 %collective-permute-done.27 = f32[1,128,256]{2,1,0:T(8,128)S(1)} collective-permute-done((f32[1,128,256]{2,1,0:T(8,128)S(1)}, f32[1,128,256]{2,1,0:T(8,128)S(1)}, u32[]{:S(2)}, u32[]{:S(2)}) %collective-permute-start.27) | collective-permute-done | bytes 131104 | tf_op jit(solution)/shard_map/ppermute | solution.py:19
  313.3 3.2 collective-permute-start.30
  316.5 1.3 collective-permute-start.32
  318.0 1.6 collective-permute-done.32
  320.7 2.2 collective-permute-start.31
  323.0 1.9 collective-permute-start.33
  325.0 0.7 collective-permute-done.33
  325.7 6.2 %collective-permute-done.31 = f32[1,128,256]{2,1,0:T(8,128)S(1)} collective-permute-done((f32[1,128,256]{2,1,0:T(8,128)S(1)}, f32[1,128,256]{2,1,0:T(8,128)S(1)}, u32[]{:S(2)}, u32[]{:S(2)}) %collective-permute-start.31) | collective-permute-done | bytes 131104 | tf_op jit(solution)/shard_map/ppermute | solution.py:19
  332.0 1.9 fusion.20
  (135 shorter events, 27.2 us)
Async XLA Ops:
  7.2 150.9 %all-reduce.4.cloned.1.call-start = ((), (), s32[]{:S(2)}) async-start(), calls=%async_computation | async-start | bytes 524288 | tf_op jit(solution)/shard_map/psum | solution.py:48
  12.4 163.8 %collective-permute-start.1 = (f32[8,1,256]{2,1,0:T(1,128)S(1)}, f32[8,1,256]{2,1,0:T(1,128)S(1)}, u32[]{:S(2)}, u32[]{:S(2)}) collective-permute-start(f32[8,1,256]{2,1,0:T(1,128)S(1)} %slice.201), channel_id=1, source_target_pairs={{0,1},{2,3},{4,5},{6,7},{8,9},{10,11},{12,13},{14,15},{16,17},{18,... | collective-permute-start | bytes 24584 | tf_op jit(solution)/shard_map/ppermute | solution.py:19
  14.1 162.0 %collective-permute-start = (f32[1,128,256]{2,1,0:T(8,128)S(1)}, f32[1,128,256]{2,1,0:T(8,128)S(1)}, u32[]{:S(2)}, u32[]{:S(2)}) collective-permute-start(f32[1,128,256]{2,1,0:T(8,128)S(1)} %slice.200), channel_id=1, source_target_pairs={{0,2},{2,4},{4,6},{6,8},{8,10},{10,12},{12,14},{14,16},{16,18},{18... | collective-permute-start | bytes 393224 | tf_op jit(solution)/shard_map/ppermute | solution.py:19
  158.1 2.4 copy-start.5
  174.4 1.8 copy-start.3
  175.0 1.3 copy-start
  175.8 1.1 copy-start.1
  178.9 8.4 %collective-permute-start.2 = (f32[1,128,256]{2,1,0:T(8,128)S(1)}, f32[1,128,256]{2,1,0:T(8,128)S(1)}, u32[]{:S(2)}, u32[]{:S(2)}) collective-permute-start(f32[1,128,256]{2,1,0:T(8,128)S(1)} %slice.267), channel_id=1, source_target_pairs={{2,0},{4,2},{6,4},{8,6},{10,8},{12,10},{14,12},{16,14},{18,16},{20... | collective-permute-start | bytes 393224 | tf_op jit(solution)/shard_map/ppermute | solution.py:19
  184.2 3.1 collective-permute-start.4
  187.7 11.7 %collective-permute-start.3 = (f32[1,128,256]{2,1,0:T(8,128)S(1)}, f32[1,128,256]{2,1,0:T(8,128)S(1)}, u32[]{:S(2)}, u32[]{:S(2)}) collective-permute-start(f32[1,128,256]{2,1,0:T(8,128)S(1)} %slice.268), channel_id=1, source_target_pairs={{0,2},{2,4},{4,6},{6,8},{8,10},{10,12},{12,14},{14,16},{16,18},{18... | collective-permute-start | bytes 393224 | tf_op jit(solution)/shard_map/ppermute | solution.py:19
  189.9 2.7 collective-permute-start.5
  199.8 6.9 %collective-permute-start.6 = (f32[1,128,256]{2,1,0:T(8,128)S(1)}, f32[1,128,256]{2,1,0:T(8,128)S(1)}, u32[]{:S(2)}, u32[]{:S(2)}) collective-permute-start(f32[1,128,256]{2,1,0:T(8,128)S(1)} %slice.275), channel_id=1, source_target_pairs={{2,0},{4,2},{6,4},{8,6},{10,8},{12,10},{14,12},{16,14},{18,16},{20... | collective-permute-start | bytes 393224 | tf_op jit(solution)/shard_map/ppermute | solution.py:19
  203.4 3.1 collective-permute-start.8
  207.2 11.5 %collective-permute-start.7 = (f32[1,128,256]{2,1,0:T(8,128)S(1)}, f32[1,128,256]{2,1,0:T(8,128)S(1)}, u32[]{:S(2)}, u32[]{:S(2)}) collective-permute-start(f32[1,128,256]{2,1,0:T(8,128)S(1)} %slice.276), channel_id=1, source_target_pairs={{0,2},{2,4},{4,6},{6,8},{8,10},{10,12},{12,14},{14,16},{16,18},{18... | collective-permute-start | bytes 393224 | tf_op jit(solution)/shard_map/ppermute | solution.py:19
  209.3 2.6 collective-permute-start.9
  219.0 6.9 %collective-permute-start.10 = (f32[1,128,256]{2,1,0:T(8,128)S(1)}, f32[1,128,256]{2,1,0:T(8,128)S(1)}, u32[]{:S(2)}, u32[]{:S(2)}) collective-permute-start(f32[1,128,256]{2,1,0:T(8,128)S(1)} %slice.283), channel_id=1, source_target_pairs={{2,0},{4,2},{6,4},{8,6},{10,8},{12,10},{14,12},{16,14},{18,16},{20... | collective-permute-start | bytes 393224 | tf_op jit(solution)/shard_map/ppermute | solution.py:19
  222.2 3.1 collective-permute-start.12
  226.4 11.1 %collective-permute-start.11 = (f32[1,128,256]{2,1,0:T(8,128)S(1)}, f32[1,128,256]{2,1,0:T(8,128)S(1)}, u32[]{:S(2)}, u32[]{:S(2)}) collective-permute-start(f32[1,128,256]{2,1,0:T(8,128)S(1)} %slice.284), channel_id=1, source_target_pairs={{0,2},{2,4},{4,6},{6,8},{8,10},{10,12},{12,14},{14,16},{16,18},{18... | collective-permute-start | bytes 393224 | tf_op jit(solution)/shard_map/ppermute | solution.py:19
  228.5 2.6 collective-permute-start.13
  237.9 6.9 %collective-permute-start.14 = (f32[1,128,256]{2,1,0:T(8,128)S(1)}, f32[1,128,256]{2,1,0:T(8,128)S(1)}, u32[]{:S(2)}, u32[]{:S(2)}) collective-permute-start(f32[1,128,256]{2,1,0:T(8,128)S(1)} %slice.291), channel_id=1, source_target_pairs={{2,0},{4,2},{6,4},{8,6},{10,8},{12,10},{14,12},{16,14},{18,16},{20... | collective-permute-start | bytes 393224 | tf_op jit(solution)/shard_map/ppermute | solution.py:19
  241.1 3.1 collective-permute-start.16
  245.3 11.1 %collective-permute-start.15 = (f32[1,128,256]{2,1,0:T(8,128)S(1)}, f32[1,128,256]{2,1,0:T(8,128)S(1)}, u32[]{:S(2)}, u32[]{:S(2)}) collective-permute-start(f32[1,128,256]{2,1,0:T(8,128)S(1)} %slice.292), channel_id=1, source_target_pairs={{0,2},{2,4},{4,6},{6,8},{8,10},{10,12},{12,14},{14,16},{16,18},{18... | collective-permute-start | bytes 393224 | tf_op jit(solution)/shard_map/ppermute | solution.py:19
  247.4 2.6 collective-permute-start.17
  256.7 6.9 %collective-permute-start.18 = (f32[1,128,256]{2,1,0:T(8,128)S(1)}, f32[1,128,256]{2,1,0:T(8,128)S(1)}, u32[]{:S(2)}, u32[]{:S(2)}) collective-permute-start(f32[1,128,256]{2,1,0:T(8,128)S(1)} %slice.299), channel_id=1, source_target_pairs={{2,0},{4,2},{6,4},{8,6},{10,8},{12,10},{14,12},{16,14},{18,16},{20... | collective-permute-start | bytes 393224 | tf_op jit(solution)/shard_map/ppermute | solution.py:19
  259.9 3.1 collective-permute-start.20
  264.1 11.1 %collective-permute-start.19 = (f32[1,128,256]{2,1,0:T(8,128)S(1)}, f32[1,128,256]{2,1,0:T(8,128)S(1)}, u32[]{:S(2)}, u32[]{:S(2)}) collective-permute-start(f32[1,128,256]{2,1,0:T(8,128)S(1)} %slice.300), channel_id=1, source_target_pairs={{0,2},{2,4},{4,6},{6,8},{8,10},{10,12},{12,14},{14,16},{16,18},{18... | collective-permute-start | bytes 393224 | tf_op jit(solution)/shard_map/ppermute | solution.py:19
  266.2 2.6 collective-permute-start.21
  275.6 6.9 %collective-permute-start.22 = (f32[1,128,256]{2,1,0:T(8,128)S(1)}, f32[1,128,256]{2,1,0:T(8,128)S(1)}, u32[]{:S(2)}, u32[]{:S(2)}) collective-permute-start(f32[1,128,256]{2,1,0:T(8,128)S(1)} %slice.307), channel_id=1, source_target_pairs={{2,0},{4,2},{6,4},{8,6},{10,8},{12,10},{14,12},{16,14},{18,16},{20... | collective-permute-start | bytes 393224 | tf_op jit(solution)/shard_map/ppermute | solution.py:19
  278.8 3.1 collective-permute-start.24
  283.0 11.1 %collective-permute-start.23 = (f32[1,128,256]{2,1,0:T(8,128)S(1)}, f32[1,128,256]{2,1,0:T(8,128)S(1)}, u32[]{:S(2)}, u32[]{:S(2)}) collective-permute-start(f32[1,128,256]{2,1,0:T(8,128)S(1)} %slice.308), channel_id=1, source_target_pairs={{0,2},{2,4},{4,6},{6,8},{8,10},{10,12},{12,14},{14,16},{16,18},{18... | collective-permute-start | bytes 393224 | tf_op jit(solution)/shard_map/ppermute | solution.py:19
  285.1 2.6 collective-permute-start.25
  294.4 6.9 %collective-permute-start.26 = (f32[1,128,256]{2,1,0:T(8,128)S(1)}, f32[1,128,256]{2,1,0:T(8,128)S(1)}, u32[]{:S(2)}, u32[]{:S(2)}) collective-permute-start(f32[1,128,256]{2,1,0:T(8,128)S(1)} %slice.315), channel_id=1, source_target_pairs={{2,0},{4,2},{6,4},{8,6},{10,8},{12,10},{14,12},{16,14},{18,16},{20... | collective-permute-start | bytes 393224 | tf_op jit(solution)/shard_map/ppermute | solution.py:19
  297.6 3.1 collective-permute-start.28
  301.8 11.1 %collective-permute-start.27 = (f32[1,128,256]{2,1,0:T(8,128)S(1)}, f32[1,128,256]{2,1,0:T(8,128)S(1)}, u32[]{:S(2)}, u32[]{:S(2)}) collective-permute-start(f32[1,128,256]{2,1,0:T(8,128)S(1)} %slice.316), channel_id=1, source_target_pairs={{0,2},{2,4},{4,6},{6,8},{8,10},{10,12},{12,14},{14,16},{16,18},{18... | collective-permute-start | bytes 393224 | tf_op jit(solution)/shard_map/ppermute | solution.py:19
  303.9 2.6 collective-permute-start.29
  313.3 6.9 %collective-permute-start.30 = (f32[1,128,256]{2,1,0:T(8,128)S(1)}, f32[1,128,256]{2,1,0:T(8,128)S(1)}, u32[]{:S(2)}, u32[]{:S(2)}) collective-permute-start(f32[1,128,256]{2,1,0:T(8,128)S(1)} %slice.323), channel_id=1, source_target_pairs={{2,0},{4,2},{6,4},{8,6},{10,8},{12,10},{14,12},{16,14},{18,16},{20... | collective-permute-start | bytes 393224 | tf_op jit(solution)/shard_map/ppermute | solution.py:19
  316.5 3.1 collective-permute-start.32
  320.7 11.2 %copy-start.4 = (f32[8,128,256]{2,1,0:T(8,128)S(1)}, f32[8,128,256]{2,1,0:T(8,128)}, u32[]{:S(2)}) copy-start(f32[8,128,256]{2,1,0:T(8,128)} %get-tuple-element.25) | copy-start | bytes 3145732
  320.7 11.2 %collective-permute-start.31 = (f32[1,128,256]{2,1,0:T(8,128)S(1)}, f32[1,128,256]{2,1,0:T(8,128)S(1)}, u32[]{:S(2)}, u32[]{:S(2)}) collective-permute-start(f32[1,128,256]{2,1,0:T(8,128)S(1)} %slice.324), channel_id=1, source_target_pairs={{0,2},{2,4},{4,6},{6,8},{8,10},{10,12},{12,14},{14,16},{16,18},{18... | collective-permute-start | bytes 393224 | tf_op jit(solution)/shard_map/ppermute | solution.py:19
  323.0 9.0 %copy-start.2 = (bf16[8,128,256]{2,1,0:T(8,128)(2,1)S(1)}, bf16[8,128,256]{2,1,0:T(8,128)(2,1)}, u32[]{:S(2)}) copy-start(bf16[8,128,256]{2,1,0:T(8,128)(2,1)} %param.3) | copy-start | bytes 1572868
  323.0 2.7 collective-permute-start.33
Sparse Core Ops, SparseCore 0:
  13.3 144.7 all-reduce.3
where the time goes:
time: 342 us; the launch traced here: 341 us
  waiting for transfers between devices  214 us (63%)
  starting transfers between devices  74.6 us (22%)
  matrix products  21.9 us (6%)
  between operations  16.6 us (5%)
  other arithmetic  10.1 us (3%)
    psum x1, waiting for transfers between devices, per_device(): gram = lax.psum(matmul(flat.T, flat), ('rows', 'cols'))  141 us
    ppermute x34, starting transfers between devices, shifted(): return lax.ppermute(x, axis, pairs)  74.6 us
    ppermute x34, waiting for transfers between devices, shifted(): return lax.ppermute(x, axis, pairs)  74 us
    dot_general x39, matrix products, matmul(): jnp.dot(left, right, precision=lax.Precision.HIGHEST, preferred_element_t...  21.9 us
  transfers between devices with their start and end apart: 35, of which 32 were waited for; matrix products, arithmetic and copies ran while one was open for 5% of the time, Pallas kernels for 0%

commit v1 on v0

v1 whole, which is shorter than its diff:
```python
import jax
import jax.numpy as jnp
from jax import lax
from jax.sharding import PartitionSpec as P

K_ROOT = 8
K_SIGN = 6
K_TV = 8


threshold_ratio = 1.0
dual_step = 0.25
tv_weight = 1.0

HALO = K_TV


def shifted(x, axis, by):
    length = lax.axis_size(axis)
    pairs = [(i, i + by) for i in range(length) if 0 <= i + by < length]
    return lax.ppermute(x, axis, pairs)


def matmul(left, right):
    return jnp.dot(left, right, precision=lax.Precision.HIGHEST, preferred_element_type=jnp.float32)


def shrink_matrix(gram):
    size = gram.shape[0]
    identity = jnp.eye(size, dtype=jnp.float32)
    scale = jnp.sqrt(jnp.sum(gram * gram))
    root = gram / scale
    inverse = identity
    for sweep in range(K_ROOT):
        factor = 1.5 * identity - 0.5 * matmul(inverse, root)
        root = matmul(root, factor)
        inverse = matmul(factor, inverse)
    cutoff = threshold_ratio * jnp.trace(root) / size
    signed = root - cutoff * identity
    for sweep in range(K_SIGN):
        signed = 1.5 * signed - 0.5 * matmul(signed, matmul(signed, signed))
    return 0.5 * matmul(identity - cutoff * inverse, identity + signed)


def with_halo(pair):
    left = shifted(pair[:, :, -HALO:], "cols", 1)
    right = shifted(pair[:, :, :HALO], "cols", -1)
    pair = jnp.concatenate([left, pair, right], axis=2)
    up = shifted(pair[:, -HALO:], "rows", 1)
    down = shifted(pair[:, :HALO], "rows", -1)
    return jnp.concatenate([up, pair, down], axis=1)


def divergence(px, py):
    prev_x = jnp.concatenate([jnp.zeros_like(px[:1]), px[:-1]], axis=0)
    prev_y = jnp.concatenate([jnp.zeros_like(py[:, :1]), py[:, :-1]], axis=1)
    return prev_x - px + prev_y - py


def slopes(s):
    down = jnp.concatenate([s[1:] - s[:-1], jnp.zeros_like(s[:1])], axis=0)
    across = jnp.concatenate([s[:, 1:] - s[:, :-1], jnp.zeros_like(s[:, :1])], axis=1)
    return down, across


def per_device(video, foreground, scaled_dual):
    rows_here, cols_here, frames = foreground.shape
    total_rows = rows_here * lax.axis_size("rows")
    total_cols = cols_here * lax.axis_size("cols")
    observed = video.astype(jnp.float32)
    mixed = observed - foreground + scaled_dual
    a = observed + scaled_dual
    ext = with_halo(jnp.stack([a, mixed]))
    a_ext, mixed_ext = ext[0], ext[1]
    flat = mixed.reshape(-1, frames)
    gram = lax.psum(matmul(flat.T, flat), ("rows", "cols"))
    shrink = shrink_matrix(gram)
    ext_rows, ext_cols = rows_here + 2 * HALO, cols_here + 2 * HALO
    background_ext = matmul(mixed_ext.reshape(-1, frames), shrink).reshape(ext_rows, ext_cols, frames)
    target = a_ext - background_ext

    first_row = lax.axis_index("rows") * rows_here - HALO
    first_col = lax.axis_index("cols") * cols_here - HALO
    g = first_row + lax.broadcasted_iota(jnp.int32, (ext_rows, 1, 1), 0)
    h = first_col + lax.broadcasted_iota(jnp.int32, (1, ext_cols, 1), 1)
    keep_x = (g >= 0) & (g <= total_rows - 2)
    keep_y = (h >= 0) & (h <= total_cols - 2)

    dual_x = jnp.zeros_like(target)
    dual_y = jnp.zeros_like(target)
    for sweep in range(K_TV):
        current = target - divergence(dual_x, dual_y)
        down, across = slopes(current)
        dual_x = jnp.where(keep_x, jnp.clip(dual_x + dual_step * down, -tv_weight, tv_weight), 0.0)
        dual_y = jnp.where(keep_y, jnp.clip(dual_y + dual_step * across, -tv_weight, tv_weight), 0.0)
    inner = (slice(HALO, HALO + rows_here), slice(HALO, HALO + cols_here))
    new_foreground = (target - divergence(dual_x, dual_y))[inner]
    background = background_ext[inner]
    new_dual = target[inner] - new_foreground
    return (background, new_foreground, new_dual)


def solution(mesh):
    return jax.shard_map(
        per_device,
        mesh=mesh,
        in_specs=(P("rows", "cols", None), P("rows", "cols", None), P("rows", "cols", None)),
        out_specs=(P("rows", "cols", None), P("rows", "cols", None), P("rows", "cols", None)),
        check_vma=False,
    )
```

time: 342 us -> 344 us (level)
  starting transfers between devices: 74.6 us -> 10.7 us
  other arithmetic: 10.1 us -> 62.3 us
  local copies, waits for them, and re-layouts: 3.03 us -> 31.9 us
  waiting for transfers between devices: 214 us -> 193 us
  matrix products: 21.9 us -> 26.6 us
    ppermute x34 -> x4, starting transfers between devices: 74.6 us -> 10.6 us  [shifted(): return lax.ppermute(x, axis, pairs)]
    sub x8 -> x24, other arithmetic: 4.37 us -> 39.5 us  [the longest x7 32.1 us: per_device(): current = target - divergence(dual_x, dual_y)]
    ppermute x34 -> x4, waiting for transfers between devices: 74 us -> 52.5 us  [shifted(): return lax.ppermute(x, axis, pairs)]
    select_n x2 -> x15, other arithmetic: 0.01 us -> 18.6 us  [the longest x8 13.8 us: per_device(): jnp.where(keep_y, jnp.clip(dual_y + dual_step * across, -tv_weight, tv_we...]
    unnamed x12 -> x38, local copies, waits for them, and re-layouts: 0.72 us -> 16.6 us
    slice x58 -> x9, local copies, waits for them, and re-layouts: 2.31 us -> 15.3 us  [the longest x8 12.7 us: divergence(): prev_x = jnp.concatenate([jnp.zeros_like(px[:1]), px[:-1]], axis=0)]
    dot_general x39, matrix products: 21.9 us -> 26.6 us  [matmul(): jnp.dot(left, right, precision=lax.Precision.HIGHEST, preferred_element_t...]
    min x8 -> x0, other arithmetic: 4.05 us -> none  [per_device(): dual_x = jnp.clip(dual_x + dual_step * down, -tv_weight, tv_weight)]
  transfers between devices with their start and end apart: 35 -> 5, of which waited for: 32 -> 3; matrix products, arithmetic and copies ran while one was open for 5% -> 6% of each run, Pallas kernels for 0% -> 0%
where the time goes in v1:
time: 344 us; the launch traced here: 341 us
  waiting for transfers between devices  193 us (56%)
  other arithmetic  62.3 us (18%)
  local copies, waits for them, and re-layouts  31.9 us (9%)
  matrix products  26.6 us (8%)
  between operations  16.3 us (5%)
  starting transfers between devices  10.7 us (3%)
    psum x1, waiting for transfers between devices, per_device(): gram = lax.psum(matmul(flat.T, flat), ('rows', 'cols'))  141 us
    ppermute x4, waiting for transfers between devices, shifted(): return lax.ppermute(x, axis, pairs)  52.5 us
    sub x7, other arithmetic, per_device(): current = target - divergence(dual_x, dual_y)  32.1 us
    dot_general x39, matrix products, matmul(): jnp.dot(left, right, precision=lax.Precision.HIGHEST, preferred_element_t...  26.6 us
    unnamed x38, local copies, waits for them, and re-layouts  16.6 us
    select_n x8, other arithmetic, per_device(): jnp.where(keep_y, jnp.clip(dual_y + dual_step * across, -tv_weight, tv_we...  13.8 us
    slice x8, local copies, waits for them, and re-layouts, divergence(): prev_x = jnp.concatenate([jnp.zeros_like(px[:1]), px[:-1]], axis=0)  12.7 us
    ppermute x4, starting transfers between devices, shifted(): return lax.ppermute(x, axis, pairs)  10.6 us
  transfers between devices with their start and end apart: 5, of which 3 were waited for; matrix products, arithmetic and copies ran while one was open for 6% of the time, Pallas kernels for 0%

profile of v1, /device:TPU:8, one launch (start us, length us, event | category | flops | bytes accessed | tf_op | source)
XLA Modules:
  0.0 341.0 jit_solution(16815311461451276916)
XLA Ops:
  7.2 5.3 %convolution_bitcast_fusion = f32[256,256]{1,0:T(8,128)} fusion(f32[8,128,256]{2,1,0:T(8,128)} %param.5, f32[8,128,256]{2,1,0:T(8,128)} %param.4, bf16[8,128,256]{2,1,0:T(8,128)(2,1)} %param.3), kind=kOutput, calls=%fused_computation.80 | convolution fusion | flops 806092800 | bytes 2883584 | tf_op jit(solution)/shard_map/dot_general | solution.py:25
  12.5 1.6 fusion.19
  14.2 1.7 collective-permute-start
  15.9 1.5 collective-permute-start.1
  17.4 140.6 %all-reduce.34.cloned.1.call-done = f32[256,256]{1,0:T(8,128)} async-done(((f32[256,256]{1,0:T(8,128)}), f32[256,256]{1,0:T(8,128)}) %all-reduce.34.cloned.1.call-update) | async-done | bytes 262160 | tf_op jit(solution)/shard_map/psum | solution.py:76
  158.1 1.6 multiply_reduce_fusion
  160.4 1.3 fusion.17
  161.9 1.3 fusion.30
  170.6 1.0 select_reduce_fusion
  173.7 5.3 %collective-permute-start.3 = (f32[2,8,144,256]{3,2,1,0:T(8,128)S(1)}, f32[2,8,144,256]{3,2,1,0:T(8,128)S(1)}, u32[]{:S(2)}, u32[]{:S(2)}) collective-permute-start(f32[2,8,144,256]{3,2,1,0:T(8,128)S(1)} %pad_maximum_fusion.1), channel_id=1, source_target_pairs={{2,0},{4,2},{6,4},{8,6},{10,8},{12,10},{14,12},{16,14},{18,16},{20... | collective-permute-start | bytes 7077896 | tf_op jit(solution)/shard_map/ppermute | solution.py:21
  179.0 2.1 collective-permute-start.2
  185.4 44.2 %collective-permute-done.3 = f32[2,8,144,256]{3,2,1,0:T(8,128)S(1)} collective-permute-done((f32[2,8,144,256]{3,2,1,0:T(8,128)S(1)}, f32[2,8,144,256]{3,2,1,0:T(8,128)S(1)}, u32[]{:S(2)}, u32[]{:S(2)}) %collective-permute-start.3) | collective-permute-done | bytes 2359328 | tf_op jit(solution)/shard_map/ppermute | solution.py:21
  229.6 8.3 %collective-permute-done.2 = f32[2,8,144,256]{3,2,1,0:T(8,128)S(1)} collective-permute-done((f32[2,8,144,256]{3,2,1,0:T(8,128)S(1)}, f32[2,8,144,256]{3,2,1,0:T(8,128)S(1)}, u32[]{:S(2)}, u32[]{:S(2)}) %collective-permute-start.2) | collective-permute-done | bytes 2359328 | tf_op jit(solution)/shard_map/ppermute | solution.py:21
  237.9 0.8 pad_maximum_fusion
  238.8 4.9 %fusion = (f32[24,144,256]{2,1,0:T(8,128)S(1)}, f32[24,144,256]{2,1,0:T(8,128)}) fusion(f32[2,24,144,256]{3,2,1,0:T(8,128)S(1)} %pad_maximum_fusion, f32[256,256,1]{1,0,2:T(8,128)S(1)} %fusion.2), kind=kOutput, calls=%fused_computation.10 | convolution fusion | flops 2718793728 | bytes 14417920 | tf_op jit(solution)/shard_map/dot_general | solution.py:25
  244.3 0.5 clamp_select_fusion.15
  245.1 0.5 clamp_select_fusion.14
  245.6 2.1 subtract_subtract_fusion.6
  248.0 0.5 slice_subtract_fusion.6
  248.5 2.3 clamp_select_fusion.12
  250.8 2.2 slice.233
  253.0 0.7 copy-done.16
  253.7 5.5 %subtract_subtract_fusion.5 = f32[24,144,256]{2,1,0:T(8,128)S(1)} fusion(f32[24,144,256]{2,1,0:T(8,128)S(1)} %get-tuple-element.11, f32[24,144,256]{2,1,0:T(8,128)S(1)} %get-tuple-element.13, f32[24,143,256]{2,1,0:T(8,128)S(1)} %bitcast.98, f32[24,144,256]{2,1,0:T(8,128)} %copy-done.16, f32[23,144,256]{2,1,0:T(8,128)} %slice.233), kind=kLoop, calls=%fused_computation.30 | loop fusion | flops 3538944 | bytes 21061632 | tf_op jit(solution)/shard_map/sub | solution.py:92
  259.4 0.5 slice_subtract_fusion.5
  259.9 1.5 copy-done.17
  261.4 0.7 clamp_select_fusion.11
  262.1 1.3 copy-done.5
  263.4 0.7 clamp_select_fusion.10
  264.1 1.1 copy-done.8
  265.2 2.0 slice.239
  267.2 4.9 %subtract_subtract_fusion.4 = f32[24,144,256]{2,1,0:T(8,128)S(1)} fusion(f32[24,144,256]{2,1,0:T(8,128)S(1)} %get-tuple-element.11, f32[24,144,256]{2,1,0:T(8,128)S(1)} %clamp_select_fusion.10, f32[24,143,256]{2,1,0:T(8,128)S(1)} %bitcast.94, f32[24,144,256]{2,1,0:T(8,128)} %copy-done.8, f32[23,144,256]{2,1,0:T(8,128)} %slice.239), kind=kLoop, calls=%fused_computation.27 | loop fusion | flops 3538944 | bytes 21061632 | tf_op jit(solution)/shard_map/sub | solution.py:92
  272.4 0.5 slice_subtract_fusion.4
  272.8 1.5 copy-done.9
  274.3 0.7 clamp_select_fusion.9
  275.0 2.9 clamp_select_fusion.8
  278.0 2.0 slice.245
  280.0 1.2 copy-done
  281.2 4.9 %subtract_subtract_fusion.3 = f32[24,144,256]{2,1,0:T(8,128)S(1)} fusion(f32[24,144,256]{2,1,0:T(8,128)S(1)} %get-tuple-element.11, f32[24,144,256]{2,1,0:T(8,128)S(1)} %copy-done, f32[24,143,256]{2,1,0:T(8,128)S(1)} %bitcast.95, f32[24,144,256]{2,1,0:T(8,128)} %copy-done.10, f32[23,144,256]{2,1,0:T(8,128)} %slice.245), kind=kLoop, calls=%fused_computation.24 | loop fusion | flops 3538944 | bytes 21061632 | tf_op jit(solution)/shard_map/sub | solution.py:92
  286.3 0.5 slice_subtract_fusion.3
  286.8 1.5 copy-done.11
  288.3 0.8 clamp_select_fusion.7
  289.2 2.9 clamp_select_fusion.6
  292.1 2.0 slice.251
  294.1 1.2 copy-done.1
  295.3 4.9 %subtract_subtract_fusion.2 = f32[24,144,256]{2,1,0:T(8,128)S(1)} fusion(f32[24,144,256]{2,1,0:T(8,128)S(1)} %get-tuple-element.11, f32[24,144,256]{2,1,0:T(8,128)S(1)} %copy-done.1, f32[24,143,256]{2,1,0:T(8,128)S(1)} %bitcast.96, f32[24,144,256]{2,1,0:T(8,128)} %copy-done.12, f32[23,144,256]{2,1,0:T(8,128)} %slice.251), kind=kLoop, calls=%fused_computation.21 | loop fusion | flops 3538944 | bytes 21061632 | tf_op jit(solution)/shard_map/sub | solution.py:92
  300.5 0.5 slice_subtract_fusion.2
  301.0 1.5 copy-done.13
  302.5 0.7 clamp_select_fusion.5
  303.2 3.0 clamp_select_fusion.4
  306.2 2.0 slice.257
  308.2 1.2 copy-done.2
  309.4 4.9 %subtract_subtract_fusion.1 = f32[24,144,256]{2,1,0:T(8,128)S(1)} fusion(f32[24,144,256]{2,1,0:T(8,128)S(1)} %get-tuple-element.11, f32[24,144,256]{2,1,0:T(8,128)S(1)} %copy-done.2, f32[24,143,256]{2,1,0:T(8,128)S(1)} %bitcast.97, f32[24,144,256]{2,1,0:T(8,128)} %copy-done.14, f32[23,144,256]{2,1,0:T(8,128)} %slice.257), kind=kLoop, calls=%fused_computation.18 | loop fusion | flops 3538944 | bytes 21061632 | tf_op jit(solution)/shard_map/sub | solution.py:92
  314.6 0.5 slice_subtract_fusion.1
  315.1 1.5 copy-done.15
  316.6 0.7 clamp_select_fusion.3
  317.3 1.3 copy-done.3
  318.6 0.7 clamp_select_fusion.2
  319.3 1.1 copy-done.6
  320.4 2.0 slice.263
  322.4 4.9 %subtract_subtract_fusion = f32[24,144,256]{2,1,0:T(8,128)S(1)} fusion(f32[24,144,256]{2,1,0:T(8,128)S(1)} %get-tuple-element.11, f32[24,144,256]{2,1,0:T(8,128)S(1)} %clamp_select_fusion.2, f32[24,143,256]{2,1,0:T(8,128)S(1)} %bitcast.93, f32[24,144,256]{2,1,0:T(8,128)} %copy-done.6, f32[23,144,256]{2,1,0:T(8,128)} %slice.263), kind=kLoop, calls=%fused_computation.15 | loop fusion | flops 3538944 | bytes 21061632 | tf_op jit(solution)/shard_map/sub | solution.py:92
  328.0 2.5 slice.223
  330.6 0.7 clamp_select_fusion.1
  331.2 0.7 clamp_select_fusion
  332.2 1.8 slice_subtract_fusion.18
  (79 shorter events, 16.5 us)
Async XLA Ops:
  7.2 5.4 %copy-start.18 = (f32[8,128,256]{2,1,0:T(8,128)S(1)}, f32[8,128,256]{2,1,0:T(8,128)}, u32[]{:S(2)}) copy-start(f32[8,128,256]{2,1,0:T(8,128)} %param.5) | copy-start | bytes 3145732
  7.2 150.9 %all-reduce.34.cloned.1.call-start = ((), (), s32[]{:S(2)}) async-start(), calls=%async_computation | async-start | bytes 524288 | tf_op jit(solution)/shard_map/psum | solution.py:76
  14.2 159.3 %collective-permute-start = (f32[2,8,8,256]{3,2,1,0:T(8,128)S(1)}, f32[2,8,8,256]{3,2,1,0:T(8,128)S(1)}, u32[]{:S(2)}, u32[]{:S(2)}) collective-permute-start(f32[2,8,8,256]{3,2,1,0:T(8,128)S(1)} %get-tuple-element.5), channel_id=1, source_target_pairs={{0,1},{2,3},{4,5},{6,7},{8,9},{10,11},{12,13},{14,15},{16,17},{18,... | collective-permute-start | bytes 393224 | tf_op jit(solution)/shard_map/ppermute | solution.py:21
  15.9 157.6 %collective-permute-start.1 = (f32[2,8,8,256]{3,2,1,0:T(8,128)S(1)}, f32[2,8,8,256]{3,2,1,0:T(8,128)S(1)}, u32[]{:S(2)}, u32[]{:S(2)}) collective-permute-start(f32[2,8,8,256]{3,2,1,0:T(8,128)S(1)} %get-tuple-element.6), channel_id=1, source_target_pairs={{1,0},{3,2},{5,4},{7,6},{9,8},{11,10},{13,12},{15,14},{17,16},{19,... | collective-permute-start | bytes 393224 | tf_op jit(solution)/shard_map/ppermute | solution.py:21
  173.7 55.9 %collective-permute-start.3 = (f32[2,8,144,256]{3,2,1,0:T(8,128)S(1)}, f32[2,8,144,256]{3,2,1,0:T(8,128)S(1)}, u32[]{:S(2)}, u32[]{:S(2)}) collective-permute-start(f32[2,8,144,256]{3,2,1,0:T(8,128)S(1)} %pad_maximum_fusion.1), channel_id=1, source_target_pairs={{2,0},{4,2},{6,4},{8,6},{10,8},{12,10},{14,12},{16,14},{18,16},{20... | collective-permute-start | bytes 7077896 | tf_op jit(solution)/shard_map/ppermute | solution.py:21
  179.0 58.9 %collective-permute-start.2 = (f32[2,8,144,256]{3,2,1,0:T(8,128)S(1)}, f32[2,8,144,256]{3,2,1,0:T(8,128)S(1)}, u32[]{:S(2)}, u32[]{:S(2)}) collective-permute-start(f32[2,8,144,256]{3,2,1,0:T(8,128)S(1)} %pad_maximum_fusion.1), channel_id=1, source_target_pairs={{0,2},{2,4},{4,6},{6,8},{8,10},{10,12},{12,14},{14,16},{16,18},{18... | collective-permute-start | bytes 7077896 | tf_op jit(solution)/shard_map/ppermute | solution.py:21
  250.8 2.9 copy-start.16
  250.8 8.3 %copy-start.4 = (f32[24,144,256]{2,1,0:T(8,128)}, f32[24,144,256]{2,1,0:T(8,128)S(1)}, u32[]{:S(2)}) copy-start(f32[24,144,256]{2,1,0:T(8,128)S(1)} %get-tuple-element.13) | copy-start | bytes 10616836
  259.4 2.0 copy-start.17
  261.4 2.0 copy-start.5
  263.4 1.8 copy-start.8
  272.3 2.0 copy-start.9
  275.0 2.9 copy-start.10
  278.0 3.2 copy-start
  286.3 2.0 copy-start.11
  289.2 2.9 copy-start.12
  292.1 3.2 copy-start.1
  300.5 2.0 copy-start.13
  303.2 3.0 copy-start.14
  306.2 3.2 copy-start.2
  314.6 2.0 copy-start.15
  316.6 2.0 copy-start.3
  318.6 1.8 copy-start.6
  327.6 3.0 copy-start.7
Sparse Core Ops, SparseCore 0:
  13.3 144.7 all-reduce.33

commit v2 on v1

--- a/solution.py
+++ b/solution.py
@@ -43,12 +43,35 @@
 
 
 def with_halo(pair):
+    up = shifted(pair[:, -HALO:], "rows", 1)
+    down = shifted(pair[:, :HALO], "rows", -1)
+    pair = jnp.concatenate([up, pair, down], axis=1)
     left = shifted(pair[:, :, -HALO:], "cols", 1)
     right = shifted(pair[:, :, :HALO], "cols", -1)
-    pair = jnp.concatenate([left, pair, right], axis=2)
-    up = shifted(pair[:, -HALO:], "rows", 1)
-    down = shifted(pair[:, :HALO], "rows", -1)
-    return jnp.concatenate([up, pair, down], axis=1)
+    return jnp.concatenate([left, pair, right], axis=2)
+
+
+def all_sum(x):
+    for axis in ("cols", "rows"):
+        length = lax.axis_size(axis)
+        if length & (length - 1):
+            x = lax.psum(x, axis)
+            continue
+        step = 1
+        while step < length:
+            x = x + lax.ppermute(x, axis, [(i, i ^ step) for i in range(length)])
+            step *= 2
+    return x
+
+
+def summed_gram(flat):
+    local = matmul(flat.T, flat)
+    half = local.shape[0] // 2
+    packed = all_sum(jnp.concatenate([local[:half], local[half:, half:]], axis=1))
+    top = packed[:, : 2 * half]
+    corner = packed[:, 2 * half :]
+    bottom = jnp.concatenate([top[:, half:].T, corner], axis=1)
+    return jnp.concatenate([top, bottom], axis=0)
 
 
 def divergence(px, py):
@@ -73,7 +96,7 @@
     ext = with_halo(jnp.stack([a, mixed]))
     a_ext, mixed_ext = ext[0], ext[1]
     flat = mixed.reshape(-1, frames)
-    gram = lax.psum(matmul(flat.T, flat), ("rows", "cols"))
+    gram = summed_gram(flat)
     shrink = shrink_matrix(gram)
     ext_rows, ext_cols = rows_here + 2 * HALO, cols_here + 2 * HALO
     background_ext = matmul(mixed_ext.reshape(-1, frames), shrink).reshape(ext_rows, ext_cols, frames)

time: 344 us -> 222 us (0.65)
  the two profiles are of different devices: /device:TPU:8 before, /device:TPU:97 now
where the time goes in v2:
time: 222 us; the launch traced here: 217 us
  other arithmetic  64.5 us (29%)
  starting transfers between devices  48.3 us (22%)
  waiting for transfers between devices  45.2 us (20%)
  local copies, waits for them, and re-layouts  32.1 us (14%)
  matrix products  24.4 us (11%)
  between operations  3.02 us (1%)
    ppermute x4, starting transfers between devices, shifted(): return lax.ppermute(x, axis, pairs)  38.6 us
    sub x7, other arithmetic, per_device(): current = target - divergence(dual_x, dual_y)  32.1 us
    dot_general x39, matrix products, matmul(): jnp.dot(left, right, precision=lax.Precision.HIGHEST, preferred_element_t...  24.4 us
    ppermute x7, waiting for transfers between devices, all_sum(): x = x + lax.ppermute(x, axis, [(i, i ^ step) for i in range(length)])  23.5 us
    ppermute x4, waiting for transfers between devices, shifted(): return lax.ppermute(x, axis, pairs)  21.7 us
    unnamed x43, local copies, waits for them, and re-layouts  16.7 us
    select_n x8, other arithmetic, per_device(): jnp.where(keep_y, jnp.clip(dual_y + dual_step * across, -tv_weight, tv_we...  13.8 us
    slice x8, local copies, waits for them, and re-layouts, divergence(): prev_x = jnp.concatenate([jnp.zeros_like(px[:1]), px[:-1]], axis=0)  12.8 us
  transfers between devices with their start and end apart: 11, of which 9 were waited for; matrix products, arithmetic and copies ran while one was open for 8% of the time, Pallas kernels for 0%

profile of v2, /device:TPU:97, one launch (start us, length us, event | category | flops | bytes accessed | tf_op | source)
XLA Modules:
  0.0 217.4 jit_solution(17217619082910192475)
XLA Ops:
  0.7 4.6 %convolution_bitcast_fusion = f32[256,256]{0,1:T(8,128)S(1)} fusion(f32[8,128,256]{2,1,0:T(8,128)} %param.5, f32[8,128,256]{2,1,0:T(8,128)} %param.4, bf16[8,128,256]{2,1,0:T(8,128)(2,1)} %param.3), kind=kOutput, calls=%fused_computation.80 | convolution fusion | flops 806092800 | bytes 2883584 | tf_op jit(solution)/shard_map/dot_general | solution.py:25
  5.3 0.8 collective-permute-start.4
  6.1 1.1 collective-permute-done.4
  7.2 1.3 collective-permute-start.5
  8.4 4.9 %collective-permute-done.5 = f32[128,384]{0,1:T(8,128)S(1)} collective-permute-done((f32[128,384]{0,1:T(8,128)S(1)}, f32[128,384]{0,1:T(8,128)S(1)}, u32[]{:S(2)}, u32[]{:S(2)}) %collective-permute-start.5) | collective-permute-done | bytes 196640 | tf_op jit(solution)/shard_map/ppermute | solution.py:62
  13.4 2.8 %collective-permute-start.6 = (f32[128,384]{0,1:T(8,128)S(1)}, f32[128,384]{0,1:T(8,128)S(1)}, u32[]{:S(2)}, u32[]{:S(2)}) collective-permute-start(f32[128,384]{0,1:T(8,128)S(1)} %add.188), channel_id=1, source_target_pairs={{0,4},{2,6},{4,0},{6,2},{8,12},{10,14},{12,8},{14,10},{16,20},{18,... | collective-permute-start | bytes 589832 | tf_op jit(solution)/shard_map/ppermute | solution.py:62
  16.2 4.0 %collective-permute-done.6 = f32[128,384]{0,1:T(8,128)S(1)} collective-permute-done((f32[128,384]{0,1:T(8,128)S(1)}, f32[128,384]{0,1:T(8,128)S(1)}, u32[]{:S(2)}, u32[]{:S(2)}) %collective-permute-start.6) | collective-permute-done | bytes 196640 | tf_op jit(solution)/shard_map/ppermute | solution.py:62
  20.4 4.4 %collective-permute-done.7 = f32[128,384]{0,1:T(8,128)S(1)} collective-permute-done((f32[128,384]{0,1:T(8,128)S(1)}, f32[128,384]{0,1:T(8,128)S(1)}, u32[]{:S(2)}, u32[]{:S(2)}) %collective-permute-start.7) | collective-permute-done | bytes 196640 | tf_op jit(solution)/shard_map/ppermute | solution.py:62
  25.2 5.8 %collective-permute-done.8 = f32[128,384]{0,1:T(8,128)S(1)} collective-permute-done((f32[128,384]{0,1:T(8,128)S(1)}, f32[128,384]{0,1:T(8,128)S(1)}, u32[]{:S(2)}, u32[]{:S(2)}) %collective-permute-start.8) | collective-permute-done | bytes 196640 | tf_op jit(solution)/shard_map/ppermute | solution.py:62
  30.9 1.4 collective-permute-start.9
  32.5 1.6 pad_maximum_fusion.1
  34.1 4.2 %collective-permute-start.1 = (f32[2,8,128,256]{3,2,1,0:T(8,128)}, f32[2,8,128,256]{3,2,1,0:T(8,128)}, u32[]{:S(2)}, u32[]{:S(2)}) collective-permute-start(f32[2,8,128,256]{3,2,1,0:T(8,128)} %pad_maximum_fusion.1), channel_id=1, source_target_pairs={{2,0},{4,2},{6,4},{8,6},{10,8},{12,10},{14,12},{16,14},{18,16},{20... | collective-permute-start | bytes 6291464 | tf_op jit(solution)/shard_map/ppermute | solution.py:21
  38.3 1.9 collective-permute-start
  40.3 2.9 %collective-permute-start.10 = (f32[128,384]{0,1:T(8,128)S(1)}, f32[128,384]{0,1:T(8,128)S(1)}, u32[]{:S(2)}, u32[]{:S(2)}) collective-permute-start(f32[128,384]{0,1:T(8,128)S(1)} %add.192), channel_id=1, source_target_pairs={{0,64},{2,66},{4,68},{6,70},{8,72},{10,74},{12,76},{14,78},{16,80}... | collective-permute-start | bytes 589832 | tf_op jit(solution)/shard_map/ppermute | solution.py:62
  43.2 3.4 %collective-permute-done.10 = f32[128,384]{0,1:T(8,128)S(1)} collective-permute-done((f32[128,384]{0,1:T(8,128)S(1)}, f32[128,384]{0,1:T(8,128)S(1)}, u32[]{:S(2)}, u32[]{:S(2)}) %collective-permute-start.10) | collective-permute-done | bytes 196640 | tf_op jit(solution)/shard_map/ppermute | solution.py:62
  46.7 0.7 multiply_reduce_fusion
  56.7 1.0 select_reduce_fusion
  62.8 15.6 %collective-permute-done.1 = f32[2,8,128,256]{3,2,1,0:T(8,128)} collective-permute-done((f32[2,8,128,256]{3,2,1,0:T(8,128)}, f32[2,8,128,256]{3,2,1,0:T(8,128)}, u32[]{:S(2)}, u32[]{:S(2)}) %collective-permute-start.1) | collective-permute-done | bytes 2097184 | tf_op jit(solution)/shard_map/ppermute | solution.py:21
  78.4 5.9 %collective-permute-done = f32[2,8,128,256]{3,2,1,0:T(8,128)} collective-permute-done((f32[2,8,128,256]{3,2,1,0:T(8,128)}, f32[2,8,128,256]{3,2,1,0:T(8,128)}, u32[]{:S(2)}, u32[]{:S(2)}) %collective-permute-start) | collective-permute-done | bytes 2097184 | tf_op jit(solution)/shard_map/ppermute | solution.py:21
  84.4 1.2 pad_maximum_fusion.5
  85.6 1.3 collective-permute-start.2
  86.9 31.2 %collective-permute-start.3 = (f32[2,24,8,256]{3,2,1,0:T(8,128)S(1)}, f32[2,24,8,256]{3,2,1,0:T(8,128)S(1)}, u32[]{:S(2)}, u32[]{:S(2)}) collective-permute-start(f32[2,24,8,256]{3,2,1,0:T(8,128)S(1)} %get-tuple-element.6), channel_id=1, source_target_pairs={{1,0},{3,2},{5,4},{7,6},{9,8},{11,10},{13,12},{15,14},{17,16},{19,... | collective-permute-start | bytes 1179656 | tf_op jit(solution)/shard_map/ppermute | solution.py:21
  119.3 2.7 %pad_maximum_fusion = f32[2,24,144,256]{3,2,1,0:T(8,128)S(1)} fusion(f32[2,24,8,256]{3,2,1,0:T(8,128)S(1)} %collective-permute-done.3, f32[2,8,128,256]{3,2,1,0:T(8,128)} %collective-permute-done.1, f32[1,8,128,256]{3,2,1,0:T(8,128)S(1)} %get-tuple-element.8, f32[1,8,128,256]{3,2,1,0:T(8,128)S(1)} %get-tuple-element.7, ...), kind=kLoop, calls=%fused_computation | loop fusion | flops 8847360 | bytes 14155776 | tf_op jit(solution)/shard_map/concatenate | solution.py:51
  122.0 4.8 %fusion = (f32[24,144,256]{2,1,0:T(8,128)S(1)}, f32[24,144,256]{2,1,0:T(8,128)}) fusion(f32[2,24,144,256]{3,2,1,0:T(8,128)S(1)} %pad_maximum_fusion, f32[256,256,1]{1,0,2:T(8,128)S(1)} %fusion.2), kind=kOutput, calls=%fused_computation.10 | convolution fusion | flops 2718793728 | bytes 14417920 | tf_op jit(solution)/shard_map/dot_general | solution.py:25
  128.9 2.1 subtract_subtract_fusion.6
  131.7 2.2 %clamp_select_fusion.12 = (f32[24,144,256]{2,1,0:T(8,128)S(1)}, f32[24,144,256]{2,1,0:T(8,128)S(1)}) fusion(f32[24,143,256]{2,1,0:T(8,128)S(1)} %slice_subtract_fusion.6, pred[144]{0:T(512)(128)(4,1)S(1)} %compare_and_fusion, f32[23,144,256]{2,1,0:T(8,128)S(1)} %slice_subtract_fusion.14, f32[23,144,256]{2,1,0:T(8,128)S(1)} %slice_subtract_fusion.15, ...), kind=kLoop, calls=%fused_computation.31 | loop fusion | flops 12386304 | bytes 20889768 | tf_op jit(solution)/shard_map/jit(_where)/select_n | solution.py:118
  134.0 2.2 %slice.259 = f32[23,144,256]{2,1,0:T(8,128)} slice(f32[24,144,256]{2,1,0:T(8,128)S(1)} %get-tuple-element.16), slice={[0:23], [0:144], [0:256]} | slice | bytes 6782976 | tf_op jit(solution)/shard_map/slice | solution.py:78
  136.8 5.5 %subtract_subtract_fusion.5 = f32[24,144,256]{2,1,0:T(8,128)S(1)} fusion(f32[24,144,256]{2,1,0:T(8,128)S(1)} %get-tuple-element.13, f32[24,144,256]{2,1,0:T(8,128)S(1)} %get-tuple-element.15, f32[24,143,256]{2,1,0:T(8,128)S(1)} %bitcast.99, f32[24,144,256]{2,1,0:T(8,128)} %copy-done.16, f32[23,144,256]{2,1,0:T(8,128)} %slice.259), kind=kLoop, calls=%fused_computation.30 | loop fusion | flops 3538944 | bytes 21061632 | tf_op jit(solution)/shard_map/sub | solution.py:115
  143.0 1.5 copy-done.17
  144.5 0.7 clamp_select_fusion.11
  145.2 1.3 copy-done.5
  146.5 0.7 clamp_select_fusion.10
  147.3 1.1 copy-done.8
  148.4 2.0 slice.265
  150.4 4.9 %subtract_subtract_fusion.4 = f32[24,144,256]{2,1,0:T(8,128)S(1)} fusion(f32[24,144,256]{2,1,0:T(8,128)S(1)} %get-tuple-element.13, f32[24,144,256]{2,1,0:T(8,128)S(1)} %clamp_select_fusion.10, f32[24,143,256]{2,1,0:T(8,128)S(1)} %bitcast.95, f32[24,144,256]{2,1,0:T(8,128)} %copy-done.8, f32[23,144,256]{2,1,0:T(8,128)} %slice.265), kind=kLoop, calls=%fused_computation.27 | loop fusion | flops 3538944 | bytes 21061632 | tf_op jit(solution)/shard_map/sub | solution.py:115
  156.0 1.5 copy-done.9
  157.5 0.7 clamp_select_fusion.9
  158.2 2.9 %clamp_select_fusion.8 = f32[24,144,256]{2,1,0:T(8,128)} fusion(f32[24,144,256]{2,1,0:T(8,128)S(1)} %clamp_select_fusion.10, f32[24,143,256]{2,1,0:T(8,128)S(1)} %slice_subtract_fusion.4, pred[144]{0:T(512)(128)(4,1)S(1)} %compare_and_fusion), kind=kLoop, calls=%fused_computation.25 | loop fusion | flops 3538944 | bytes 10592400 | tf_op jit(solution)/shard_map/jit(_where)/select_n | solution.py:118
  161.2 2.0 slice.271
  163.2 1.2 copy-done
  164.4 4.9 %subtract_subtract_fusion.3 = f32[24,144,256]{2,1,0:T(8,128)S(1)} fusion(f32[24,144,256]{2,1,0:T(8,128)S(1)} %get-tuple-element.13, f32[24,144,256]{2,1,0:T(8,128)S(1)} %copy-done, f32[24,143,256]{2,1,0:T(8,128)S(1)} %bitcast.96, f32[24,144,256]{2,1,0:T(8,128)} %copy-done.10, f32[23,144,256]{2,1,0:T(8,128)} %slice.271), kind=kLoop, calls=%fused_computation.24 | loop fusion | flops 3538944 | bytes 21061632 | tf_op jit(solution)/shard_map/sub | solution.py:115
  170.0 1.5 copy-done.11
  171.6 0.8 clamp_select_fusion.7
  172.4 2.9 %clamp_select_fusion.6 = f32[24,144,256]{2,1,0:T(8,128)} fusion(f32[24,144,256]{2,1,0:T(8,128)S(1)} %copy-done, f32[24,143,256]{2,1,0:T(8,128)S(1)} %slice_subtract_fusion.3, pred[144]{0:T(512)(128)(4,1)S(1)} %compare_and_fusion), kind=kLoop, calls=%fused_computation.22 | loop fusion | flops 3538944 | bytes 10592400 | tf_op jit(solution)/shard_map/jit(_where)/select_n | solution.py:118
  175.4 2.0 slice.277
  177.4 1.2 copy-done.1
  178.6 4.9 %subtract_subtract_fusion.2 = f32[24,144,256]{2,1,0:T(8,128)S(1)} fusion(f32[24,144,256]{2,1,0:T(8,128)S(1)} %get-tuple-element.13, f32[24,144,256]{2,1,0:T(8,128)S(1)} %copy-done.1, f32[24,143,256]{2,1,0:T(8,128)S(1)} %bitcast.97, f32[24,144,256]{2,1,0:T(8,128)} %copy-done.12, f32[23,144,256]{2,1,0:T(8,128)} %slice.277), kind=kLoop, calls=%fused_computation.21 | loop fusion | flops 3538944 | bytes 21061632 | tf_op jit(solution)/shard_map/sub | solution.py:115
  184.2 1.5 copy-done.13
  185.7 0.7 clamp_select_fusion.5
  186.4 3.0 %clamp_select_fusion.4 = f32[24,144,256]{2,1,0:T(8,128)} fusion(f32[24,144,256]{2,1,0:T(8,128)S(1)} %copy-done.1, f32[24,143,256]{2,1,0:T(8,128)S(1)} %slice_subtract_fusion.2, pred[144]{0:T(512)(128)(4,1)S(1)} %compare_and_fusion), kind=kLoop, calls=%fused_computation.19 | loop fusion | flops 3538944 | bytes 10592400 | tf_op jit(solution)/shard_map/jit(_where)/select_n | solution.py:118
  189.4 2.0 slice.283
  191.4 1.2 copy-done.2
  192.6 4.9 %subtract_subtract_fusion.1 = f32[24,144,256]{2,1,0:T(8,128)S(1)} fusion(f32[24,144,256]{2,1,0:T(8,128)S(1)} %get-tuple-element.13, f32[24,144,256]{2,1,0:T(8,128)S(1)} %copy-done.2, f32[24,143,256]{2,1,0:T(8,128)S(1)} %bitcast.98, f32[24,144,256]{2,1,0:T(8,128)} %copy-done.14, f32[23,144,256]{2,1,0:T(8,128)} %slice.283), kind=kLoop, calls=%fused_computation.18 | loop fusion | flops 3538944 | bytes 21061632 | tf_op jit(solution)/shard_map/sub | solution.py:115
  198.3 1.5 copy-done.15
  199.8 0.7 clamp_select_fusion.3
  200.5 1.3 copy-done.3
  201.8 0.7 clamp_select_fusion.2
  202.5 1.1 copy-done.6
  203.6 2.0 slice.289
  205.6 4.9 %subtract_subtract_fusion = f32[24,144,256]{2,1,0:T(8,128)S(1)} fusion(f32[24,144,256]{2,1,0:T(8,128)S(1)} %get-tuple-element.13, f32[24,144,256]{2,1,0:T(8,128)S(1)} %clamp_select_fusion.2, f32[24,143,256]{2,1,0:T(8,128)S(1)} %bitcast.94, f32[24,144,256]{2,1,0:T(8,128)} %copy-done.6, f32[23,144,256]{2,1,0:T(8,128)} %slice.289), kind=kLoop, calls=%fused_computation.15 | loop fusion | flops 3538944 | bytes 21061632 | tf_op jit(solution)/shard_map/sub | solution.py:115
  211.3 2.5 %slice.249 = f32[8,128,256]{2,1,0:T(8,128)} slice(f32[24,144,256]{2,1,0:T(8,128)} %get-tuple-element.14), slice={[8:16], [8:136], [0:256]} | slice | bytes 2097152 | tf_op jit(solution)/shard_map/slice | solution.py:121
  213.8 0.7 clamp_select_fusion.1
  214.5 0.7 clamp_select_fusion
  215.4 1.8 slice_subtract_fusion.18
  (107 shorter events, 23.0 us)
Async XLA Ops:
  0.6 31.7 %copy-start.18 = (f32[8,128,256]{2,1,0:T(8,128)S(1)}, f32[8,128,256]{2,1,0:T(8,128)}, u32[]{:S(2)}) copy-start(f32[8,128,256]{2,1,0:T(8,128)} %param.5) | copy-start | bytes 3145732
  0.6 31.7 %copy-start.19 = (f32[8,128,256]{2,1,0:T(8,128)S(1)}, f32[8,128,256]{2,1,0:T(8,128)}, u32[]{:S(2)}) copy-start(f32[8,128,256]{2,1,0:T(8,128)} %param.4) | copy-start | bytes 3145732
  0.7 31.7 %copy-start.20 = (bf16[8,128,256]{2,1,0:T(8,128)(2,1)S(1)}, bf16[8,128,256]{2,1,0:T(8,128)(2,1)}, u32[]{:S(2)}) copy-start(bf16[8,128,256]{2,1,0:T(8,128)(2,1)} %param.3) | copy-start | bytes 1572868
  5.3 1.8 collective-permute-start.4
  7.2 6.2 %collective-permute-start.5 = (f32[128,384]{0,1:T(8,128)S(1)}, f32[128,384]{0,1:T(8,128)S(1)}, u32[]{:S(2)}, u32[]{:S(2)}) collective-permute-start(f32[128,384]{0,1:T(8,128)S(1)} %fusion.38), channel_id=1, source_target_pairs={{0,2},{2,0},{4,6},{6,4},{8,10},{10,8},{12,14},{14,12},{16,18},{18,... | collective-permute-start | bytes 589832 | tf_op jit(solution)/shard_map/ppermute | solution.py:62
  13.4 6.8 %collective-permute-start.6 = (f32[128,384]{0,1:T(8,128)S(1)}, f32[128,384]{0,1:T(8,128)S(1)}, u32[]{:S(2)}, u32[]{:S(2)}) collective-permute-start(f32[128,384]{0,1:T(8,128)S(1)} %add.188), channel_id=1, source_target_pairs={{0,4},{2,6},{4,0},{6,2},{8,12},{10,14},{12,8},{14,10},{16,20},{18,... | collective-permute-start | bytes 589832 | tf_op jit(solution)/shard_map/ppermute | solution.py:62
  20.2 4.6 %collective-permute-start.7 = (f32[128,384]{0,1:T(8,128)S(1)}, f32[128,384]{0,1:T(8,128)S(1)}, u32[]{:S(2)}, u32[]{:S(2)}) collective-permute-start(f32[128,384]{0,1:T(8,128)S(1)} %add.189), channel_id=1, source_target_pairs={{0,8},{2,10},{4,12},{6,14},{8,0},{10,2},{12,4},{14,6},{16,24},{18,... | collective-permute-start | bytes 589832 | tf_op jit(solution)/shard_map/ppermute | solution.py:62
  24.8 6.1 %collective-permute-start.8 = (f32[128,384]{0,1:T(8,128)S(1)}, f32[128,384]{0,1:T(8,128)S(1)}, u32[]{:S(2)}, u32[]{:S(2)}) collective-permute-start(f32[128,384]{0,1:T(8,128)S(1)} %add.190), channel_id=1, source_target_pairs={{0,16},{2,18},{4,20},{6,22},{8,24},{10,26},{12,28},{14,30},{16,0},... | collective-permute-start | bytes 589832 | tf_op jit(solution)/shard_map/ppermute | solution.py:62
  30.9 9.3 %collective-permute-start.9 = (f32[128,384]{0,1:T(8,128)S(1)}, f32[128,384]{0,1:T(8,128)S(1)}, u32[]{:S(2)}, u32[]{:S(2)}) collective-permute-start(f32[128,384]{0,1:T(8,128)S(1)} %add.191), channel_id=1, source_target_pairs={{0,32},{2,34},{4,36},{6,38},{8,40},{10,42},{12,44},{14,46},{16,48}... | collective-permute-start | bytes 589832 | tf_op jit(solution)/shard_map/ppermute | solution.py:62
  34.1 44.4 %collective-permute-start.1 = (f32[2,8,128,256]{3,2,1,0:T(8,128)}, f32[2,8,128,256]{3,2,1,0:T(8,128)}, u32[]{:S(2)}, u32[]{:S(2)}) collective-permute-start(f32[2,8,128,256]{3,2,1,0:T(8,128)} %pad_maximum_fusion.1), channel_id=1, source_target_pairs={{2,0},{4,2},{6,4},{8,6},{10,8},{12,10},{14,12},{16,14},{18,16},{20... | collective-permute-start | bytes 6291464 | tf_op jit(solution)/shard_map/ppermute | solution.py:21
  38.3 46.1 %collective-permute-start = (f32[2,8,128,256]{3,2,1,0:T(8,128)}, f32[2,8,128,256]{3,2,1,0:T(8,128)}, u32[]{:S(2)}, u32[]{:S(2)}) collective-permute-start(f32[2,8,128,256]{3,2,1,0:T(8,128)} %pad_maximum_fusion.1), channel_id=1, source_target_pairs={{0,2},{2,4},{4,6},{6,8},{8,10},{10,12},{12,14},{14,16},{16,18},{18... | collective-permute-start | bytes 6291464 | tf_op jit(solution)/shard_map/ppermute | solution.py:21
  40.3 6.3 %collective-permute-start.10 = (f32[128,384]{0,1:T(8,128)S(1)}, f32[128,384]{0,1:T(8,128)S(1)}, u32[]{:S(2)}, u32[]{:S(2)}) collective-permute-start(f32[128,384]{0,1:T(8,128)S(1)} %add.192), channel_id=1, source_target_pairs={{0,64},{2,66},{4,68},{6,70},{8,72},{10,74},{12,76},{14,78},{16,80}... | collective-permute-start | bytes 589832 | tf_op jit(solution)/shard_map/ppermute | solution.py:62
  85.6 33.6 %collective-permute-start.2 = (f32[2,24,8,256]{3,2,1,0:T(8,128)S(1)}, f32[2,24,8,256]{3,2,1,0:T(8,128)S(1)}, u32[]{:S(2)}, u32[]{:S(2)}) collective-permute-start(f32[2,24,8,256]{3,2,1,0:T(8,128)S(1)} %get-tuple-element.5), channel_id=1, source_target_pairs={{0,1},{2,3},{4,5},{6,7},{8,9},{10,11},{12,13},{14,15},{16,17},{18,... | collective-permute-start | bytes 1179656 | tf_op jit(solution)/shard_map/ppermute | solution.py:21
  86.9 32.5 %collective-permute-start.3 = (f32[2,24,8,256]{3,2,1,0:T(8,128)S(1)}, f32[2,24,8,256]{3,2,1,0:T(8,128)S(1)}, u32[]{:S(2)}, u32[]{:S(2)}) collective-permute-start(f32[2,24,8,256]{3,2,1,0:T(8,128)S(1)} %get-tuple-element.6), channel_id=1, source_target_pairs={{1,0},{3,2},{5,4},{7,6},{9,8},{11,10},{13,12},{15,14},{17,16},{19,... | collective-permute-start | bytes 1179656 | tf_op jit(solution)/shard_map/ppermute | solution.py:21
  134.0 2.8 %copy-start.16 = (f32[24,144,256]{2,1,0:T(8,128)}, f32[24,144,256]{2,1,0:T(8,128)S(1)}, u32[]{:S(2)}) copy-start(f32[24,144,256]{2,1,0:T(8,128)S(1)} %get-tuple-element.16) | copy-start | bytes 10616836
  134.0 8.3 %copy-start.4 = (f32[24,144,256]{2,1,0:T(8,128)}, f32[24,144,256]{2,1,0:T(8,128)S(1)}, u32[]{:S(2)}) copy-start(f32[24,144,256]{2,1,0:T(8,128)S(1)} %get-tuple-element.15) | copy-start | bytes 10616836
  142.5 2.0 copy-start.17
  144.5 2.0 copy-start.5
  146.5 1.8 copy-start.8
  155.5 2.0 copy-start.9
  158.2 2.9 %copy-start.10 = (f32[24,144,256]{2,1,0:T(8,128)}, f32[24,144,256]{2,1,0:T(8,128)S(1)}, u32[]{:S(2)}) copy-start(f32[24,144,256]{2,1,0:T(8,128)S(1)} %clamp_select_fusion.9) | copy-start | bytes 10616836
  161.2 3.2 %copy-start = (f32[24,144,256]{2,1,0:T(8,128)S(1)}, f32[24,144,256]{2,1,0:T(8,128)}, u32[]{:S(2)}) copy-start(f32[24,144,256]{2,1,0:T(8,128)} %clamp_select_fusion.8) | copy-start | bytes 10616836
  169.6 2.0 copy-start.11
  172.4 2.9 %copy-start.12 = (f32[24,144,256]{2,1,0:T(8,128)}, f32[24,144,256]{2,1,0:T(8,128)S(1)}, u32[]{:S(2)}) copy-start(f32[24,144,256]{2,1,0:T(8,128)S(1)} %clamp_select_fusion.7) | copy-start | bytes 10616836
  175.4 3.2 %copy-start.1 = (f32[24,144,256]{2,1,0:T(8,128)S(1)}, f32[24,144,256]{2,1,0:T(8,128)}, u32[]{:S(2)}) copy-start(f32[24,144,256]{2,1,0:T(8,128)} %clamp_select_fusion.6) | copy-start | bytes 10616836
  183.7 2.0 copy-start.13
  186.4 3.0 %copy-start.14 = (f32[24,144,256]{2,1,0:T(8,128)}, f32[24,144,256]{2,1,0:T(8,128)S(1)}, u32[]{:S(2)}) copy-start(f32[24,144,256]{2,1,0:T(8,128)S(1)} %clamp_select_fusion.5) | copy-start | bytes 10616836
  189.4 3.2 %copy-start.2 = (f32[24,144,256]{2,1,0:T(8,128)S(1)}, f32[24,144,256]{2,1,0:T(8,128)}, u32[]{:S(2)}) copy-start(f32[24,144,256]{2,1,0:T(8,128)} %clamp_select_fusion.4) | copy-start | bytes 10616836
  197.8 2.0 copy-start.15
  199.8 2.0 copy-start.3
  201.8 1.8 copy-start.6
  210.8 3.0 %copy-start.7 = (f32[24,144,256]{2,1,0:T(8,128)S(1)}, f32[24,144,256]{2,1,0:T(8,128)}, u32[]{:S(2)}) copy-start(f32[24,144,256]{2,1,0:T(8,128)} %copy-done.6) | copy-start | bytes 10616836

commit v3 on v2

--- a/solution.py
+++ b/solution.py
@@ -2,6 +2,8 @@
 import jax.numpy as jnp
 from jax import lax
 from jax.sharding import PartitionSpec as P
+from jax.experimental import pallas as pl
+from jax.experimental.pallas import tpu as pltpu
 
 K_ROOT = 8
 K_SIGN = 6
@@ -86,6 +88,60 @@
     return down, across
 
 
+def tv_kernel(target_ref, kx_ref, ky_ref, fg_ref, dual_ref):
+    t = target_ref[...]
+    rows, cols = t.shape[0], t.shape[1]
+    kx = kx_ref[...]
+    ky = ky_ref[...][None]
+
+    def prev_y(q):
+        return pltpu.roll(q, 1, 1)
+
+    def next_y(q):
+        return pltpu.roll(q, cols - 1, 1)
+
+    s = t
+    px = jnp.clip(dual_step * (s[1:] - s[:-1]), -tv_weight, tv_weight) * kx[: rows - 1]
+    py = jnp.clip(dual_step * (next_y(s[: rows - 1]) - s[: rows - 1]), -tv_weight, tv_weight) * ky
+    for sweep in range(2, K_TV + 1):
+        n = rows + 3 - 2 * sweep
+        q = py[1:n]
+        s = t[sweep - 1 : rows + 1 - sweep] - (px[: n - 1] - px[1:n] + prev_y(q) - q)
+        down = s[1:] - s[:-1]
+        across = next_y(s[:-1]) - s[:-1]
+        px = jnp.clip(px[1 : n - 1] + dual_step * down, -tv_weight, tv_weight) * kx[sweep - 1 : rows - sweep]
+        py = jnp.clip(py[1 : n - 1] + dual_step * across, -tv_weight, tv_weight) * ky
+    q = py[1:]
+    inner = rows - 2 * HALO
+    middle = t[HALO : HALO + inner]
+    fg = middle - (px[:-1] - px[1:] + prev_y(q) - q)
+    width = cols - 2 * HALO
+    fg = fg[:, HALO : HALO + width]
+    fg_ref[...] = fg
+    dual_ref[...] = middle[:, HALO : HALO + width] - fg
+
+
+def tv_local(target, kx, ky):
+    rows, cols, frames = target.shape
+    inner_rows, inner_cols = rows - 2 * HALO, cols - 2 * HALO
+    lanes = 128 if frames % 128 == 0 else frames
+    out = jax.ShapeDtypeStruct((inner_rows, inner_cols, frames), jnp.float32)
+    return pl.pallas_call(
+        tv_kernel,
+        grid=(frames // lanes,),
+        in_specs=[
+            pl.BlockSpec((rows, cols, lanes), lambda f: (0, 0, f)),
+            pl.BlockSpec((rows, 1, lanes), lambda f: (0, 0, 0)),
+            pl.BlockSpec((cols, lanes), lambda f: (0, 0)),
+        ],
+        out_specs=[
+            pl.BlockSpec((inner_rows, inner_cols, lanes), lambda f: (0, 0, f)),
+            pl.BlockSpec((inner_rows, inner_cols, lanes), lambda f: (0, 0, f)),
+        ],
+        out_shape=[out, out],
+    )(target, kx, ky)
+
+
 def per_device(video, foreground, scaled_dual):
     rows_here, cols_here, frames = foreground.shape
     total_rows = rows_here * lax.axis_size("rows")
@@ -108,18 +164,12 @@
     h = first_col + lax.broadcasted_iota(jnp.int32, (1, ext_cols, 1), 1)
     keep_x = (g >= 0) & (g <= total_rows - 2)
     keep_y = (h >= 0) & (h <= total_cols - 2)
-
-    dual_x = jnp.zeros_like(target)
-    dual_y = jnp.zeros_like(target)
-    for sweep in range(K_TV):
-        current = target - divergence(dual_x, dual_y)
-        down, across = slopes(current)
-        dual_x = jnp.where(keep_x, jnp.clip(dual_x + dual_step * down, -tv_weight, tv_weight), 0.0)
-        dual_y = jnp.where(keep_y, jnp.clip(dual_y + dual_step * across, -tv_weight, tv_weight), 0.0)
+    lanes = 128 if frames % 128 == 0 else frames
+    kx = jnp.broadcast_to(jnp.where(keep_x, 1.0, 0.0).astype(jnp.float32), (ext_rows, 1, lanes))
+    ky = jnp.broadcast_to(jnp.where(keep_y, 1.0, 0.0).astype(jnp.float32)[0], (ext_cols, lanes))
+    new_foreground, new_dual = tv_local(target, kx, ky)
     inner = (slice(HALO, HALO + rows_here), slice(HALO, HALO + cols_here))
-    new_foreground = (target - divergence(dual_x, dual_y))[inner]
     background = background_ext[inner]
-    new_dual = target[inner] - new_foreground
     return (background, new_foreground, new_dual)
 
 

time: 222 us -> 144 us (0.65)
  the two profiles are of different devices: /device:TPU:97 before, /device:TPU:105 now
where the time goes in v3:
time: 144 us
  starting transfers between devices  52.2 us (36%)
  waiting for transfers between devices  40.3 us (28%)
  matrix products  24.2 us (17%)
  Pallas kernels  16.1 us (11%)
  other arithmetic  6.4 us (4%)
  local copies, waits for them, and re-layouts  2.6 us (2%)
  between operations  2.46 us (2%)
    ppermute x4, starting transfers between devices, shifted(): return lax.ppermute(x, axis, pairs)  43.9 us
    dot_general x39, matrix products, matmul(): jnp.dot(left, right, precision=lax.Precision.HIGHEST, preferred_element_t...  24.2 us
    ppermute x7, waiting for transfers between devices, all_sum(): x = x + lax.ppermute(x, axis, [(i, i ^ step) for i in range(length)])  24.2 us
    pallas_call x1, Pallas kernels, tv_local(): pl.pallas_call(tv_kernel, grid=(frames // lanes,), in_specs=[pl.BlockSpec...  16.1 us
    ppermute x4, waiting for transfers between devices, shifted(): return lax.ppermute(x, axis, pairs)  16.1 us
    ppermute x7, starting transfers between devices, all_sum(): x = x + lax.ppermute(x, axis, [(i, i ^ step) for i in range(length)])  8.25 us
  transfers between devices with their start and end apart: 11, of which 9 were waited for; matrix products, arithmetic and copies ran while one was open for 12% of the time, Pallas kernels for 0%

profile of v3, /device:TPU:105, one launch (start us, length us, event | category | flops | bytes accessed | tf_op | source)
XLA Modules:
  0.0 144.2 jit_solution(3003146023642846831)
XLA Ops:
  0.7 4.5 %convolution_bitcast_fusion = f32[256,256]{0,1:T(8,128)S(1)} fusion(f32[8,128,256]{2,1,0:T(8,128)} %param.5, f32[8,128,256]{2,1,0:T(8,128)} %param.4, bf16[8,128,256]{2,1,0:T(8,128)(2,1)} %param.3), kind=kOutput, calls=%fused_computation.41 | convolution fusion | flops 806092800 | bytes 2883584 | tf_op jit(solution)/shard_map/dot_general | solution.py:27
  5.3 0.8 collective-permute-start.4
  6.0 1.1 collective-permute-done.4
  7.1 1.3 collective-permute-start.5
  8.4 4.9 %collective-permute-done.5 = f32[128,384]{0,1:T(8,128)S(1)} collective-permute-done((f32[128,384]{0,1:T(8,128)S(1)}, f32[128,384]{0,1:T(8,128)S(1)}, u32[]{:S(2)}, u32[]{:S(2)}) %collective-permute-start.5) | collective-permute-done | bytes 196640 | tf_op jit(solution)/shard_map/ppermute | solution.py:64
  13.3 2.8 %collective-permute-start.6 = (f32[128,384]{0,1:T(8,128)S(1)}, f32[128,384]{0,1:T(8,128)S(1)}, u32[]{:S(2)}, u32[]{:S(2)}) collective-permute-start(f32[128,384]{0,1:T(8,128)S(1)} %add.58), channel_id=1, source_target_pairs={{0,4},{2,6},{4,0},{6,2},{8,12},{10,14},{12,8},{14,10},{16,20},{18,... | collective-permute-start | bytes 589832 | tf_op jit(solution)/shard_map/ppermute | solution.py:64
  16.1 4.0 %collective-permute-done.6 = f32[128,384]{0,1:T(8,128)S(1)} collective-permute-done((f32[128,384]{0,1:T(8,128)S(1)}, f32[128,384]{0,1:T(8,128)S(1)}, u32[]{:S(2)}, u32[]{:S(2)}) %collective-permute-start.6) | collective-permute-done | bytes 196640 | tf_op jit(solution)/shard_map/ppermute | solution.py:64
  20.3 4.4 %collective-permute-done.7 = f32[128,384]{0,1:T(8,128)S(1)} collective-permute-done((f32[128,384]{0,1:T(8,128)S(1)}, f32[128,384]{0,1:T(8,128)S(1)}, u32[]{:S(2)}, u32[]{:S(2)}) %collective-permute-start.7) | collective-permute-done | bytes 196640 | tf_op jit(solution)/shard_map/ppermute | solution.py:64
  24.8 0.4 collective-permute-start.8
  25.1 5.8 %collective-permute-done.8 = f32[128,384]{0,1:T(8,128)S(1)} collective-permute-done((f32[128,384]{0,1:T(8,128)S(1)}, f32[128,384]{0,1:T(8,128)S(1)}, u32[]{:S(2)}, u32[]{:S(2)}) %collective-permute-start.8) | collective-permute-done | bytes 196640 | tf_op jit(solution)/shard_map/ppermute | solution.py:64
  31.3 1.5 %pad_maximum_fusion.1 = f32[2,8,128,256]{3,2,1,0:T(8,128)} fusion(f32[1,8,128,256]{3,2,1,0:T(8,128)S(1)} %get-tuple-element.10, f32[1,8,128,256]{3,2,1,0:T(8,128)S(1)} %get-tuple-element.9), kind=kLoop, calls=%fused_computation.5 | loop fusion | flops 524288 | bytes 4194304 | tf_op jit(solution)/shard_map/stack | solution.py:152
  32.9 3.1 %collective-permute-start = (f32[2,8,128,256]{3,2,1,0:T(8,128)}, f32[2,8,128,256]{3,2,1,0:T(8,128)}, u32[]{:S(2)}, u32[]{:S(2)}) collective-permute-start(f32[2,8,128,256]{3,2,1,0:T(8,128)} %pad_maximum_fusion.1), channel_id=1, source_target_pairs={{0,2},{2,4},{4,6},{6,8},{8,10},{10,12},{12,14},{14,16},{16,18},{18... | collective-permute-start | bytes 6291464 | tf_op jit(solution)/shard_map/ppermute | solution.py:23
  36.0 4.3 %collective-permute-start.1 = (f32[2,8,128,256]{3,2,1,0:T(8,128)}, f32[2,8,128,256]{3,2,1,0:T(8,128)}, u32[]{:S(2)}, u32[]{:S(2)}) collective-permute-start(f32[2,8,128,256]{3,2,1,0:T(8,128)} %pad_maximum_fusion.1), channel_id=1, source_target_pairs={{2,0},{4,2},{6,4},{8,6},{10,8},{12,10},{14,12},{16,14},{18,16},{20... | collective-permute-start | bytes 6291464 | tf_op jit(solution)/shard_map/ppermute | solution.py:23
  40.3 2.6 %collective-permute-start.10 = (f32[128,384]{0,1:T(8,128)S(1)}, f32[128,384]{0,1:T(8,128)S(1)}, u32[]{:S(2)}, u32[]{:S(2)}) collective-permute-start(f32[128,384]{0,1:T(8,128)S(1)} %add.62), channel_id=1, source_target_pairs={{0,64},{2,66},{4,68},{6,70},{8,72},{10,74},{12,76},{14,78},{16,80}... | collective-permute-start | bytes 589832 | tf_op jit(solution)/shard_map/ppermute | solution.py:64
  42.9 4.1 %collective-permute-done.10 = f32[128,384]{0,1:T(8,128)S(1)} collective-permute-done((f32[128,384]{0,1:T(8,128)S(1)}, f32[128,384]{0,1:T(8,128)S(1)}, u32[]{:S(2)}, u32[]{:S(2)}) %collective-permute-start.10) | collective-permute-done | bytes 196640 | tf_op jit(solution)/shard_map/ppermute | solution.py:64
  47.2 0.7 multiply_reduce_fusion
  48.5 0.3 fusion.17
  48.9 0.6 fusion.30
  49.5 0.3 fusion.21
  49.8 0.4 fusion.16
  50.2 0.4 fusion.39
  50.5 0.4 fusion.40
  50.9 0.4 fusion.15
  51.3 0.4 fusion.41
  51.7 0.4 fusion.42
  52.1 0.4 fusion.14
  52.5 0.4 fusion.43
  52.9 0.4 fusion.44
  53.3 0.4 fusion.13
  53.6 0.4 fusion.45
  54.0 0.4 fusion.46
  54.4 0.4 fusion.12
  54.8 0.4 fusion.47
  55.2 0.4 fusion.48
  55.6 0.4 fusion.11
  56.0 0.4 fusion.49
  56.4 0.4 fusion.50
  56.7 0.4 fusion.10
  57.1 1.0 select_reduce_fusion
  58.8 0.4 fusion.9
  59.2 0.4 fusion.22
  59.6 0.4 fusion.8
  60.0 0.4 fusion.51
  60.4 0.4 fusion.7
  60.7 0.4 fusion.52
  61.1 0.4 fusion.6
  61.5 0.4 fusion.53
  61.9 0.4 fusion.5
  62.3 0.6 fusion.54
  62.9 0.4 fusion.4
  63.3 15.1 %collective-permute-done = f32[2,8,128,256]{3,2,1,0:T(8,128)} collective-permute-done((f32[2,8,128,256]{3,2,1,0:T(8,128)}, f32[2,8,128,256]{3,2,1,0:T(8,128)}, u32[]{:S(2)}, u32[]{:S(2)}) %collective-permute-start) | collective-permute-done | bytes 2097184 | tf_op jit(solution)/shard_map/ppermute | solution.py:23
  78.4 0.9 collective-permute-done.1
  79.3 1.2 pad_maximum_fusion.5
  80.4 1.3 collective-permute-start.2
  81.7 35.3 %collective-permute-start.3 = (f32[2,24,8,256]{3,2,1,0:T(8,128)S(1)}, f32[2,24,8,256]{3,2,1,0:T(8,128)S(1)}, u32[]{:S(2)}, u32[]{:S(2)}) collective-permute-start(f32[2,24,8,256]{3,2,1,0:T(8,128)S(1)} %get-tuple-element.8), channel_id=1, source_target_pairs={{1,0},{3,2},{5,4},{7,6},{9,8},{11,10},{13,12},{15,14},{17,16},{19,... | collective-permute-start | bytes 1179656 | tf_op jit(solution)/shard_map/ppermute | solution.py:23
  117.0 0.4 fusion.55
  117.4 0.4 fusion.18
  117.8 0.4 fusion.2
  118.3 2.7 %pad_maximum_fusion = f32[2,24,144,256]{3,2,1,0:T(8,128)S(1)} fusion(f32[2,24,8,256]{3,2,1,0:T(8,128)S(1)} %collective-permute-done.3, f32[2,8,128,256]{3,2,1,0:T(8,128)} %collective-permute-done.1, f32[1,8,128,256]{3,2,1,0:T(8,128)S(1)} %get-tuple-element.10, f32[1,8,128,256]{3,2,1,0:T(8,128)S(1)} %get-tuple-element.9, ...), kind=kLoop, calls=%fused_computation | loop fusion | flops 8847360 | bytes 14155776 | tf_op jit(solution)/shard_map/concatenate | solution.py:53
  121.0 4.7 %fusion = (f32[24,144,256]{2,1,0:T(8,128)}, f32[24,144,256]{2,1,0:T(8,128)S(1)}) fusion(f32[2,24,144,256]{3,2,1,0:T(8,128)S(1)} %pad_maximum_fusion, f32[256,256,1]{1,0,2:T(8,128)S(1)} %fusion.2), kind=kOutput, calls=%fused_computation.2 | convolution fusion | flops 2718793728 | bytes 14417920 | tf_op jit(solution)/shard_map/dot_general | solution.py:27
  125.6 1.1 slice.47
  126.7 0.7 broadcast_in_dim.33.ky_ref
  127.4 0.7 broadcast_in_dim.30.kx_ref
  128.1 16.1 %shard_map.58 = (f32[8,128,256]{2,1,0:T(8,128)}, f32[8,128,256]{2,1,0:T(8,128)}) custom-call(f32[24,144,256]{2,1,0:T(8,128)} %get-tuple-element.15.target_ref, f32[24,1,128]{2,1,0:T(1,128)} %broadcast_in_dim.30.kx_ref, f32[144,128]{1,0:T(8,128)} %broadcast_in_dim.33.ky_ref), custom_call_target="tpu_custom_call" | custom-call | tf_op jit(solution)/shard_map/pallas_call | solution.py:129
  (27 shorter events, 1.1 us)
Async XLA Ops:
  0.6 30.5 %copy-start.2 = (bf16[8,128,256]{2,1,0:T(8,128)(2,1)S(1)}, bf16[8,128,256]{2,1,0:T(8,128)(2,1)}, u32[]{:S(2)}) copy-start(bf16[8,128,256]{2,1,0:T(8,128)(2,1)} %param.3) | copy-start | bytes 1572868
  0.6 30.5 %copy-start.1 = (f32[8,128,256]{2,1,0:T(8,128)S(1)}, f32[8,128,256]{2,1,0:T(8,128)}, u32[]{:S(2)}) copy-start(f32[8,128,256]{2,1,0:T(8,128)} %param.4) | copy-start | bytes 3145732
  0.7 30.5 %copy-start = (f32[8,128,256]{2,1,0:T(8,128)S(1)}, f32[8,128,256]{2,1,0:T(8,128)}, u32[]{:S(2)}) copy-start(f32[8,128,256]{2,1,0:T(8,128)} %param.5) | copy-start | bytes 3145732
  5.3 1.8 %collective-permute-start.4 = (f32[128,384]{0,1:T(8,128)S(1)}, f32[128,384]{0,1:T(8,128)S(1)}, u32[]{:S(2)}, u32[]{:S(2)}) collective-permute-start(f32[128,384]{0,1:T(8,128)S(1)} %pad_maximum_fusion.6), channel_id=1, source_target_pairs={{0,1},{1,0},{2,3},{3,2},{4,5},{5,4},{6,7},{7,6},{8,9},{9,8},{10,11... | collective-permute-start | bytes 589832 | tf_op jit(solution)/shard_map/ppermute | solution.py:64
  7.1 6.2 %collective-permute-start.5 = (f32[128,384]{0,1:T(8,128)S(1)}, f32[128,384]{0,1:T(8,128)S(1)}, u32[]{:S(2)}, u32[]{:S(2)}) collective-permute-start(f32[128,384]{0,1:T(8,128)S(1)} %fusion.37), channel_id=1, source_target_pairs={{0,2},{2,0},{4,6},{6,4},{8,10},{10,8},{12,14},{14,12},{16,18},{18,... | collective-permute-start | bytes 589832 | tf_op jit(solution)/shard_map/ppermute | solution.py:64
  13.3 6.8 %collective-permute-start.6 = (f32[128,384]{0,1:T(8,128)S(1)}, f32[128,384]{0,1:T(8,128)S(1)}, u32[]{:S(2)}, u32[]{:S(2)}) collective-permute-start(f32[128,384]{0,1:T(8,128)S(1)} %add.58), channel_id=1, source_target_pairs={{0,4},{2,6},{4,0},{6,2},{8,12},{10,14},{12,8},{14,10},{16,20},{18,... | collective-permute-start | bytes 589832 | tf_op jit(solution)/shard_map/ppermute | solution.py:64
  20.1 4.6 %collective-permute-start.7 = (f32[128,384]{0,1:T(8,128)S(1)}, f32[128,384]{0,1:T(8,128)S(1)}, u32[]{:S(2)}, u32[]{:S(2)}) collective-permute-start(f32[128,384]{0,1:T(8,128)S(1)} %add.59), channel_id=1, source_target_pairs={{0,8},{2,10},{4,12},{6,14},{8,0},{10,2},{12,4},{14,6},{16,24},{18,... | collective-permute-start | bytes 589832 | tf_op jit(solution)/shard_map/ppermute | solution.py:64
  24.8 6.1 %collective-permute-start.8 = (f32[128,384]{0,1:T(8,128)S(1)}, f32[128,384]{0,1:T(8,128)S(1)}, u32[]{:S(2)}, u32[]{:S(2)}) collective-permute-start(f32[128,384]{0,1:T(8,128)S(1)} %add.60), channel_id=1, source_target_pairs={{0,16},{2,18},{4,20},{6,22},{8,24},{10,26},{12,28},{14,30},{16,0},... | collective-permute-start | bytes 589832 | tf_op jit(solution)/shard_map/ppermute | solution.py:64
  30.9 9.4 %collective-permute-start.9 = (f32[128,384]{0,1:T(8,128)S(1)}, f32[128,384]{0,1:T(8,128)S(1)}, u32[]{:S(2)}, u32[]{:S(2)}) collective-permute-start(f32[128,384]{0,1:T(8,128)S(1)} %add.61), channel_id=1, source_target_pairs={{0,32},{2,34},{4,36},{6,38},{8,40},{10,42},{12,44},{14,46},{16,48}... | collective-permute-start | bytes 589832 | tf_op jit(solution)/shard_map/ppermute | solution.py:64
  32.9 45.5 %collective-permute-start = (f32[2,8,128,256]{3,2,1,0:T(8,128)}, f32[2,8,128,256]{3,2,1,0:T(8,128)}, u32[]{:S(2)}, u32[]{:S(2)}) collective-permute-start(f32[2,8,128,256]{3,2,1,0:T(8,128)} %pad_maximum_fusion.1), channel_id=1, source_target_pairs={{0,2},{2,4},{4,6},{6,8},{8,10},{10,12},{12,14},{14,16},{16,18},{18... | collective-permute-start | bytes 6291464 | tf_op jit(solution)/shard_map/ppermute | solution.py:23
  36.0 43.3 %collective-permute-start.1 = (f32[2,8,128,256]{3,2,1,0:T(8,128)}, f32[2,8,128,256]{3,2,1,0:T(8,128)}, u32[]{:S(2)}, u32[]{:S(2)}) collective-permute-start(f32[2,8,128,256]{3,2,1,0:T(8,128)} %pad_maximum_fusion.1), channel_id=1, source_target_pairs={{2,0},{4,2},{6,4},{8,6},{10,8},{12,10},{14,12},{16,14},{18,16},{20... | collective-permute-start | bytes 6291464 | tf_op jit(solution)/shard_map/ppermute | solution.py:23
  40.3 6.7 %collective-permute-start.10 = (f32[128,384]{0,1:T(8,128)S(1)}, f32[128,384]{0,1:T(8,128)S(1)}, u32[]{:S(2)}, u32[]{:S(2)}) collective-permute-start(f32[128,384]{0,1:T(8,128)S(1)} %add.62), channel_id=1, source_target_pairs={{0,64},{2,66},{4,68},{6,70},{8,72},{10,74},{12,76},{14,78},{16,80}... | collective-permute-start | bytes 589832 | tf_op jit(solution)/shard_map/ppermute | solution.py:64
  80.4 37.7 %collective-permute-start.2 = (f32[2,24,8,256]{3,2,1,0:T(8,128)S(1)}, f32[2,24,8,256]{3,2,1,0:T(8,128)S(1)}, u32[]{:S(2)}, u32[]{:S(2)}) collective-permute-start(f32[2,24,8,256]{3,2,1,0:T(8,128)S(1)} %get-tuple-element.7), channel_id=1, source_target_pairs={{0,1},{2,3},{4,5},{6,7},{8,9},{10,11},{12,13},{14,15},{16,17},{18,... | collective-permute-start | bytes 1179656 | tf_op jit(solution)/shard_map/ppermute | solution.py:23
  81.7 36.6 %collective-permute-start.3 = (f32[2,24,8,256]{3,2,1,0:T(8,128)S(1)}, f32[2,24,8,256]{3,2,1,0:T(8,128)S(1)}, u32[]{:S(2)}, u32[]{:S(2)}) collective-permute-start(f32[2,24,8,256]{3,2,1,0:T(8,128)S(1)} %get-tuple-element.8), channel_id=1, source_target_pairs={{1,0},{3,2},{5,4},{7,6},{9,8},{11,10},{13,12},{15,14},{17,16},{19,... | collective-permute-start | bytes 1179656 | tf_op jit(solution)/shard_map/ppermute | solution.py:23

commit v4 on v3

--- a/solution.py
+++ b/solution.py
@@ -4,6 +4,7 @@
 from jax.sharding import PartitionSpec as P
 from jax.experimental import pallas as pl
 from jax.experimental.pallas import tpu as pltpu
+
 
 K_ROOT = 8
 K_SIGN = 6
@@ -33,13 +34,13 @@
     scale = jnp.sqrt(jnp.sum(gram * gram))
     root = gram / scale
     inverse = identity
-    for sweep in range(K_ROOT):
+    for _ in range(K_ROOT):
         factor = 1.5 * identity - 0.5 * matmul(inverse, root)
         root = matmul(root, factor)
         inverse = matmul(factor, inverse)
     cutoff = threshold_ratio * jnp.trace(root) / size
     signed = root - cutoff * identity
-    for sweep in range(K_SIGN):
+    for _ in range(K_SIGN):
         signed = 1.5 * signed - 0.5 * matmul(signed, matmul(signed, signed))
     return 0.5 * matmul(identity - cutoff * inverse, identity + signed)
 
@@ -61,8 +62,13 @@
             continue
         step = 1
         while step < length:
-            x = x + lax.ppermute(x, axis, [(i, i ^ step) for i in range(length)])
-            step *= 2
+            if 4 * step <= length:
+                r1, r2, r3 = (lax.ppermute(x, axis, [(i, i ^ (k * step)) for i in range(length)]) for k in (1, 2, 3))
+                x = (x + r1) + (r2 + r3)
+                step *= 4
+            else:
+                x = x + lax.ppermute(x, axis, [(i, i ^ step) for i in range(length)])
+                step *= 2
     return x
 
 
@@ -74,18 +80,6 @@
     corner = packed[:, 2 * half :]
     bottom = jnp.concatenate([top[:, half:].T, corner], axis=1)
     return jnp.concatenate([top, bottom], axis=0)
-
-
-def divergence(px, py):
-    prev_x = jnp.concatenate([jnp.zeros_like(px[:1]), px[:-1]], axis=0)
-    prev_y = jnp.concatenate([jnp.zeros_like(py[:, :1]), py[:, :-1]], axis=1)
-    return prev_x - px + prev_y - py
-
-
-def slopes(s):
-    down = jnp.concatenate([s[1:] - s[:-1], jnp.zeros_like(s[:1])], axis=0)
-    across = jnp.concatenate([s[:, 1:] - s[:, :-1], jnp.zeros_like(s[:, :1])], axis=1)
-    return down, across
 
 
 def tv_kernel(target_ref, kx_ref, ky_ref, fg_ref, dual_ref):

time: 144 us -> 142 us (0.986)
  the two profiles are of different devices: /device:TPU:105 before, /device:TPU:1 now
where the time goes in v4:
time: 142 us
  starting transfers between devices  55.2 us (39%)
  waiting for transfers between devices  34.6 us (24%)
  matrix products  24.2 us (17%)
  Pallas kernels  16.1 us (11%)
  other arithmetic  6.4 us (5%)
  local copies, waits for them, and re-layouts  2.59 us (2%)
  between operations  2.46 us (2%)
    ppermute x4, starting transfers between devices, shifted(): return lax.ppermute(x, axis, pairs)  37.2 us
    dot_general x39, matrix products, matmul(): jnp.dot(left, right, precision=lax.Precision.HIGHEST, preferred_element_t...  24.2 us
    ppermute x9, waiting for transfers between devices, all_sum(): lax.ppermute(x, axis, [(i, i ^ k * step) for i in range(length)])  20.5 us
    ppermute x9, starting transfers between devices, all_sum(): lax.ppermute(x, axis, [(i, i ^ k * step) for i in range(length)])  16.6 us
    pallas_call x1, Pallas kernels, tv_local(): pl.pallas_call(tv_kernel, grid=(frames // lanes,), in_specs=[pl.BlockSpec...  16.1 us
    ppermute x4, waiting for transfers between devices, shifted(): return lax.ppermute(x, axis, pairs)  13 us
  transfers between devices with their start and end apart: 14, of which 11 were waited for; matrix products, arithmetic and copies ran while one was open for 12% of the time, Pallas kernels for 0%

profile of v4, /device:TPU:1, one launch (start us, length us, event | category | flops | bytes accessed | tf_op | source)
XLA Modules:
  0.0 141.6 jit_solution(5631486890772484795)
XLA Ops:
  0.7 4.5 %convolution_bitcast_fusion = f32[256,256]{0,1:T(8,128)S(1)} fusion(f32[8,128,256]{2,1,0:T(8,128)} %param.5, f32[8,128,256]{2,1,0:T(8,128)} %param.4, bf16[8,128,256]{2,1,0:T(8,128)(2,1)} %param.3), kind=kOutput, calls=%fused_computation.41 | convolution fusion | flops 806092800 | bytes 2883584 | tf_op jit(solution)/shard_map/dot_general | solution.py:28
  5.3 1.5 %collective-permute-start.4 = (f32[128,384]{0,1:T(8,128)S(1)}, f32[128,384]{0,1:T(8,128)S(1)}, u32[]{:S(2)}, u32[]{:S(2)}) collective-permute-start(f32[128,384]{0,1:T(8,128)S(1)} %pad_maximum_fusion.6), channel_id=1, source_target_pairs={{0,1},{1,0},{2,3},{3,2},{4,5},{5,4},{6,7},{7,6},{8,9},{9,8},{10,11... | collective-permute-start | bytes 589832 | tf_op jit(solution)/shard_map/ppermute | solution.py:70
  6.7 1.1 collective-permute-done.4
  7.8 1.4 collective-permute-start.5
  9.2 2.5 %collective-permute-start.6 = (f32[128,384]{0,1:T(8,128)S(1)}, f32[128,384]{0,1:T(8,128)S(1)}, u32[]{:S(2)}, u32[]{:S(2)}) collective-permute-start(f32[128,384]{0,1:T(8,128)S(1)} %fusion.37), channel_id=1, source_target_pairs={{0,4},{2,6},{4,0},{6,2},{8,12},{10,14},{12,8},{14,10},{16,20},{18,... | collective-permute-start | bytes 589832 | tf_op jit(solution)/shard_map/ppermute | solution.py:66
  11.7 2.2 %collective-permute-done.5 = f32[128,384]{0,1:T(8,128)S(1)} collective-permute-done((f32[128,384]{0,1:T(8,128)S(1)}, f32[128,384]{0,1:T(8,128)S(1)}, u32[]{:S(2)}, u32[]{:S(2)}) %collective-permute-start.5) | collective-permute-done | bytes 196640 | tf_op jit(solution)/shard_map/ppermute | solution.py:66
  14.0 6.6 %collective-permute-done.6 = f32[128,384]{0,1:T(8,128)S(1)} collective-permute-done((f32[128,384]{0,1:T(8,128)S(1)}, f32[128,384]{0,1:T(8,128)S(1)}, u32[]{:S(2)}, u32[]{:S(2)}) %collective-permute-start.6) | collective-permute-done | bytes 196640 | tf_op jit(solution)/shard_map/ppermute | solution.py:66
  20.5 2.4 %collective-permute-done.7 = f32[128,384]{0,1:T(8,128)S(1)} collective-permute-done((f32[128,384]{0,1:T(8,128)S(1)}, f32[128,384]{0,1:T(8,128)S(1)}, u32[]{:S(2)}, u32[]{:S(2)}) %collective-permute-start.7) | collective-permute-done | bytes 196640 | tf_op jit(solution)/shard_map/ppermute | solution.py:66
  23.0 3.8 %collective-permute-start.10 = (f32[128,384]{0,1:T(8,128)S(1)}, f32[128,384]{0,1:T(8,128)S(1)}, u32[]{:S(2)}, u32[]{:S(2)}) collective-permute-start(f32[128,384]{0,1:T(8,128)S(1)} %add_add_fusion.2), channel_id=1, source_target_pairs={{0,24},{2,26},{4,28},{6,30},{8,16},{10,18},{12,20},{14,22},{16,8},... | collective-permute-start | bytes 589832 | tf_op jit(solution)/shard_map/ppermute | solution.py:66
  26.8 1.3 collective-permute-start.9
  28.3 1.5 %pad_maximum_fusion.1 = f32[2,8,128,256]{3,2,1,0:T(8,128)} fusion(f32[1,8,128,256]{3,2,1,0:T(8,128)S(1)} %get-tuple-element.10, f32[1,8,128,256]{3,2,1,0:T(8,128)S(1)} %get-tuple-element.9), kind=kLoop, calls=%fused_computation.5 | loop fusion | flops 524288 | bytes 4194304 | tf_op jit(solution)/shard_map/stack | solution.py:146
  29.9 2.6 %collective-permute-start = (f32[2,8,128,256]{3,2,1,0:T(8,128)}, f32[2,8,128,256]{3,2,1,0:T(8,128)}, u32[]{:S(2)}, u32[]{:S(2)}) collective-permute-start(f32[2,8,128,256]{3,2,1,0:T(8,128)} %pad_maximum_fusion.1), channel_id=1, source_target_pairs={{0,2},{2,4},{4,6},{6,8},{8,10},{10,12},{12,14},{14,16},{16,18},{18... | collective-permute-start | bytes 6291464 | tf_op jit(solution)/shard_map/ppermute | solution.py:24
  32.5 1.3 collective-permute-start.1
  33.8 2.1 %collective-permute-done.9 = f32[128,384]{0,1:T(8,128)S(1)} collective-permute-done((f32[128,384]{0,1:T(8,128)S(1)}, f32[128,384]{0,1:T(8,128)S(1)}, u32[]{:S(2)}, u32[]{:S(2)}) %collective-permute-start.9) | collective-permute-done | bytes 196640 | tf_op jit(solution)/shard_map/ppermute | solution.py:66
  35.9 4.9 %collective-permute-start.11 = (f32[128,384]{0,1:T(8,128)S(1)}, f32[128,384]{0,1:T(8,128)S(1)}, u32[]{:S(2)}, u32[]{:S(2)}) collective-permute-start(f32[128,384]{0,1:T(8,128)S(1)} %add_add_fusion.1), channel_id=1, source_target_pairs={{0,32},{2,34},{4,36},{6,38},{8,40},{10,42},{12,44},{14,46},{16,48}... | collective-permute-start | bytes 589832 | tf_op jit(solution)/shard_map/ppermute | solution.py:66
  40.8 2.6 %collective-permute-start.12 = (f32[128,384]{0,1:T(8,128)S(1)}, f32[128,384]{0,1:T(8,128)S(1)}, u32[]{:S(2)}, u32[]{:S(2)}) collective-permute-start(f32[128,384]{0,1:T(8,128)S(1)} %add_add_fusion.1), channel_id=1, source_target_pairs={{0,64},{2,66},{4,68},{6,70},{8,72},{10,74},{12,76},{14,78},{16,80}... | collective-permute-start | bytes 589832 | tf_op jit(solution)/shard_map/ppermute | solution.py:66
  43.5 0.8 collective-permute-done.11
  44.3 4.4 %collective-permute-done.12 = f32[128,384]{0,1:T(8,128)S(1)} collective-permute-done((f32[128,384]{0,1:T(8,128)S(1)}, f32[128,384]{0,1:T(8,128)S(1)}, u32[]{:S(2)}, u32[]{:S(2)}) %collective-permute-start.12) | collective-permute-done | bytes 196640 | tf_op jit(solution)/shard_map/ppermute | solution.py:66
  48.7 2.0 %collective-permute-done.13 = f32[128,384]{0,1:T(8,128)S(1)} collective-permute-done((f32[128,384]{0,1:T(8,128)S(1)}, f32[128,384]{0,1:T(8,128)S(1)}, u32[]{:S(2)}, u32[]{:S(2)}) %collective-permute-start.13) | collective-permute-done | bytes 196640 | tf_op jit(solution)/shard_map/ppermute | solution.py:66
  50.9 0.7 multiply_reduce_fusion
  52.6 0.6 fusion.30
  53.5 0.4 fusion.16
  53.9 0.4 fusion.39
  54.3 0.4 fusion.40
  54.7 0.4 fusion.15
  55.0 0.4 fusion.41
  55.4 0.4 fusion.42
  55.8 0.4 fusion.14
  56.2 0.4 fusion.43
  56.6 0.4 fusion.44
  57.0 0.4 fusion.13
  57.4 0.4 fusion.45
  57.8 0.4 fusion.46
  58.2 0.4 fusion.12
  58.5 0.4 fusion.47
  58.9 0.4 fusion.48
  59.3 0.4 fusion.11
  59.7 0.4 fusion.49
  60.1 0.4 fusion.50
  60.5 0.4 fusion.10
  60.9 1.0 select_reduce_fusion
  62.5 0.4 fusion.9
  62.9 0.4 fusion.22
  63.3 0.4 fusion.8
  64.1 0.4 fusion.7
  64.5 0.4 fusion.52
  64.9 0.4 fusion.6
  65.6 0.4 fusion.5
  66.0 0.6 fusion.54
  66.6 0.4 fusion.4
  67.0 7.7 %collective-permute-done = f32[2,8,128,256]{3,2,1,0:T(8,128)} collective-permute-done((f32[2,8,128,256]{3,2,1,0:T(8,128)}, f32[2,8,128,256]{3,2,1,0:T(8,128)}, u32[]{:S(2)}, u32[]{:S(2)}) %collective-permute-start) | collective-permute-done | bytes 2097184 | tf_op jit(solution)/shard_map/ppermute | solution.py:24
  74.7 5.2 %collective-permute-done.1 = f32[2,8,128,256]{3,2,1,0:T(8,128)} collective-permute-done((f32[2,8,128,256]{3,2,1,0:T(8,128)}, f32[2,8,128,256]{3,2,1,0:T(8,128)}, u32[]{:S(2)}, u32[]{:S(2)}) %collective-permute-start.1) | collective-permute-done | bytes 2097184 | tf_op jit(solution)/shard_map/ppermute | solution.py:24
  79.9 1.2 pad_maximum_fusion.5
  81.0 1.3 collective-permute-start.2
  82.3 32.0 %collective-permute-start.3 = (f32[2,24,8,256]{3,2,1,0:T(8,128)S(1)}, f32[2,24,8,256]{3,2,1,0:T(8,128)S(1)}, u32[]{:S(2)}, u32[]{:S(2)}) collective-permute-start(f32[2,24,8,256]{3,2,1,0:T(8,128)S(1)} %get-tuple-element.8), channel_id=1, source_target_pairs={{1,0},{3,2},{5,4},{7,6},{9,8},{11,10},{13,12},{15,14},{17,16},{19,... | collective-permute-start | bytes 1179656 | tf_op jit(solution)/shard_map/ppermute | solution.py:24
  114.3 0.4 fusion.55
  114.7 0.4 fusion.18
  115.1 0.4 fusion.2
  115.6 2.7 %pad_maximum_fusion = f32[2,24,144,256]{3,2,1,0:T(8,128)S(1)} fusion(f32[2,24,8,256]{3,2,1,0:T(8,128)S(1)} %collective-permute-done.3, f32[2,8,128,256]{3,2,1,0:T(8,128)} %collective-permute-done.1, f32[1,8,128,256]{3,2,1,0:T(8,128)S(1)} %get-tuple-element.10, f32[1,8,128,256]{3,2,1,0:T(8,128)S(1)} %get-tuple-element.9, ...), kind=kLoop, calls=%fused_computation | loop fusion | flops 8847360 | bytes 14155776 | tf_op jit(solution)/shard_map/concatenate | solution.py:54
  118.3 4.7 %fusion = (f32[24,144,256]{2,1,0:T(8,128)}, f32[24,144,256]{2,1,0:T(8,128)S(1)}) fusion(f32[2,24,144,256]{3,2,1,0:T(8,128)S(1)} %pad_maximum_fusion, f32[256,256,1]{1,0,2:T(8,128)S(1)} %fusion.2), kind=kOutput, calls=%fused_computation.2 | convolution fusion | flops 2718793728 | bytes 14417920 | tf_op jit(solution)/shard_map/dot_general | solution.py:28
  123.0 1.1 slice.47
  124.1 0.7 broadcast_in_dim.33.ky_ref
  124.8 0.7 broadcast_in_dim.30.kx_ref
  125.4 16.1 %shard_map.58 = (f32[8,128,256]{2,1,0:T(8,128)}, f32[8,128,256]{2,1,0:T(8,128)}) custom-call(f32[24,144,256]{2,1,0:T(8,128)} %get-tuple-element.15.target_ref, f32[24,1,128]{2,1,0:T(1,128)} %broadcast_in_dim.30.kx_ref, f32[144,128]{1,0:T(8,128)} %broadcast_in_dim.33.ky_ref), custom_call_target="tpu_custom_call" | custom-call | tf_op jit(solution)/shard_map/pallas_call | solution.py:123
  (30 shorter events, 2.1 us)
Async XLA Ops:
  0.6 27.5 %copy-start.2 = (bf16[8,128,256]{2,1,0:T(8,128)(2,1)S(1)}, bf16[8,128,256]{2,1,0:T(8,128)(2,1)}, u32[]{:S(2)}) copy-start(bf16[8,128,256]{2,1,0:T(8,128)(2,1)} %param.3) | copy-start | bytes 1572868
  0.6 27.5 %copy-start.1 = (f32[8,128,256]{2,1,0:T(8,128)S(1)}, f32[8,128,256]{2,1,0:T(8,128)}, u32[]{:S(2)}) copy-start(f32[8,128,256]{2,1,0:T(8,128)} %param.4) | copy-start | bytes 3145732
  0.7 27.5 %copy-start = (f32[8,128,256]{2,1,0:T(8,128)S(1)}, f32[8,128,256]{2,1,0:T(8,128)}, u32[]{:S(2)}) copy-start(f32[8,128,256]{2,1,0:T(8,128)} %param.5) | copy-start | bytes 3145732
  5.3 2.5 %collective-permute-start.4 = (f32[128,384]{0,1:T(8,128)S(1)}, f32[128,384]{0,1:T(8,128)S(1)}, u32[]{:S(2)}, u32[]{:S(2)}) collective-permute-start(f32[128,384]{0,1:T(8,128)S(1)} %pad_maximum_fusion.6), channel_id=1, source_target_pairs={{0,1},{1,0},{2,3},{3,2},{4,5},{5,4},{6,7},{7,6},{8,9},{9,8},{10,11... | collective-permute-start | bytes 589832 | tf_op jit(solution)/shard_map/ppermute | solution.py:70
  7.8 6.2 %collective-permute-start.5 = (f32[128,384]{0,1:T(8,128)S(1)}, f32[128,384]{0,1:T(8,128)S(1)}, u32[]{:S(2)}, u32[]{:S(2)}) collective-permute-start(f32[128,384]{0,1:T(8,128)S(1)} %fusion.37), channel_id=1, source_target_pairs={{0,2},{2,0},{4,6},{6,4},{8,10},{10,8},{12,14},{14,12},{16,18},{18,... | collective-permute-start | bytes 589832 | tf_op jit(solution)/shard_map/ppermute | solution.py:66
  9.2 11.3 %collective-permute-start.6 = (f32[128,384]{0,1:T(8,128)S(1)}, f32[128,384]{0,1:T(8,128)S(1)}, u32[]{:S(2)}, u32[]{:S(2)}) collective-permute-start(f32[128,384]{0,1:T(8,128)S(1)} %fusion.37), channel_id=1, source_target_pairs={{0,4},{2,6},{4,0},{6,2},{8,12},{10,14},{12,8},{14,10},{16,20},{18,... | collective-permute-start | bytes 589832 | tf_op jit(solution)/shard_map/ppermute | solution.py:66
  11.7 11.3 %collective-permute-start.7 = (f32[128,384]{0,1:T(8,128)S(1)}, f32[128,384]{0,1:T(8,128)S(1)}, u32[]{:S(2)}, u32[]{:S(2)}) collective-permute-start(f32[128,384]{0,1:T(8,128)S(1)} %fusion.37), channel_id=1, source_target_pairs={{0,6},{2,4},{4,2},{6,0},{8,14},{10,12},{12,10},{14,8},{16,22},{18,... | collective-permute-start | bytes 589832 | tf_op jit(solution)/shard_map/ppermute | solution.py:66
  23.0 10.8 %collective-permute-start.10 = (f32[128,384]{0,1:T(8,128)S(1)}, f32[128,384]{0,1:T(8,128)S(1)}, u32[]{:S(2)}, u32[]{:S(2)}) collective-permute-start(f32[128,384]{0,1:T(8,128)S(1)} %add_add_fusion.2), channel_id=1, source_target_pairs={{0,24},{2,26},{4,28},{6,30},{8,16},{10,18},{12,20},{14,22},{16,8},... | collective-permute-start | bytes 589832 | tf_op jit(solution)/shard_map/ppermute | solution.py:66
  26.8 7.0 %collective-permute-start.8 = (f32[128,384]{0,1:T(8,128)S(1)}, f32[128,384]{0,1:T(8,128)S(1)}, u32[]{:S(2)}, u32[]{:S(2)}) collective-permute-start(f32[128,384]{0,1:T(8,128)S(1)} %add_add_fusion.2), channel_id=1, source_target_pairs={{0,8},{2,10},{4,12},{6,14},{8,0},{10,2},{12,4},{14,6},{16,24},{18,... | collective-permute-start | bytes 589832 | tf_op jit(solution)/shard_map/ppermute | solution.py:66
  26.8 9.0 %collective-permute-start.9 = (f32[128,384]{0,1:T(8,128)S(1)}, f32[128,384]{0,1:T(8,128)S(1)}, u32[]{:S(2)}, u32[]{:S(2)}) collective-permute-start(f32[128,384]{0,1:T(8,128)S(1)} %add_add_fusion.2), channel_id=1, source_target_pairs={{0,16},{2,18},{4,20},{6,22},{8,24},{10,26},{12,28},{14,30},{16,0},... | collective-permute-start | bytes 589832 | tf_op jit(solution)/shard_map/ppermute | solution.py:66
  29.9 44.8 %collective-permute-start = (f32[2,8,128,256]{3,2,1,0:T(8,128)}, f32[2,8,128,256]{3,2,1,0:T(8,128)}, u32[]{:S(2)}, u32[]{:S(2)}) collective-permute-start(f32[2,8,128,256]{3,2,1,0:T(8,128)} %pad_maximum_fusion.1), channel_id=1, source_target_pairs={{0,2},{2,4},{4,6},{6,8},{8,10},{10,12},{12,14},{14,16},{16,18},{18... | collective-permute-start | bytes 6291464 | tf_op jit(solution)/shard_map/ppermute | solution.py:24
  32.5 47.4 %collective-permute-start.1 = (f32[2,8,128,256]{3,2,1,0:T(8,128)}, f32[2,8,128,256]{3,2,1,0:T(8,128)}, u32[]{:S(2)}, u32[]{:S(2)}) collective-permute-start(f32[2,8,128,256]{3,2,1,0:T(8,128)} %pad_maximum_fusion.1), channel_id=1, source_target_pairs={{2,0},{4,2},{6,4},{8,6},{10,8},{12,10},{14,12},{16,14},{18,16},{20... | collective-permute-start | bytes 6291464 | tf_op jit(solution)/shard_map/ppermute | solution.py:24
  35.9 8.4 %collective-permute-start.11 = (f32[128,384]{0,1:T(8,128)S(1)}, f32[128,384]{0,1:T(8,128)S(1)}, u32[]{:S(2)}, u32[]{:S(2)}) collective-permute-start(f32[128,384]{0,1:T(8,128)S(1)} %add_add_fusion.1), channel_id=1, source_target_pairs={{0,32},{2,34},{4,36},{6,38},{8,40},{10,42},{12,44},{14,46},{16,48}... | collective-permute-start | bytes 589832 | tf_op jit(solution)/shard_map/ppermute | solution.py:66
  40.8 7.9 %collective-permute-start.12 = (f32[128,384]{0,1:T(8,128)S(1)}, f32[128,384]{0,1:T(8,128)S(1)}, u32[]{:S(2)}, u32[]{:S(2)}) collective-permute-start(f32[128,384]{0,1:T(8,128)S(1)} %add_add_fusion.1), channel_id=1, source_target_pairs={{0,64},{2,66},{4,68},{6,70},{8,72},{10,74},{12,76},{14,78},{16,80}... | collective-permute-start | bytes 589832 | tf_op jit(solution)/shard_map/ppermute | solution.py:66
  43.5 7.3 %collective-permute-start.13 = (f32[128,384]{0,1:T(8,128)S(1)}, f32[128,384]{0,1:T(8,128)S(1)}, u32[]{:S(2)}, u32[]{:S(2)}) collective-permute-start(f32[128,384]{0,1:T(8,128)S(1)} %add_add_fusion.1), channel_id=1, source_target_pairs={{0,96},{2,98},{4,100},{6,102},{8,104},{10,106},{12,108},{14,110},{... | collective-permute-start | bytes 589832 | tf_op jit(solution)/shard_map/ppermute | solution.py:66
  81.0 34.4 %collective-permute-start.2 = (f32[2,24,8,256]{3,2,1,0:T(8,128)S(1)}, f32[2,24,8,256]{3,2,1,0:T(8,128)S(1)}, u32[]{:S(2)}, u32[]{:S(2)}) collective-permute-start(f32[2,24,8,256]{3,2,1,0:T(8,128)S(1)} %get-tuple-element.7), channel_id=1, source_target_pairs={{0,1},{2,3},{4,5},{6,7},{8,9},{10,11},{12,13},{14,15},{16,17},{18,... | collective-permute-start | bytes 1179656 | tf_op jit(solution)/shard_map/ppermute | solution.py:24
  82.3 33.3 %collective-permute-start.3 = (f32[2,24,8,256]{3,2,1,0:T(8,128)S(1)}, f32[2,24,8,256]{3,2,1,0:T(8,128)S(1)}, u32[]{:S(2)}, u32[]{:S(2)}) collective-permute-start(f32[2,24,8,256]{3,2,1,0:T(8,128)S(1)} %get-tuple-element.8), channel_id=1, source_target_pairs={{1,0},{3,2},{5,4},{7,6},{9,8},{11,10},{13,12},{15,14},{17,16},{19,... | collective-permute-start | bytes 1179656 | tf_op jit(solution)/shard_map/ppermute | solution.py:24

commit v5 on v4

--- a/solution.py
+++ b/solution.py
@@ -60,15 +60,17 @@
         if length & (length - 1):
             x = lax.psum(x, axis)
             continue
-        step = 1
+        groups, step = [], 1
         while step < length:
-            if 4 * step <= length:
+            radix = 4 if 4 * step <= length else 2
+            groups.append((step, radix))
+            step *= radix
+        for step, radix in groups[1:] + groups[:1]:
+            if radix == 4:
                 r1, r2, r3 = (lax.ppermute(x, axis, [(i, i ^ (k * step)) for i in range(length)]) for k in (1, 2, 3))
                 x = (x + r1) + (r2 + r3)
-                step *= 4
             else:
                 x = x + lax.ppermute(x, axis, [(i, i ^ step) for i in range(length)])
-                step *= 2
     return x
 
 

time: 142 us -> 142 us (level)
  the two profiles are of different devices: /device:TPU:1 before, /device:TPU:8 now
where the time goes in v5:
time: 142 us; the launch traced here: 140 us
  waiting for transfers between devices  61.4 us (43%)
  starting transfers between devices  26.7 us (19%)
  matrix products  24.2 us (17%)
  Pallas kernels  16.1 us (11%)
  other arithmetic  6.41 us (5%)
  local copies, waits for them, and re-layouts  2.59 us (2%)
  between operations  2.5 us (2%)
    ppermute x9, waiting for transfers between devices, all_sum(): lax.ppermute(x, axis, [(i, i ^ k * step) for i in range(length)])  58.8 us
    dot_general x39, matrix products, matmul(): jnp.dot(left, right, precision=lax.Precision.HIGHEST, preferred_element_t...  24.2 us
    pallas_call x1, Pallas kernels, tv_local(): pl.pallas_call(tv_kernel, grid=(frames // lanes,), in_specs=[pl.BlockSpec...  16.1 us
    ppermute x9, starting transfers between devices, all_sum(): lax.ppermute(x, axis, [(i, i ^ k * step) for i in range(length)])  13.9 us
    ppermute x4, starting transfers between devices, shifted(): return lax.ppermute(x, axis, pairs)  12.7 us
  transfers between devices with their start and end apart: 14, of which 8 were waited for; matrix products, arithmetic and copies ran while one was open for 13% of the time, Pallas kernels for 0%

profile of v5, /device:TPU:8, one launch (start us, length us, event | category | flops | bytes accessed | tf_op | source)
XLA Modules:
  0.0 139.9 jit_solution(10846455505456459324)
XLA Ops:
  0.7 4.5 %convolution_bitcast_fusion = f32[256,256]{0,1:T(8,128)S(1)} fusion(f32[8,128,256]{2,1,0:T(8,128)} %param.5, f32[8,128,256]{2,1,0:T(8,128)} %param.4, bf16[8,128,256]{2,1,0:T(8,128)(2,1)} %param.3), kind=kOutput, calls=%fused_computation.41 | convolution fusion | flops 806092800 | bytes 2883584 | tf_op jit(solution)/shard_map/dot_general | solution.py:28
  5.3 1.4 %collective-permute-done.4 = f32[128,384]{0,1:T(8,128)S(1)} collective-permute-done((f32[128,384]{0,1:T(8,128)S(1)}, f32[128,384]{0,1:T(8,128)S(1)}, u32[]{:S(2)}, u32[]{:S(2)}) %collective-permute-start.4) | collective-permute-done | bytes 196640 | tf_op jit(solution)/shard_map/ppermute | solution.py:73
  6.8 2.0 %collective-permute-start.5 = (f32[128,384]{0,1:T(8,128)S(1)}, f32[128,384]{0,1:T(8,128)S(1)}, u32[]{:S(2)}, u32[]{:S(2)}) collective-permute-start(f32[128,384]{0,1:T(8,128)S(1)} %fusion.37), channel_id=1, source_target_pairs={{0,8},{2,10},{4,12},{6,14},{8,0},{10,2},{12,4},{14,6},{16,24},{18,... | collective-permute-start | bytes 589832 | tf_op jit(solution)/shard_map/ppermute | solution.py:70
  8.8 3.6 %collective-permute-start.6 = (f32[128,384]{0,1:T(8,128)S(1)}, f32[128,384]{0,1:T(8,128)S(1)}, u32[]{:S(2)}, u32[]{:S(2)}) collective-permute-start(f32[128,384]{0,1:T(8,128)S(1)} %fusion.37), channel_id=1, source_target_pairs={{0,16},{2,18},{4,20},{6,22},{8,24},{10,26},{12,28},{14,30},{16,0},... | collective-permute-start | bytes 589832 | tf_op jit(solution)/shard_map/ppermute | solution.py:70
  12.4 2.3 %collective-permute-done.5 = f32[128,384]{0,1:T(8,128)S(1)} collective-permute-done((f32[128,384]{0,1:T(8,128)S(1)}, f32[128,384]{0,1:T(8,128)S(1)}, u32[]{:S(2)}, u32[]{:S(2)}) %collective-permute-start.5) | collective-permute-done | bytes 196640 | tf_op jit(solution)/shard_map/ppermute | solution.py:70
  14.7 7.0 %collective-permute-done.6 = f32[128,384]{0,1:T(8,128)S(1)} collective-permute-done((f32[128,384]{0,1:T(8,128)S(1)}, f32[128,384]{0,1:T(8,128)S(1)}, u32[]{:S(2)}, u32[]{:S(2)}) %collective-permute-start.6) | collective-permute-done | bytes 196640 | tf_op jit(solution)/shard_map/ppermute | solution.py:70
  21.6 2.6 %collective-permute-done.7 = f32[128,384]{0,1:T(8,128)S(1)} collective-permute-done((f32[128,384]{0,1:T(8,128)S(1)}, f32[128,384]{0,1:T(8,128)S(1)}, u32[]{:S(2)}, u32[]{:S(2)}) %collective-permute-start.7) | collective-permute-done | bytes 196640 | tf_op jit(solution)/shard_map/ppermute | solution.py:70
  24.2 1.7 %collective-permute-start.10 = (f32[128,384]{0,1:T(8,128)S(1)}, f32[128,384]{0,1:T(8,128)S(1)}, u32[]{:S(2)}, u32[]{:S(2)}) collective-permute-start(f32[128,384]{0,1:T(8,128)S(1)} %add_add_fusion.2), channel_id=1, source_target_pairs={{0,96},{2,98},{4,100},{6,102},{8,104},{10,106},{12,108},{14,110},{... | collective-permute-start | bytes 589832 | tf_op jit(solution)/shard_map/ppermute | solution.py:70
  25.9 1.9 %collective-permute-start.8 = (f32[128,384]{0,1:T(8,128)S(1)}, f32[128,384]{0,1:T(8,128)S(1)}, u32[]{:S(2)}, u32[]{:S(2)}) collective-permute-start(f32[128,384]{0,1:T(8,128)S(1)} %add_add_fusion.2), channel_id=1, source_target_pairs={{0,32},{2,34},{4,36},{6,38},{8,40},{10,42},{12,44},{14,46},{16,48}... | collective-permute-start | bytes 589832 | tf_op jit(solution)/shard_map/ppermute | solution.py:70
  28.0 1.5 %pad_maximum_fusion.1 = f32[2,8,128,256]{3,2,1,0:T(8,128)} fusion(f32[1,8,128,256]{3,2,1,0:T(8,128)S(1)} %get-tuple-element.10, f32[1,8,128,256]{3,2,1,0:T(8,128)S(1)} %get-tuple-element.9), kind=kLoop, calls=%fused_computation.5 | loop fusion | flops 524288 | bytes 4194304 | tf_op jit(solution)/shard_map/stack | solution.py:148
  29.5 3.4 %collective-permute-start = (f32[2,8,128,256]{3,2,1,0:T(8,128)}, f32[2,8,128,256]{3,2,1,0:T(8,128)}, u32[]{:S(2)}, u32[]{:S(2)}) collective-permute-start(f32[2,8,128,256]{3,2,1,0:T(8,128)} %pad_maximum_fusion.1), channel_id=1, source_target_pairs={{0,2},{2,4},{4,6},{6,8},{8,10},{10,12},{12,14},{14,16},{16,18},{18... | collective-permute-start | bytes 6291464 | tf_op jit(solution)/shard_map/ppermute | solution.py:24
  32.9 6.7 %collective-permute-start.1 = (f32[2,8,128,256]{3,2,1,0:T(8,128)}, f32[2,8,128,256]{3,2,1,0:T(8,128)}, u32[]{:S(2)}, u32[]{:S(2)}) collective-permute-start(f32[2,8,128,256]{3,2,1,0:T(8,128)} %pad_maximum_fusion.1), channel_id=1, source_target_pairs={{2,0},{4,2},{6,4},{8,6},{10,8},{12,10},{14,12},{16,14},{18,16},{20... | collective-permute-start | bytes 6291464 | tf_op jit(solution)/shard_map/ppermute | solution.py:24
  40.0 4.5 %collective-permute-start.13 = (f32[128,384]{0,1:T(8,128)S(1)}, f32[128,384]{0,1:T(8,128)S(1)}, u32[]{:S(2)}, u32[]{:S(2)}) collective-permute-start(f32[128,384]{0,1:T(8,128)S(1)} %add_add_fusion.1), channel_id=1, source_target_pairs={{0,6},{2,4},{4,2},{6,0},{8,14},{10,12},{12,10},{14,8},{16,22},{18,... | collective-permute-start | bytes 589832 | tf_op jit(solution)/shard_map/ppermute | solution.py:70
  44.5 42.6 %collective-permute-done.11 = f32[128,384]{0,1:T(8,128)S(1)} collective-permute-done((f32[128,384]{0,1:T(8,128)S(1)}, f32[128,384]{0,1:T(8,128)S(1)}, u32[]{:S(2)}, u32[]{:S(2)}) %collective-permute-start.11) | collective-permute-done | bytes 196640 | tf_op jit(solution)/shard_map/ppermute | solution.py:70
  87.1 1.2 collective-permute-done.12
  88.3 3.2 %collective-permute-done.13 = f32[128,384]{0,1:T(8,128)S(1)} collective-permute-done((f32[128,384]{0,1:T(8,128)S(1)}, f32[128,384]{0,1:T(8,128)S(1)}, u32[]{:S(2)}, u32[]{:S(2)}) %collective-permute-start.13) | collective-permute-done | bytes 196640 | tf_op jit(solution)/shard_map/ppermute | solution.py:70
  91.7 0.7 multiply_reduce_fusion
  93.0 0.3 fusion.17
  93.4 0.6 fusion.30
  94.0 0.3 fusion.21
  94.3 0.4 fusion.16
  94.7 0.4 fusion.39
  95.0 0.4 fusion.40
  95.4 0.4 fusion.15
  95.8 0.4 fusion.41
  96.2 0.4 fusion.42
  96.6 0.4 fusion.14
  97.0 0.4 fusion.43
  97.4 0.4 fusion.44
  97.8 0.4 fusion.13
  98.2 0.4 fusion.45
  98.5 0.4 fusion.46
  98.9 0.4 fusion.12
  99.3 0.4 fusion.47
  99.7 0.4 fusion.48
  100.1 0.4 fusion.11
  100.5 0.4 fusion.49
  100.9 0.4 fusion.50
  101.2 0.4 fusion.10
  101.6 1.0 select_reduce_fusion
  103.3 0.4 fusion.9
  103.7 0.4 fusion.22
  104.1 0.4 fusion.8
  104.5 0.4 fusion.51
  104.9 0.4 fusion.7
  105.2 0.4 fusion.52
  105.6 0.4 fusion.6
  106.0 0.4 fusion.53
  106.4 0.4 fusion.5
  106.8 0.6 fusion.54
  107.4 0.4 fusion.4
  107.8 1.2 pad_maximum_fusion.5
  109.0 1.3 collective-permute-start.2
  110.3 1.3 collective-permute-start.3
  111.6 0.4 fusion.55
  112.0 0.4 fusion.18
  112.4 0.4 fusion.2
  112.8 1.1 collective-permute-done.3
  113.9 2.7 %pad_maximum_fusion = f32[2,24,144,256]{3,2,1,0:T(8,128)S(1)} fusion(f32[2,24,8,256]{3,2,1,0:T(8,128)S(1)} %collective-permute-done.3, f32[2,8,128,256]{3,2,1,0:T(8,128)} %collective-permute-done.1, f32[1,8,128,256]{3,2,1,0:T(8,128)S(1)} %get-tuple-element.10, f32[1,8,128,256]{3,2,1,0:T(8,128)S(1)} %get-tuple-element.9, ...), kind=kLoop, calls=%fused_computation | loop fusion | flops 8847360 | bytes 14155776 | tf_op jit(solution)/shard_map/concatenate | solution.py:54
  116.6 4.7 %fusion = (f32[24,144,256]{2,1,0:T(8,128)}, f32[24,144,256]{2,1,0:T(8,128)S(1)}) fusion(f32[2,24,144,256]{3,2,1,0:T(8,128)S(1)} %pad_maximum_fusion, f32[256,256,1]{1,0,2:T(8,128)S(1)} %fusion.2), kind=kOutput, calls=%fused_computation.2 | convolution fusion | flops 2718793728 | bytes 14417920 | tf_op jit(solution)/shard_map/dot_general | solution.py:28
  121.3 1.1 slice.47
  122.4 0.7 broadcast_in_dim.33.ky_ref
  123.1 0.7 broadcast_in_dim.30.kx_ref
  123.8 16.1 %shard_map.58 = (f32[8,128,256]{2,1,0:T(8,128)}, f32[8,128,256]{2,1,0:T(8,128)}) custom-call(f32[24,144,256]{2,1,0:T(8,128)} %get-tuple-element.15.target_ref, f32[24,1,128]{2,1,0:T(1,128)} %broadcast_in_dim.30.kx_ref, f32[144,128]{1,0:T(8,128)} %broadcast_in_dim.33.ky_ref), custom_call_target="tpu_custom_call" | custom-call | tf_op jit(solution)/shard_map/pallas_call | solution.py:125
  (30 shorter events, 0.9 us)
Async XLA Ops:
  0.6 27.2 %copy-start.2 = (bf16[8,128,256]{2,1,0:T(8,128)(2,1)S(1)}, bf16[8,128,256]{2,1,0:T(8,128)(2,1)}, u32[]{:S(2)}) copy-start(bf16[8,128,256]{2,1,0:T(8,128)(2,1)} %param.3) | copy-start | bytes 1572868
  0.6 27.2 %copy-start.1 = (f32[8,128,256]{2,1,0:T(8,128)S(1)}, f32[8,128,256]{2,1,0:T(8,128)}, u32[]{:S(2)}) copy-start(f32[8,128,256]{2,1,0:T(8,128)} %param.4) | copy-start | bytes 3145732
  0.7 27.2 %copy-start = (f32[8,128,256]{2,1,0:T(8,128)S(1)}, f32[8,128,256]{2,1,0:T(8,128)}, u32[]{:S(2)}) copy-start(f32[8,128,256]{2,1,0:T(8,128)} %param.5) | copy-start | bytes 3145732
  5.3 1.5 %collective-permute-start.4 = (f32[128,384]{0,1:T(8,128)S(1)}, f32[128,384]{0,1:T(8,128)S(1)}, u32[]{:S(2)}, u32[]{:S(2)}) collective-permute-start(f32[128,384]{0,1:T(8,128)S(1)} %pad_maximum_fusion.6), channel_id=1, source_target_pairs={{0,1},{1,0},{2,3},{3,2},{4,5},{5,4},{6,7},{7,6},{8,9},{9,8},{10,11... | collective-permute-start | bytes 589832 | tf_op jit(solution)/shard_map/ppermute | solution.py:73
  6.8 7.9 %collective-permute-start.5 = (f32[128,384]{0,1:T(8,128)S(1)}, f32[128,384]{0,1:T(8,128)S(1)}, u32[]{:S(2)}, u32[]{:S(2)}) collective-permute-start(f32[128,384]{0,1:T(8,128)S(1)} %fusion.37), channel_id=1, source_target_pairs={{0,8},{2,10},{4,12},{6,14},{8,0},{10,2},{12,4},{14,6},{16,24},{18,... | collective-permute-start | bytes 589832 | tf_op jit(solution)/shard_map/ppermute | solution.py:70
  8.8 12.8 %collective-permute-start.6 = (f32[128,384]{0,1:T(8,128)S(1)}, f32[128,384]{0,1:T(8,128)S(1)}, u32[]{:S(2)}, u32[]{:S(2)}) collective-permute-start(f32[128,384]{0,1:T(8,128)S(1)} %fusion.37), channel_id=1, source_target_pairs={{0,16},{2,18},{4,20},{6,22},{8,24},{10,26},{12,28},{14,30},{16,0},... | collective-permute-start | bytes 589832 | tf_op jit(solution)/shard_map/ppermute | solution.py:70
  12.4 11.8 %collective-permute-start.7 = (f32[128,384]{0,1:T(8,128)S(1)}, f32[128,384]{0,1:T(8,128)S(1)}, u32[]{:S(2)}, u32[]{:S(2)}) collective-permute-start(f32[128,384]{0,1:T(8,128)S(1)} %fusion.37), channel_id=1, source_target_pairs={{0,24},{2,26},{4,28},{6,30},{8,16},{10,18},{12,20},{14,22},{16,8},... | collective-permute-start | bytes 589832 | tf_op jit(solution)/shard_map/ppermute | solution.py:70
  24.2 15.4 %collective-permute-start.10 = (f32[128,384]{0,1:T(8,128)S(1)}, f32[128,384]{0,1:T(8,128)S(1)}, u32[]{:S(2)}, u32[]{:S(2)}) collective-permute-start(f32[128,384]{0,1:T(8,128)S(1)} %add_add_fusion.2), channel_id=1, source_target_pairs={{0,96},{2,98},{4,100},{6,102},{8,104},{10,106},{12,108},{14,110},{... | collective-permute-start | bytes 589832 | tf_op jit(solution)/shard_map/ppermute | solution.py:70
  25.9 13.7 %collective-permute-start.8 = (f32[128,384]{0,1:T(8,128)S(1)}, f32[128,384]{0,1:T(8,128)S(1)}, u32[]{:S(2)}, u32[]{:S(2)}) collective-permute-start(f32[128,384]{0,1:T(8,128)S(1)} %add_add_fusion.2), channel_id=1, source_target_pairs={{0,32},{2,34},{4,36},{6,38},{8,40},{10,42},{12,44},{14,46},{16,48}... | collective-permute-start | bytes 589832 | tf_op jit(solution)/shard_map/ppermute | solution.py:70
  27.8 11.9 %collective-permute-start.9 = (f32[128,384]{0,1:T(8,128)S(1)}, f32[128,384]{0,1:T(8,128)S(1)}, u32[]{:S(2)}, u32[]{:S(2)}) collective-permute-start(f32[128,384]{0,1:T(8,128)S(1)} %add_add_fusion.2), channel_id=1, source_target_pairs={{0,64},{2,66},{4,68},{6,70},{8,72},{10,74},{12,76},{14,78},{16,80}... | collective-permute-start | bytes 589832 | tf_op jit(solution)/shard_map/ppermute | solution.py:70
  29.5 78.3 %collective-permute-start = (f32[2,8,128,256]{3,2,1,0:T(8,128)}, f32[2,8,128,256]{3,2,1,0:T(8,128)}, u32[]{:S(2)}, u32[]{:S(2)}) collective-permute-start(f32[2,8,128,256]{3,2,1,0:T(8,128)} %pad_maximum_fusion.1), channel_id=1, source_target_pairs={{0,2},{2,4},{4,6},{6,8},{8,10},{10,12},{12,14},{14,16},{16,18},{18... | collective-permute-start | bytes 6291464 | tf_op jit(solution)/shard_map/ppermute | solution.py:24
  32.9 74.9 %collective-permute-start.1 = (f32[2,8,128,256]{3,2,1,0:T(8,128)}, f32[2,8,128,256]{3,2,1,0:T(8,128)}, u32[]{:S(2)}, u32[]{:S(2)}) collective-permute-start(f32[2,8,128,256]{3,2,1,0:T(8,128)} %pad_maximum_fusion.1), channel_id=1, source_target_pairs={{2,0},{4,2},{6,4},{8,6},{10,8},{12,10},{14,12},{16,14},{18,16},{20... | collective-permute-start | bytes 6291464 | tf_op jit(solution)/shard_map/ppermute | solution.py:24
  39.7 47.4 %collective-permute-start.11 = (f32[128,384]{0,1:T(8,128)S(1)}, f32[128,384]{0,1:T(8,128)S(1)}, u32[]{:S(2)}, u32[]{:S(2)}) collective-permute-start(f32[128,384]{0,1:T(8,128)S(1)} %add_add_fusion.1), channel_id=1, source_target_pairs={{0,2},{2,0},{4,6},{6,4},{8,10},{10,8},{12,14},{14,12},{16,18},{18,... | collective-permute-start | bytes 589832 | tf_op jit(solution)/shard_map/ppermute | solution.py:70
  39.8 48.5 %collective-permute-start.12 = (f32[128,384]{0,1:T(8,128)S(1)}, f32[128,384]{0,1:T(8,128)S(1)}, u32[]{:S(2)}, u32[]{:S(2)}) collective-permute-start(f32[128,384]{0,1:T(8,128)S(1)} %add_add_fusion.1), channel_id=1, source_target_pairs={{0,4},{2,6},{4,0},{6,2},{8,12},{10,14},{12,8},{14,10},{16,20},{18,... | collective-permute-start | bytes 589832 | tf_op jit(solution)/shard_map/ppermute | solution.py:70
  40.0 51.5 %collective-permute-start.13 = (f32[128,384]{0,1:T(8,128)S(1)}, f32[128,384]{0,1:T(8,128)S(1)}, u32[]{:S(2)}, u32[]{:S(2)}) collective-permute-start(f32[128,384]{0,1:T(8,128)S(1)} %add_add_fusion.1), channel_id=1, source_target_pairs={{0,6},{2,4},{4,2},{6,0},{8,14},{10,12},{12,10},{14,8},{16,22},{18,... | collective-permute-start | bytes 589832 | tf_op jit(solution)/shard_map/ppermute | solution.py:70
  109.0 3.8 %collective-permute-start.2 = (f32[2,24,8,256]{3,2,1,0:T(8,128)S(1)}, f32[2,24,8,256]{3,2,1,0:T(8,128)S(1)}, u32[]{:S(2)}, u32[]{:S(2)}) collective-permute-start(f32[2,24,8,256]{3,2,1,0:T(8,128)S(1)} %get-tuple-element.7), channel_id=1, source_target_pairs={{0,1},{2,3},{4,5},{6,7},{8,9},{10,11},{12,13},{14,15},{16,17},{18,... | collective-permute-start | bytes 1179656 | tf_op jit(solution)/shard_map/ppermute | solution.py:24
  110.3 3.6 %collective-permute-start.3 = (f32[2,24,8,256]{3,2,1,0:T(8,128)S(1)}, f32[2,24,8,256]{3,2,1,0:T(8,128)S(1)}, u32[]{:S(2)}, u32[]{:S(2)}) collective-permute-start(f32[2,24,8,256]{3,2,1,0:T(8,128)S(1)} %get-tuple-element.8), channel_id=1, source_target_pairs={{1,0},{3,2},{5,4},{7,6},{9,8},{11,10},{13,12},{15,14},{17,16},{19,... | collective-permute-start | bytes 1179656 | tf_op jit(solution)/shard_map/ppermute | solution.py:24

commit v6 on v5

--- a/solution.py
+++ b/solution.py
@@ -4,7 +4,6 @@
 from jax.sharding import PartitionSpec as P
 from jax.experimental import pallas as pl
 from jax.experimental.pallas import tpu as pltpu
-
 
 K_ROOT = 8
 K_SIGN = 6
@@ -65,7 +64,7 @@
             radix = 4 if 4 * step <= length else 2
             groups.append((step, radix))
             step *= radix
-        for step, radix in groups[1:] + groups[:1]:
+        for step, radix in groups:
             if radix == 4:
                 r1, r2, r3 = (lax.ppermute(x, axis, [(i, i ^ (k * step)) for i in range(length)]) for k in (1, 2, 3))
                 x = (x + r1) + (r2 + r3)
@@ -144,15 +143,13 @@
     total_cols = cols_here * lax.axis_size("cols")
     observed = video.astype(jnp.float32)
     mixed = observed - foreground + scaled_dual
-    a = observed + scaled_dual
-    ext = with_halo(jnp.stack([a, mixed]))
-    a_ext, mixed_ext = ext[0], ext[1]
     flat = mixed.reshape(-1, frames)
     gram = summed_gram(flat)
     shrink = shrink_matrix(gram)
+    background = matmul(flat, shrink).reshape(foreground.shape)
+    target = observed - background + scaled_dual
+    target = with_halo(target[None])[0]
     ext_rows, ext_cols = rows_here + 2 * HALO, cols_here + 2 * HALO
-    background_ext = matmul(mixed_ext.reshape(-1, frames), shrink).reshape(ext_rows, ext_cols, frames)
-    target = a_ext - background_ext
 
     first_row = lax.axis_index("rows") * rows_here - HALO
     first_col = lax.axis_index("cols") * cols_here - HALO
@@ -164,8 +161,6 @@
     kx = jnp.broadcast_to(jnp.where(keep_x, 1.0, 0.0).astype(jnp.float32), (ext_rows, 1, lanes))
     ky = jnp.broadcast_to(jnp.where(keep_y, 1.0, 0.0).astype(jnp.float32)[0], (ext_cols, lanes))
     new_foreground, new_dual = tv_local(target, kx, ky)
-    inner = (slice(HALO, HALO + rows_here), slice(HALO, HALO + cols_here))
-    background = background_ext[inner]
     return (background, new_foreground, new_dual)
 
 

time: 142 us -> 127 us (0.89)
  the two profiles are of different devices: /device:TPU:8 before, /device:TPU:119 now
where the time goes in v6:
time: 127 us
  waiting for transfers between devices  52.8 us (42%)
  starting transfers between devices  29.4 us (23%)
  matrix products  20.5 us (16%)
  Pallas kernels  16.1 us (13%)
  other arithmetic  3.11 us (2%)
  between operations  2.48 us (2%)
  local copies, waits for them, and re-layouts  2.33 us (2%)
    ppermute x4, waiting for transfers between devices, shifted(): return lax.ppermute(x, axis, pairs)  27.9 us
    ppermute x9, waiting for transfers between devices, all_sum(): lax.ppermute(x, axis, [(i, i ^ k * step) for i in range(length)])  23.8 us
    dot_general x39, matrix products, matmul(): jnp.dot(left, right, precision=lax.Precision.HIGHEST, preferred_element_t...  20.5 us
    ppermute x4, starting transfers between devices, shifted(): return lax.ppermute(x, axis, pairs)  18.1 us
    pallas_call x1, Pallas kernels, tv_local(): pl.pallas_call(tv_kernel, grid=(frames // lanes,), in_specs=[pl.BlockSpec...  16.1 us
    ppermute x9, starting transfers between devices, all_sum(): lax.ppermute(x, axis, [(i, i ^ k * step) for i in range(length)])  10.6 us
  transfers between devices with their start and end apart: 14, of which 12 were waited for; matrix products, arithmetic and copies ran while one was open for 0% of the time, Pallas kernels for 0%

profile of v6, /device:TPU:119, one launch (start us, length us, event | category | flops | bytes accessed | tf_op | source)
XLA Modules:
  0.0 126.8 jit_solution(5317415984789775737)
XLA Ops:
  0.6 4.5 %convolution_bitcast_fusion = f32[256,256]{0,1:T(8,128)S(1)} fusion(f32[8,128,256]{2,1,0:T(8,128)} %param.5, f32[8,128,256]{2,1,0:T(8,128)} %param.4, bf16[8,128,256]{2,1,0:T(8,128)(2,1)} %param.3), kind=kOutput, calls=%fused_computation.36 | convolution fusion | flops 806092800 | bytes 2883584 | tf_op jit(solution)/shard_map/dot_general | solution.py:27
  5.2 0.8 collective-permute-start
  5.9 1.1 collective-permute-done
  7.0 0.6 collective-permute-start.1
  7.6 0.8 collective-permute-start.2
  8.5 2.5 %collective-permute-start.3 = (f32[128,384]{0,1:T(8,128)S(1)}, f32[128,384]{0,1:T(8,128)S(1)}, u32[]{:S(2)}, u32[]{:S(2)}) collective-permute-start(f32[128,384]{0,1:T(8,128)S(1)} %fusion.37), channel_id=1, source_target_pairs={{0,6},{2,4},{4,2},{6,0},{8,14},{10,12},{12,10},{14,8},{16,22},{18,... | collective-permute-start | bytes 589832 | tf_op jit(solution)/shard_map/ppermute | solution.py:69
  10.9 2.2 %collective-permute-done.1 = f32[128,384]{0,1:T(8,128)S(1)} collective-permute-done((f32[128,384]{0,1:T(8,128)S(1)}, f32[128,384]{0,1:T(8,128)S(1)}, u32[]{:S(2)}, u32[]{:S(2)}) %collective-permute-start.1) | collective-permute-done | bytes 196640 | tf_op jit(solution)/shard_map/ppermute | solution.py:69
  13.2 4.2 %collective-permute-done.2 = f32[128,384]{0,1:T(8,128)S(1)} collective-permute-done((f32[128,384]{0,1:T(8,128)S(1)}, f32[128,384]{0,1:T(8,128)S(1)}, u32[]{:S(2)}, u32[]{:S(2)}) %collective-permute-start.2) | collective-permute-done | bytes 196640 | tf_op jit(solution)/shard_map/ppermute | solution.py:69
  17.3 2.4 %collective-permute-done.3 = f32[128,384]{0,1:T(8,128)S(1)} collective-permute-done((f32[128,384]{0,1:T(8,128)S(1)}, f32[128,384]{0,1:T(8,128)S(1)}, u32[]{:S(2)}, u32[]{:S(2)}) %collective-permute-start.3) | collective-permute-done | bytes 196640 | tf_op jit(solution)/shard_map/ppermute | solution.py:69
  20.3 3.5 %collective-permute-start.6 = (f32[128,384]{0,1:T(8,128)S(1)}, f32[128,384]{0,1:T(8,128)S(1)}, u32[]{:S(2)}, u32[]{:S(2)}) collective-permute-start(f32[128,384]{0,1:T(8,128)S(1)} %add_add_fusion.2), channel_id=1, source_target_pairs={{0,24},{2,26},{4,28},{6,30},{8,16},{10,18},{12,20},{14,22},{16,8},... | collective-permute-start | bytes 589832 | tf_op jit(solution)/shard_map/ppermute | solution.py:69
  23.7 1.2 collective-permute-done.4
  24.9 3.6 %collective-permute-done.5 = f32[128,384]{0,1:T(8,128)S(1)} collective-permute-done((f32[128,384]{0,1:T(8,128)S(1)}, f32[128,384]{0,1:T(8,128)S(1)}, u32[]{:S(2)}, u32[]{:S(2)}) %collective-permute-start.5) | collective-permute-done | bytes 196640 | tf_op jit(solution)/shard_map/ppermute | solution.py:69
  28.5 3.4 %collective-permute-done.6 = f32[128,384]{0,1:T(8,128)S(1)} collective-permute-done((f32[128,384]{0,1:T(8,128)S(1)}, f32[128,384]{0,1:T(8,128)S(1)}, u32[]{:S(2)}, u32[]{:S(2)}) %collective-permute-start.6) | collective-permute-done | bytes 196640 | tf_op jit(solution)/shard_map/ppermute | solution.py:69
  32.0 1.1 collective-permute-start.7
  33.4 1.3 %collective-permute-start.9 = (f32[128,384]{0,1:T(8,128)S(1)}, f32[128,384]{0,1:T(8,128)S(1)}, u32[]{:S(2)}, u32[]{:S(2)}) collective-permute-start(f32[128,384]{0,1:T(8,128)S(1)} %add_add_fusion.1), channel_id=1, source_target_pairs={{0,96},{2,98},{4,100},{6,102},{8,104},{10,106},{12,108},{14,110},{... | collective-permute-start | bytes 589832 | tf_op jit(solution)/shard_map/ppermute | solution.py:69
  34.7 2.3 %collective-permute-done.7 = f32[128,384]{0,1:T(8,128)S(1)} collective-permute-done((f32[128,384]{0,1:T(8,128)S(1)}, f32[128,384]{0,1:T(8,128)S(1)}, u32[]{:S(2)}, u32[]{:S(2)}) %collective-permute-start.7) | collective-permute-done | bytes 196640 | tf_op jit(solution)/shard_map/ppermute | solution.py:69
  37.0 4.5 %collective-permute-done.8 = f32[128,384]{0,1:T(8,128)S(1)} collective-permute-done((f32[128,384]{0,1:T(8,128)S(1)}, f32[128,384]{0,1:T(8,128)S(1)}, u32[]{:S(2)}, u32[]{:S(2)}) %collective-permute-start.8) | collective-permute-done | bytes 196640 | tf_op jit(solution)/shard_map/ppermute | solution.py:69
  41.7 0.7 multiply_reduce_fusion
  43.4 0.6 fusion.30
  44.3 0.4 fusion.14
  44.7 0.4 fusion.39
  45.1 0.4 fusion.40
  45.5 0.4 fusion.13
  45.8 0.4 fusion.41
  46.2 0.4 fusion.42
  46.6 0.4 fusion.12
  47.0 0.4 fusion.43
  47.4 0.4 fusion.44
  47.8 0.4 fusion.11
  48.2 0.4 fusion.45
  48.6 0.4 fusion.46
  48.9 0.4 fusion.10
  49.3 0.4 fusion.47
  49.7 0.4 fusion.48
  50.1 0.4 fusion.9
  50.5 0.4 fusion.49
  50.9 0.4 fusion.50
  51.3 0.4 fusion.8
  51.7 1.0 select_reduce_fusion
  53.3 0.4 fusion.7
  53.7 0.4 fusion.21
  54.1 0.4 fusion.6
  54.9 0.4 fusion.5
  55.7 0.4 fusion.4
  56.1 0.4 fusion.53
  56.5 0.4 fusion.3
  56.8 0.6 fusion.54
  57.5 0.4 fusion.2
  57.9 0.4 fusion.55
  58.2 0.4 fusion.16
  58.6 0.4 fusion
  59.1 1.0 fusion.23
  60.3 0.8 copy-done.2
  61.1 10.1 %collective-permute-start.10 = (f32[1,8,128,256]{3,2,1,0:T(8,128)S(1)}, f32[1,8,128,256]{3,2,1,0:T(8,128)S(1)}, u32[]{:S(2)}, u32[]{:S(2)}) collective-permute-start(f32[1,8,128,256]{3,2,1,0:T(8,128)S(1)} %fusion.19), channel_id=1, source_target_pairs={{0,2},{2,4},{4,6},{6,8},{8,10},{10,12},{12,14},{14,16},{16,18},{18... | collective-permute-start | bytes 3145736 | tf_op jit(solution)/shard_map/ppermute | solution.py:23
  71.2 1.9 %collective-permute-start.11 = (f32[1,8,128,256]{3,2,1,0:T(8,128)S(1)}, f32[1,8,128,256]{3,2,1,0:T(8,128)S(1)}, u32[]{:S(2)}, u32[]{:S(2)}) collective-permute-start(f32[1,8,128,256]{3,2,1,0:T(8,128)S(1)} %fusion.19), channel_id=1, source_target_pairs={{2,0},{4,2},{6,4},{8,6},{10,8},{12,10},{14,12},{16,14},{18,16},{20... | collective-permute-start | bytes 3145736 | tf_op jit(solution)/shard_map/ppermute | solution.py:23
  73.1 18.9 %collective-permute-done.10 = f32[1,8,128,256]{3,2,1,0:T(8,128)S(1)} collective-permute-done((f32[1,8,128,256]{3,2,1,0:T(8,128)S(1)}, f32[1,8,128,256]{3,2,1,0:T(8,128)S(1)}, u32[]{:S(2)}, u32[]{:S(2)}) %collective-permute-start.10) | collective-permute-done | bytes 1048608 | tf_op jit(solution)/shard_map/ppermute | solution.py:23
  92.0 8.1 %collective-permute-done.11 = f32[1,8,128,256]{3,2,1,0:T(8,128)S(1)} collective-permute-done((f32[1,8,128,256]{3,2,1,0:T(8,128)S(1)}, f32[1,8,128,256]{3,2,1,0:T(8,128)S(1)}, u32[]{:S(2)}, u32[]{:S(2)}) %collective-permute-start.11) | collective-permute-done | bytes 1048608 | tf_op jit(solution)/shard_map/ppermute | solution.py:23
  100.1 1.3 %collective-permute-start.12 = (f32[1,24,8,256]{3,2,1,0:T(8,128)S(1)}, f32[1,24,8,256]{3,2,1,0:T(8,128)S(1)}, u32[]{:S(2)}, u32[]{:S(2)}) collective-permute-start(f32[1,24,8,256]{3,2,1,0:T(8,128)S(1)} %get-tuple-element.7), channel_id=1, source_target_pairs={{0,1},{2,3},{4,5},{6,7},{8,9},{10,11},{12,13},{14,15},{16,17},{18,... | collective-permute-start | bytes 589832 | tf_op jit(solution)/shard_map/ppermute | solution.py:23
  101.4 4.8 %collective-permute-start.13 = (f32[1,24,8,256]{3,2,1,0:T(8,128)S(1)}, f32[1,24,8,256]{3,2,1,0:T(8,128)S(1)}, u32[]{:S(2)}, u32[]{:S(2)}) collective-permute-start(f32[1,24,8,256]{3,2,1,0:T(8,128)S(1)} %get-tuple-element.8), channel_id=1, source_target_pairs={{1,0},{3,2},{5,4},{7,6},{9,8},{11,10},{13,12},{15,14},{17,16},{19,... | collective-permute-start | bytes 589832 | tf_op jit(solution)/shard_map/ppermute | solution.py:23
  106.2 1.0 collective-permute-done.13
  107.2 2.1 %maximum_bitcast_fusion.target_ref = f32[24,144,256]{2,1,0:T(8,128)} fusion(f32[1,24,8,256]{3,2,1,0:T(8,128)S(1)} %collective-permute-done.13, f32[1,8,128,256]{3,2,1,0:T(8,128)S(1)} %collective-permute-done.11, f32[1,8,128,256]{3,2,1,0:T(8,128)S(1)} %fusion.19, f32[1,8,128,256]{3,2,1,0:T(8,128)S(1)} %collective-permute-done.10, ...), kind=kLoop, calls=%fused_computation | loop fusion | flops 3538944 | bytes 7077888 | tf_op jit(solution)/shard_map/squeeze | solution.py:151
  109.3 0.7 broadcast_in_dim.37.ky_ref
  110.0 0.7 broadcast_in_dim.34.kx_ref
  110.7 16.1 %shard_map.58 = (f32[8,128,256]{2,1,0:T(8,128)}, f32[8,128,256]{2,1,0:T(8,128)}) custom-call(f32[24,144,256]{2,1,0:T(8,128)} %maximum_bitcast_fusion.target_ref, f32[24,1,128]{2,1,0:T(1,128)} %broadcast_in_dim.34.kx_ref, f32[144,128]{1,0:T(8,128)} %broadcast_in_dim.37.ky_ref), custom_call_target="tpu_custom_call" | custom-call | tf_op jit(solution)/shard_map/pallas_call | solution.py:124
  (30 shorter events, 2.7 us)
Async XLA Ops:
  5.2 1.8 %collective-permute-start = (f32[128,384]{0,1:T(8,128)S(1)}, f32[128,384]{0,1:T(8,128)S(1)}, u32[]{:S(2)}, u32[]{:S(2)}) collective-permute-start(f32[128,384]{0,1:T(8,128)S(1)} %pad_maximum_fusion.3), channel_id=1, source_target_pairs={{0,1},{1,0},{2,3},{3,2},{4,5},{5,4},{6,7},{7,6},{8,9},{9,8},{10,11... | collective-permute-start | bytes 589832 | tf_op jit(solution)/shard_map/ppermute | solution.py:72
  7.0 6.2 %collective-permute-start.1 = (f32[128,384]{0,1:T(8,128)S(1)}, f32[128,384]{0,1:T(8,128)S(1)}, u32[]{:S(2)}, u32[]{:S(2)}) collective-permute-start(f32[128,384]{0,1:T(8,128)S(1)} %fusion.37), channel_id=1, source_target_pairs={{0,2},{2,0},{4,6},{6,4},{8,10},{10,8},{12,14},{14,12},{16,18},{18,... | collective-permute-start | bytes 589832 | tf_op jit(solution)/shard_map/ppermute | solution.py:69
  7.6 9.7 %collective-permute-start.2 = (f32[128,384]{0,1:T(8,128)S(1)}, f32[128,384]{0,1:T(8,128)S(1)}, u32[]{:S(2)}, u32[]{:S(2)}) collective-permute-start(f32[128,384]{0,1:T(8,128)S(1)} %fusion.37), channel_id=1, source_target_pairs={{0,4},{2,6},{4,0},{6,2},{8,12},{10,14},{12,8},{14,10},{16,20},{18,... | collective-permute-start | bytes 589832 | tf_op jit(solution)/shard_map/ppermute | solution.py:69
  8.5 11.3 %collective-permute-start.3 = (f32[128,384]{0,1:T(8,128)S(1)}, f32[128,384]{0,1:T(8,128)S(1)}, u32[]{:S(2)}, u32[]{:S(2)}) collective-permute-start(f32[128,384]{0,1:T(8,128)S(1)} %fusion.37), channel_id=1, source_target_pairs={{0,6},{2,4},{4,2},{6,0},{8,14},{10,12},{12,10},{14,8},{16,22},{18,... | collective-permute-start | bytes 589832 | tf_op jit(solution)/shard_map/ppermute | solution.py:69
  19.8 5.1 %collective-permute-start.4 = (f32[128,384]{0,1:T(8,128)S(1)}, f32[128,384]{0,1:T(8,128)S(1)}, u32[]{:S(2)}, u32[]{:S(2)}) collective-permute-start(f32[128,384]{0,1:T(8,128)S(1)} %add_add_fusion.2), channel_id=1, source_target_pairs={{0,8},{2,10},{4,12},{6,14},{8,0},{10,2},{12,4},{14,6},{16,24},{18,... | collective-permute-start | bytes 589832 | tf_op jit(solution)/shard_map/ppermute | solution.py:69
  20.0 8.5 %collective-permute-start.5 = (f32[128,384]{0,1:T(8,128)S(1)}, f32[128,384]{0,1:T(8,128)S(1)}, u32[]{:S(2)}, u32[]{:S(2)}) collective-permute-start(f32[128,384]{0,1:T(8,128)S(1)} %add_add_fusion.2), channel_id=1, source_target_pairs={{0,16},{2,18},{4,20},{6,22},{8,24},{10,26},{12,28},{14,30},{16,0},... | collective-permute-start | bytes 589832 | tf_op jit(solution)/shard_map/ppermute | solution.py:69
  20.3 11.7 %collective-permute-start.6 = (f32[128,384]{0,1:T(8,128)S(1)}, f32[128,384]{0,1:T(8,128)S(1)}, u32[]{:S(2)}, u32[]{:S(2)}) collective-permute-start(f32[128,384]{0,1:T(8,128)S(1)} %add_add_fusion.2), channel_id=1, source_target_pairs={{0,24},{2,26},{4,28},{6,30},{8,16},{10,18},{12,20},{14,22},{16,8},... | collective-permute-start | bytes 589832 | tf_op jit(solution)/shard_map/ppermute | solution.py:69
  32.0 5.0 %collective-permute-start.7 = (f32[128,384]{0,1:T(8,128)S(1)}, f32[128,384]{0,1:T(8,128)S(1)}, u32[]{:S(2)}, u32[]{:S(2)}) collective-permute-start(f32[128,384]{0,1:T(8,128)S(1)} %add_add_fusion.1), channel_id=1, source_target_pairs={{0,32},{2,34},{4,36},{6,38},{8,40},{10,42},{12,44},{14,46},{16,48}... | collective-permute-start | bytes 589832 | tf_op jit(solution)/shard_map/ppermute | solution.py:69
  33.0 8.5 %collective-permute-start.8 = (f32[128,384]{0,1:T(8,128)S(1)}, f32[128,384]{0,1:T(8,128)S(1)}, u32[]{:S(2)}, u32[]{:S(2)}) collective-permute-start(f32[128,384]{0,1:T(8,128)S(1)} %add_add_fusion.1), channel_id=1, source_target_pairs={{0,64},{2,66},{4,68},{6,70},{8,72},{10,74},{12,76},{14,78},{16,80}... | collective-permute-start | bytes 589832 | tf_op jit(solution)/shard_map/ppermute | solution.py:69
  33.4 8.1 %collective-permute-start.9 = (f32[128,384]{0,1:T(8,128)S(1)}, f32[128,384]{0,1:T(8,128)S(1)}, u32[]{:S(2)}, u32[]{:S(2)}) collective-permute-start(f32[128,384]{0,1:T(8,128)S(1)} %add_add_fusion.1), channel_id=1, source_target_pairs={{0,96},{2,98},{4,100},{6,102},{8,104},{10,106},{12,108},{14,110},{... | collective-permute-start | bytes 589832 | tf_op jit(solution)/shard_map/ppermute | solution.py:69
  55.3 3.8 %copy-start = (f32[8,128,256]{2,1,0:T(8,128)S(1)}, f32[8,128,256]{2,1,0:T(8,128)}, u32[]{:S(2)}) copy-start(f32[8,128,256]{2,1,0:T(8,128)} %param.5) | copy-start | bytes 3145732
  55.3 3.8 %copy-start.1 = (bf16[8,128,256]{2,1,0:T(8,128)(2,1)S(1)}, bf16[8,128,256]{2,1,0:T(8,128)(2,1)}, u32[]{:S(2)}) copy-start(bf16[8,128,256]{2,1,0:T(8,128)(2,1)} %param.3) | copy-start | bytes 1572868
  55.3 3.8 %copy-start.3 = (f32[8,128,256]{2,1,0:T(8,128)S(1)}, f32[8,128,256]{2,1,0:T(8,128)}, u32[]{:S(2)}) copy-start(f32[8,128,256]{2,1,0:T(8,128)} %param.4) | copy-start | bytes 3145732
  60.1 1.0 copy-start.2
  61.1 30.9 %collective-permute-start.10 = (f32[1,8,128,256]{3,2,1,0:T(8,128)S(1)}, f32[1,8,128,256]{3,2,1,0:T(8,128)S(1)}, u32[]{:S(2)}, u32[]{:S(2)}) collective-permute-start(f32[1,8,128,256]{3,2,1,0:T(8,128)S(1)} %fusion.19), channel_id=1, source_target_pairs={{0,2},{2,4},{4,6},{6,8},{8,10},{10,12},{12,14},{14,16},{16,18},{18... | collective-permute-start | bytes 3145736 | tf_op jit(solution)/shard_map/ppermute | solution.py:23
  71.2 28.9 %collective-permute-start.11 = (f32[1,8,128,256]{3,2,1,0:T(8,128)S(1)}, f32[1,8,128,256]{3,2,1,0:T(8,128)S(1)}, u32[]{:S(2)}, u32[]{:S(2)}) collective-permute-start(f32[1,8,128,256]{3,2,1,0:T(8,128)S(1)} %fusion.19), channel_id=1, source_target_pairs={{2,0},{4,2},{6,4},{8,6},{10,8},{12,10},{14,12},{16,14},{18,16},{20... | collective-permute-start | bytes 3145736 | tf_op jit(solution)/shard_map/ppermute | solution.py:23
  100.1 6.1 %collective-permute-start.12 = (f32[1,24,8,256]{3,2,1,0:T(8,128)S(1)}, f32[1,24,8,256]{3,2,1,0:T(8,128)S(1)}, u32[]{:S(2)}, u32[]{:S(2)}) collective-permute-start(f32[1,24,8,256]{3,2,1,0:T(8,128)S(1)} %get-tuple-element.7), channel_id=1, source_target_pairs={{0,1},{2,3},{4,5},{6,7},{8,9},{10,11},{12,13},{14,15},{16,17},{18,... | collective-permute-start | bytes 589832 | tf_op jit(solution)/shard_map/ppermute | solution.py:23
  101.4 5.8 %collective-permute-start.13 = (f32[1,24,8,256]{3,2,1,0:T(8,128)S(1)}, f32[1,24,8,256]{3,2,1,0:T(8,128)S(1)}, u32[]{:S(2)}, u32[]{:S(2)}) collective-permute-start(f32[1,24,8,256]{3,2,1,0:T(8,128)S(1)} %get-tuple-element.8), channel_id=1, source_target_pairs={{1,0},{3,2},{5,4},{7,6},{9,8},{11,10},{13,12},{15,14},{17,16},{19,... | collective-permute-start | bytes 589832 | tf_op jit(solution)/shard_map/ppermute | solution.py:23

commit v7 on v6

--- a/solution.py
+++ b/solution.py
@@ -4,6 +4,7 @@
 from jax.sharding import PartitionSpec as P
 from jax.experimental import pallas as pl
 from jax.experimental.pallas import tpu as pltpu
+
 
 K_ROOT = 8
 K_SIGN = 6
@@ -116,25 +117,37 @@
     dual_ref[...] = middle[:, HALO : HALO + width] - fg
 
 
-def tv_local(target, kx, ky):
-    rows, cols, frames = target.shape
+def tv_local(target, kx, ky, chunk, frames, into=None):
+    rows, cols, lanes = target.shape
     inner_rows, inner_cols = rows - 2 * HALO, cols - 2 * HALO
-    lanes = 128 if frames % 128 == 0 else frames
     out = jax.ShapeDtypeStruct((inner_rows, inner_cols, frames), jnp.float32)
+    in_specs = [
+        pl.BlockSpec((rows, cols, lanes), lambda f: (0, 0, 0)),
+        pl.BlockSpec((rows, 1, lanes), lambda f: (0, 0, 0)),
+        pl.BlockSpec((cols, lanes), lambda f: (0, 0)),
+    ]
+    operands = [target, kx, ky]
+    aliases = {}
+    body = tv_kernel
+    if into is not None:
+        in_specs += [pl.BlockSpec(memory_space=pl.ANY), pl.BlockSpec(memory_space=pl.ANY)]
+        operands += list(into)
+        aliases = {3: 0, 4: 1}
+
+        def body(target_ref, kx_ref, ky_ref, fg_in, dual_in, fg_ref, dual_ref):
+            tv_kernel(target_ref, kx_ref, ky_ref, fg_ref, dual_ref)
+
     return pl.pallas_call(
-        tv_kernel,
-        grid=(frames // lanes,),
-        in_specs=[
-            pl.BlockSpec((rows, cols, lanes), lambda f: (0, 0, f)),
-            pl.BlockSpec((rows, 1, lanes), lambda f: (0, 0, 0)),
-            pl.BlockSpec((cols, lanes), lambda f: (0, 0)),
-        ],
+        body,
+        grid=(1,),
+        in_specs=in_specs,
         out_specs=[
-            pl.BlockSpec((inner_rows, inner_cols, lanes), lambda f: (0, 0, f)),
-            pl.BlockSpec((inner_rows, inner_cols, lanes), lambda f: (0, 0, f)),
+            pl.BlockSpec((inner_rows, inner_cols, lanes), lambda f: (0, 0, chunk)),
+            pl.BlockSpec((inner_rows, inner_cols, lanes), lambda f: (0, 0, chunk)),
         ],
         out_shape=[out, out],
-    )(target, kx, ky)
+        input_output_aliases=aliases,
+    )(*operands)
 
 
 def per_device(video, foreground, scaled_dual):
@@ -148,7 +161,6 @@
     shrink = shrink_matrix(gram)
     background = matmul(flat, shrink).reshape(foreground.shape)
     target = observed - background + scaled_dual
-    target = with_halo(target[None])[0]
     ext_rows, ext_cols = rows_here + 2 * HALO, cols_here + 2 * HALO
 
     first_row = lax.axis_index("rows") * rows_here - HALO
@@ -160,7 +172,11 @@
     lanes = 128 if frames % 128 == 0 else frames
     kx = jnp.broadcast_to(jnp.where(keep_x, 1.0, 0.0).astype(jnp.float32), (ext_rows, 1, lanes))
     ky = jnp.broadcast_to(jnp.where(keep_y, 1.0, 0.0).astype(jnp.float32)[0], (ext_cols, lanes))
-    new_foreground, new_dual = tv_local(target, kx, ky)
+    outs = None
+    for chunk in range(frames // lanes):
+        piece = with_halo(target[None, :, :, chunk * lanes : (chunk + 1) * lanes])[0]
+        outs = tv_local(piece, kx, ky, chunk, frames, outs)
+    new_foreground, new_dual = outs
     return (background, new_foreground, new_dual)
 
 

time: 127 us -> 128 us (level)
  the two profiles are of different devices: /device:TPU:119 before, /device:TPU:8 now
where the time goes in v7:
time: 128 us; the launch traced here: 126 us
  waiting for transfers between devices  39.5 us (31%)
  starting transfers between devices  38.6 us (30%)
  matrix products  21.5 us (17%)
  Pallas kernels  18.4 us (14%)
  other arithmetic  3.59 us (3%)
  between operations  2.53 us (2%)
  local copies, waits for them, and re-layouts  1.71 us (1%)
    ppermute x8, starting transfers between devices, shifted(): return lax.ppermute(x, axis, pairs)  25.1 us
    ppermute x9, waiting for transfers between devices, all_sum(): lax.ppermute(x, axis, [(i, i ^ k * step) for i in range(length)])  24 us
    dot_general x39, matrix products, matmul(): jnp.dot(left, right, precision=lax.Precision.HIGHEST, preferred_element_t...  21.5 us
    pallas_call x2, Pallas kernels, tv_local(): pl.pallas_call(body, grid=(1,), in_specs=in_specs, out_specs=[pl.BlockSpe...  18.4 us
    ppermute x8, waiting for transfers between devices, shifted(): return lax.ppermute(x, axis, pairs)  14.1 us
    ppermute x9, starting transfers between devices, all_sum(): lax.ppermute(x, axis, [(i, i ^ k * step) for i in range(length)])  13.4 us
    squeeze x2, other arithmetic, per_device(): piece = with_halo(target[None, :, :, chunk * lanes:(chunk + 1) * lanes])[0]  2.73 us
  transfers between devices with their start and end apart: 18, of which 10 were waited for; matrix products, arithmetic and copies ran while one was open for 2% of the time, Pallas kernels for 7%

profile of v7, /device:TPU:8, one launch (start us, length us, event | category | flops | bytes accessed | tf_op | source)
XLA Modules:
  0.0 125.9 jit_solution(12980859200695923985)
XLA Ops:
  0.6 4.5 %convolution_bitcast_fusion = f32[256,256]{0,1:T(8,128)S(1)} fusion(f32[8,128,256]{2,1,0:T(8,128)} %param.5, f32[8,128,256]{2,1,0:T(8,128)} %param.4, bf16[8,128,256]{2,1,0:T(8,128)(2,1)} %param.3), kind=kOutput, calls=%fused_computation.37 | convolution fusion | flops 806092800 | bytes 2883584 | tf_op jit(solution)/shard_map/dot_general | solution.py:28
  5.2 1.4 %collective-permute-done = f32[128,384]{0,1:T(8,128)S(1)} collective-permute-done((f32[128,384]{0,1:T(8,128)S(1)}, f32[128,384]{0,1:T(8,128)S(1)}, u32[]{:S(2)}, u32[]{:S(2)}) %collective-permute-start) | collective-permute-done | bytes 196640 | tf_op jit(solution)/shard_map/ppermute | solution.py:73
  6.7 2.8 %collective-permute-start.3 = (f32[128,384]{0,1:T(8,128)S(1)}, f32[128,384]{0,1:T(8,128)S(1)}, u32[]{:S(2)}, u32[]{:S(2)}) collective-permute-start(f32[128,384]{0,1:T(8,128)S(1)} %fusion.36), channel_id=1, source_target_pairs={{0,6},{2,4},{4,2},{6,0},{8,14},{10,12},{12,10},{14,8},{16,22},{18,... | collective-permute-start | bytes 589832 | tf_op jit(solution)/shard_map/ppermute | solution.py:70
  9.5 0.8 collective-permute-start.2
  10.3 0.5 collective-permute-start.1
  10.9 8.3 %collective-permute-done.3 = f32[128,384]{0,1:T(8,128)S(1)} collective-permute-done((f32[128,384]{0,1:T(8,128)S(1)}, f32[128,384]{0,1:T(8,128)S(1)}, u32[]{:S(2)}, u32[]{:S(2)}) %collective-permute-start.3) | collective-permute-done | bytes 196640 | tf_op jit(solution)/shard_map/ppermute | solution.py:70
  19.2 0.6 collective-permute-done.1
  19.8 4.1 %collective-permute-start.6 = (f32[128,384]{0,1:T(8,128)S(1)}, f32[128,384]{0,1:T(8,128)S(1)}, u32[]{:S(2)}, u32[]{:S(2)}) collective-permute-start(f32[128,384]{0,1:T(8,128)S(1)} %add_add_fusion.2), channel_id=1, source_target_pairs={{0,24},{2,26},{4,28},{6,30},{8,16},{10,18},{12,20},{14,22},{16,8},... | collective-permute-start | bytes 589832 | tf_op jit(solution)/shard_map/ppermute | solution.py:70
  23.9 0.9 collective-permute-start.4
  24.9 6.6 %collective-permute-done.6 = f32[128,384]{0,1:T(8,128)S(1)} collective-permute-done((f32[128,384]{0,1:T(8,128)S(1)}, f32[128,384]{0,1:T(8,128)S(1)}, u32[]{:S(2)}, u32[]{:S(2)}) %collective-permute-start.6) | collective-permute-done | bytes 196640 | tf_op jit(solution)/shard_map/ppermute | solution.py:70
  31.5 1.6 %collective-permute-done.5 = f32[128,384]{0,1:T(8,128)S(1)} collective-permute-done((f32[128,384]{0,1:T(8,128)S(1)}, f32[128,384]{0,1:T(8,128)S(1)}, u32[]{:S(2)}, u32[]{:S(2)}) %collective-permute-start.5) | collective-permute-done | bytes 196640 | tf_op jit(solution)/shard_map/ppermute | solution.py:70
  33.2 1.7 %collective-permute-start.9 = (f32[128,384]{0,1:T(8,128)S(1)}, f32[128,384]{0,1:T(8,128)S(1)}, u32[]{:S(2)}, u32[]{:S(2)}) collective-permute-start(f32[128,384]{0,1:T(8,128)S(1)} %add_add_fusion.1), channel_id=1, source_target_pairs={{0,96},{2,98},{4,100},{6,102},{8,104},{10,106},{12,108},{14,110},{... | collective-permute-start | bytes 589832 | tf_op jit(solution)/shard_map/ppermute | solution.py:70
  34.9 0.9 collective-permute-start.8
  35.8 1.6 %collective-permute-start.7 = (f32[128,384]{0,1:T(8,128)S(1)}, f32[128,384]{0,1:T(8,128)S(1)}, u32[]{:S(2)}, u32[]{:S(2)}) collective-permute-start(f32[128,384]{0,1:T(8,128)S(1)} %add_add_fusion.1), channel_id=1, source_target_pairs={{0,32},{2,34},{4,36},{6,38},{8,40},{10,42},{12,44},{14,46},{16,48}... | collective-permute-start | bytes 589832 | tf_op jit(solution)/shard_map/ppermute | solution.py:70
  37.4 4.5 %collective-permute-done.9 = f32[128,384]{0,1:T(8,128)S(1)} collective-permute-done((f32[128,384]{0,1:T(8,128)S(1)}, f32[128,384]{0,1:T(8,128)S(1)}, u32[]{:S(2)}, u32[]{:S(2)}) %collective-permute-start.9) | collective-permute-done | bytes 196640 | tf_op jit(solution)/shard_map/ppermute | solution.py:70
  41.9 1.2 collective-permute-done.8
  43.1 1.1 collective-permute-done.7
  44.4 0.7 multiply_reduce_fusion
  46.1 0.6 fusion.29
  47.0 0.4 fusion.14
  47.4 0.4 fusion.39
  47.8 0.4 fusion.38
  48.2 0.4 fusion.13
  48.6 0.4 fusion.41
  48.9 0.4 fusion.40
  49.3 0.4 fusion.12
  49.7 0.4 fusion.43
  50.5 0.4 fusion.11
  51.3 0.4 fusion.44
  51.6 0.4 fusion.10
  52.0 0.4 fusion.47
  52.4 0.4 fusion.46
  52.8 0.4 fusion.9
  53.6 0.4 fusion.48
  54.0 0.4 fusion.8
  54.4 1.0 select_reduce_fusion
  56.0 0.4 fusion.7
  56.4 0.4 fusion.20
  56.8 0.4 fusion.6
  57.6 0.4 fusion.5
  58.0 0.4 fusion.51
  58.4 0.4 fusion.4
  59.1 0.4 fusion.3
  59.5 0.6 fusion.53
  60.2 0.4 fusion.2
  60.9 0.4 fusion.16
  61.3 0.4 fusion
  61.8 2.0 %fusion.18 = (f32[8,128,256]{2,1,0:T(8,128)S(1)}, f32[8,128,256]{2,1,0:T(8,128)}) fusion(f32[8,128,256]{2,1,0:T(8,128)S(1)} %copy-done, bf16[8,128,256]{2,1,0:T(8,128)(2,1)S(1)} %copy-done.2, f32[256,256,1]{1,0,2:T(8,128)S(1)} %fusion, f32[8,128,256]{2,1,0:T(8,128)S(1)} %copy-done.1), kind=kOutput, calls=%fused_computation.39 | convolution fusion | flops 806879232 | bytes 4980736 | tf_op jit(solution)/shard_map/dot_general | solution.py:28
  63.9 7.9 %collective-permute-start.15 = (f32[1,8,128,128]{3,2,1,0:T(8,128)S(1)}, f32[1,8,128,128]{3,2,1,0:T(8,128)S(1)}, u32[]{:S(2)}, u32[]{:S(2)}) collective-permute-start(f32[1,8,128,128]{3,2,1,0:T(8,128)S(1)} %get-tuple-element.15), channel_id=1, source_target_pairs={{2,0},{4,2},{6,4},{8,6},{10,8},{12,10},{14,12},{16,14},{18,16},{20... | collective-permute-start | bytes 1572872 | tf_op jit(solution)/shard_map/ppermute | solution.py:24
  71.9 1.9 %collective-permute-start.14 = (f32[1,8,128,128]{3,2,1,0:T(8,128)S(1)}, f32[1,8,128,128]{3,2,1,0:T(8,128)S(1)}, u32[]{:S(2)}, u32[]{:S(2)}) collective-permute-start(f32[1,8,128,128]{3,2,1,0:T(8,128)S(1)} %get-tuple-element.15), channel_id=1, source_target_pairs={{0,2},{2,4},{4,6},{6,8},{8,10},{10,12},{12,14},{14,16},{16,18},{18... | collective-permute-start | bytes 1572872 | tf_op jit(solution)/shard_map/ppermute | solution.py:24
  73.8 8.1 %collective-permute-start.11 = (f32[1,8,128,128]{3,2,1,0:T(8,128)S(1)}, f32[1,8,128,128]{3,2,1,0:T(8,128)S(1)}, u32[]{:S(2)}, u32[]{:S(2)}) collective-permute-start(f32[1,8,128,128]{3,2,1,0:T(8,128)S(1)} %get-tuple-element.16), channel_id=1, source_target_pairs={{2,0},{4,2},{6,4},{8,6},{10,8},{12,10},{14,12},{16,14},{18,16},{20... | collective-permute-start | bytes 1572872 | tf_op jit(solution)/shard_map/ppermute | solution.py:24
  82.0 1.9 %collective-permute-start.10 = (f32[1,8,128,128]{3,2,1,0:T(8,128)S(1)}, f32[1,8,128,128]{3,2,1,0:T(8,128)S(1)}, u32[]{:S(2)}, u32[]{:S(2)}) collective-permute-start(f32[1,8,128,128]{3,2,1,0:T(8,128)S(1)} %get-tuple-element.16), channel_id=1, source_target_pairs={{0,2},{2,4},{4,6},{6,8},{8,10},{10,12},{12,14},{14,16},{16,18},{18... | collective-permute-start | bytes 1572872 | tf_op jit(solution)/shard_map/ppermute | solution.py:24
  83.9 7.2 %collective-permute-done.14 = f32[1,8,128,128]{3,2,1,0:T(8,128)S(1)} collective-permute-done((f32[1,8,128,128]{3,2,1,0:T(8,128)S(1)}, f32[1,8,128,128]{3,2,1,0:T(8,128)S(1)}, u32[]{:S(2)}, u32[]{:S(2)}) %collective-permute-start.14) | collective-permute-done | bytes 524320 | tf_op jit(solution)/shard_map/ppermute | solution.py:24
  91.2 1.3 %collective-permute-start.16 = (f32[1,24,8,128]{3,2,1,0:T(8,128)S(1)}, f32[1,24,8,128]{3,2,1,0:T(8,128)S(1)}, u32[]{:S(2)}, u32[]{:S(2)}) collective-permute-start(f32[1,24,8,128]{3,2,1,0:T(8,128)S(1)} %get-tuple-element.11), channel_id=1, source_target_pairs={{0,1},{2,3},{4,5},{6,7},{8,9},{10,11},{12,13},{14,15},{16,17},{18,... | collective-permute-start | bytes 294920 | tf_op jit(solution)/shard_map/ppermute | solution.py:24
  92.5 1.3 %collective-permute-start.17 = (f32[1,24,8,128]{3,2,1,0:T(8,128)S(1)}, f32[1,24,8,128]{3,2,1,0:T(8,128)S(1)}, u32[]{:S(2)}, u32[]{:S(2)}) collective-permute-start(f32[1,24,8,128]{3,2,1,0:T(8,128)S(1)} %get-tuple-element.12), channel_id=1, source_target_pairs={{1,0},{3,2},{5,4},{7,6},{9,8},{11,10},{13,12},{15,14},{17,16},{19,... | collective-permute-start | bytes 294920 | tf_op jit(solution)/shard_map/ppermute | solution.py:24
  93.8 6.9 %collective-permute-done.10 = f32[1,8,128,128]{3,2,1,0:T(8,128)S(1)} collective-permute-done((f32[1,8,128,128]{3,2,1,0:T(8,128)S(1)}, f32[1,8,128,128]{3,2,1,0:T(8,128)S(1)}, u32[]{:S(2)}, u32[]{:S(2)}) %collective-permute-start.10) | collective-permute-done | bytes 524320 | tf_op jit(solution)/shard_map/ppermute | solution.py:24
  100.7 1.3 %collective-permute-start.12 = (f32[1,24,8,128]{3,2,1,0:T(8,128)S(1)}, f32[1,24,8,128]{3,2,1,0:T(8,128)S(1)}, u32[]{:S(2)}, u32[]{:S(2)}) collective-permute-start(f32[1,24,8,128]{3,2,1,0:T(8,128)S(1)} %get-tuple-element.13), channel_id=1, source_target_pairs={{0,1},{2,3},{4,5},{6,7},{8,9},{10,11},{12,13},{14,15},{16,17},{18,... | collective-permute-start | bytes 294920 | tf_op jit(solution)/shard_map/ppermute | solution.py:24
  102.0 1.3 %collective-permute-start.13 = (f32[1,24,8,128]{3,2,1,0:T(8,128)S(1)}, f32[1,24,8,128]{3,2,1,0:T(8,128)S(1)}, u32[]{:S(2)}, u32[]{:S(2)}) collective-permute-start(f32[1,24,8,128]{3,2,1,0:T(8,128)S(1)} %get-tuple-element.14), channel_id=1, source_target_pairs={{1,0},{3,2},{5,4},{7,6},{9,8},{11,10},{13,12},{15,14},{17,16},{19,... | collective-permute-start | bytes 294920 | tf_op jit(solution)/shard_map/ppermute | solution.py:24
  103.3 1.4 %maximum_bitcast_fusion.1.target_ref = f32[24,144,128]{2,1,0:T(8,128)} fusion(f32[1,24,8,128]{3,2,1,0:T(8,128)S(1)} %collective-permute-done.17, f32[1,8,128,128]{3,2,1,0:T(8,128)S(1)} %collective-permute-done.15, f32[1,8,128,128]{3,2,1,0:T(8,128)S(1)} %get-tuple-element.15, f32[1,8,128,128]{3,2,1,0:T(8,128)S(1)} %collective-permute-done.14, ...), kind=kLoop, calls=%fused_computation.1 | loop fusion | flops 1769472 | bytes 3538944 | tf_op jit(solution)/shard_map/squeeze | solution.py:177
  104.7 0.7 broadcast_in_dim.37.kx_ref
  105.4 0.7 broadcast_in_dim.40.ky_ref
  106.1 9.2 %shard_map.58 = (f32[8,128,256]{2,1,0:T(8,128)}, f32[8,128,256]{2,1,0:T(8,128)}) custom-call(f32[24,144,128]{2,1,0:T(8,128)} %maximum_bitcast_fusion.1.target_ref, f32[24,1,128]{2,1,0:T(1,128)} %broadcast_in_dim.37.kx_ref, f32[144,128]{1,0:T(8,128)} %broadcast_in_dim.40.ky_ref), custom_call_target="tpu_custom_call" | custom-call | tf_op jit(solution)/shard_map/pallas_call | solution.py:140
  115.3 1.4 %maximum_bitcast_fusion.target_ref = f32[24,144,128]{2,1,0:T(8,128)} fusion(f32[1,24,8,128]{3,2,1,0:T(8,128)S(1)} %collective-permute-done.13, f32[1,8,128,128]{3,2,1,0:T(8,128)S(1)} %collective-permute-done.11, f32[1,8,128,128]{3,2,1,0:T(8,128)S(1)} %get-tuple-element.16, f32[1,8,128,128]{3,2,1,0:T(8,128)S(1)} %collective-permute-done.10, ...), kind=kLoop, calls=%fused_computation | loop fusion | flops 1769472 | bytes 3538944 | tf_op jit(solution)/shard_map/squeeze | solution.py:177
  116.6 9.2 %shard_map.59 = (f32[8,128,256]{2,1,0:T(8,128)}, f32[8,128,256]{2,1,0:T(8,128)}) custom-call(f32[24,144,128]{2,1,0:T(8,128)} %maximum_bitcast_fusion.target_ref, f32[24,1,128]{2,1,0:T(1,128)} %broadcast_in_dim.37.kx_ref, f32[144,128]{1,0:T(8,128)} %broadcast_in_dim.40.ky_ref, ...), custom_call_target="tpu_custom_call", output_to_operand_aliasing={{0}: (3, {}), {1}: (4, {})} | custom-call | tf_op jit(solution)/shard_map/pallas_call | solution.py:140
  (39 shorter events, 3.5 us)
Async XLA Ops:
  5.2 1.5 %collective-permute-start = (f32[128,384]{0,1:T(8,128)S(1)}, f32[128,384]{0,1:T(8,128)S(1)}, u32[]{:S(2)}, u32[]{:S(2)}) collective-permute-start(f32[128,384]{0,1:T(8,128)S(1)} %pad_maximum_fusion), channel_id=1, source_target_pairs={{0,1},{1,0},{2,3},{3,2},{4,5},{5,4},{6,7},{7,6},{8,9},{9,8},{10,11... | collective-permute-start | bytes 589832 | tf_op jit(solution)/shard_map/ppermute | solution.py:73
  6.7 12.4 %collective-permute-start.3 = (f32[128,384]{0,1:T(8,128)S(1)}, f32[128,384]{0,1:T(8,128)S(1)}, u32[]{:S(2)}, u32[]{:S(2)}) collective-permute-start(f32[128,384]{0,1:T(8,128)S(1)} %fusion.36), channel_id=1, source_target_pairs={{0,6},{2,4},{4,2},{6,0},{8,14},{10,12},{12,10},{14,8},{16,22},{18,... | collective-permute-start | bytes 589832 | tf_op jit(solution)/shard_map/ppermute | solution.py:70
  9.5 9.6 %collective-permute-start.2 = (f32[128,384]{0,1:T(8,128)S(1)}, f32[128,384]{0,1:T(8,128)S(1)}, u32[]{:S(2)}, u32[]{:S(2)}) collective-permute-start(f32[128,384]{0,1:T(8,128)S(1)} %fusion.36), channel_id=1, source_target_pairs={{0,4},{2,6},{4,0},{6,2},{8,12},{10,14},{12,8},{14,10},{16,20},{18,... | collective-permute-start | bytes 589832 | tf_op jit(solution)/shard_map/ppermute | solution.py:70
  10.3 9.4 %collective-permute-start.1 = (f32[128,384]{0,1:T(8,128)S(1)}, f32[128,384]{0,1:T(8,128)S(1)}, u32[]{:S(2)}, u32[]{:S(2)}) collective-permute-start(f32[128,384]{0,1:T(8,128)S(1)} %fusion.36), channel_id=1, source_target_pairs={{0,2},{2,0},{4,6},{6,4},{8,10},{10,8},{12,14},{14,12},{16,18},{18,... | collective-permute-start | bytes 589832 | tf_op jit(solution)/shard_map/ppermute | solution.py:70
  19.8 11.7 %collective-permute-start.6 = (f32[128,384]{0,1:T(8,128)S(1)}, f32[128,384]{0,1:T(8,128)S(1)}, u32[]{:S(2)}, u32[]{:S(2)}) collective-permute-start(f32[128,384]{0,1:T(8,128)S(1)} %add_add_fusion.2), channel_id=1, source_target_pairs={{0,24},{2,26},{4,28},{6,30},{8,16},{10,18},{12,20},{14,22},{16,8},... | collective-permute-start | bytes 589832 | tf_op jit(solution)/shard_map/ppermute | solution.py:70
  23.9 9.2 %collective-permute-start.5 = (f32[128,384]{0,1:T(8,128)S(1)}, f32[128,384]{0,1:T(8,128)S(1)}, u32[]{:S(2)}, u32[]{:S(2)}) collective-permute-start(f32[128,384]{0,1:T(8,128)S(1)} %add_add_fusion.2), channel_id=1, source_target_pairs={{0,16},{2,18},{4,20},{6,22},{8,24},{10,26},{12,28},{14,30},{16,0},... | collective-permute-start | bytes 589832 | tf_op jit(solution)/shard_map/ppermute | solution.py:70
  23.9 9.2 %collective-permute-start.4 = (f32[128,384]{0,1:T(8,128)S(1)}, f32[128,384]{0,1:T(8,128)S(1)}, u32[]{:S(2)}, u32[]{:S(2)}) collective-permute-start(f32[128,384]{0,1:T(8,128)S(1)} %add_add_fusion.2), channel_id=1, source_target_pairs={{0,8},{2,10},{4,12},{6,14},{8,0},{10,2},{12,4},{14,6},{16,24},{18,... | collective-permute-start | bytes 589832 | tf_op jit(solution)/shard_map/ppermute | solution.py:70
  33.2 8.7 %collective-permute-start.9 = (f32[128,384]{0,1:T(8,128)S(1)}, f32[128,384]{0,1:T(8,128)S(1)}, u32[]{:S(2)}, u32[]{:S(2)}) collective-permute-start(f32[128,384]{0,1:T(8,128)S(1)} %add_add_fusion.1), channel_id=1, source_target_pairs={{0,96},{2,98},{4,100},{6,102},{8,104},{10,106},{12,108},{14,110},{... | collective-permute-start | bytes 589832 | tf_op jit(solution)/shard_map/ppermute | solution.py:70
  34.9 8.2 %collective-permute-start.8 = (f32[128,384]{0,1:T(8,128)S(1)}, f32[128,384]{0,1:T(8,128)S(1)}, u32[]{:S(2)}, u32[]{:S(2)}) collective-permute-start(f32[128,384]{0,1:T(8,128)S(1)} %add_add_fusion.1), channel_id=1, source_target_pairs={{0,64},{2,66},{4,68},{6,70},{8,72},{10,74},{12,76},{14,78},{16,80}... | collective-permute-start | bytes 589832 | tf_op jit(solution)/shard_map/ppermute | solution.py:70
  35.8 8.4 %collective-permute-start.7 = (f32[128,384]{0,1:T(8,128)S(1)}, f32[128,384]{0,1:T(8,128)S(1)}, u32[]{:S(2)}, u32[]{:S(2)}) collective-permute-start(f32[128,384]{0,1:T(8,128)S(1)} %add_add_fusion.1), channel_id=1, source_target_pairs={{0,32},{2,34},{4,36},{6,38},{8,40},{10,42},{12,44},{14,46},{16,48}... | collective-permute-start | bytes 589832 | tf_op jit(solution)/shard_map/ppermute | solution.py:70
  60.1 1.6 %copy-start = (f32[8,128,256]{2,1,0:T(8,128)S(1)}, f32[8,128,256]{2,1,0:T(8,128)}, u32[]{:S(2)}) copy-start(f32[8,128,256]{2,1,0:T(8,128)} %param.5) | copy-start | bytes 3145732
  60.1 1.6 %copy-start.1 = (f32[8,128,256]{2,1,0:T(8,128)S(1)}, f32[8,128,256]{2,1,0:T(8,128)}, u32[]{:S(2)}) copy-start(f32[8,128,256]{2,1,0:T(8,128)} %param.4) | copy-start | bytes 3145732
  60.2 1.7 %copy-start.2 = (bf16[8,128,256]{2,1,0:T(8,128)(2,1)S(1)}, bf16[8,128,256]{2,1,0:T(8,128)(2,1)}, u32[]{:S(2)}) copy-start(bf16[8,128,256]{2,1,0:T(8,128)(2,1)} %param.3) | copy-start | bytes 1572868
  63.9 20.0 %collective-permute-start.15 = (f32[1,8,128,128]{3,2,1,0:T(8,128)S(1)}, f32[1,8,128,128]{3,2,1,0:T(8,128)S(1)}, u32[]{:S(2)}, u32[]{:S(2)}) collective-permute-start(f32[1,8,128,128]{3,2,1,0:T(8,128)S(1)} %get-tuple-element.15), channel_id=1, source_target_pairs={{2,0},{4,2},{6,4},{8,6},{10,8},{12,10},{14,12},{16,14},{18,16},{20... | collective-permute-start | bytes 1572872 | tf_op jit(solution)/shard_map/ppermute | solution.py:24
  71.9 19.3 %collective-permute-start.14 = (f32[1,8,128,128]{3,2,1,0:T(8,128)S(1)}, f32[1,8,128,128]{3,2,1,0:T(8,128)S(1)}, u32[]{:S(2)}, u32[]{:S(2)}) collective-permute-start(f32[1,8,128,128]{3,2,1,0:T(8,128)S(1)} %get-tuple-element.15), channel_id=1, source_target_pairs={{0,2},{2,4},{4,6},{6,8},{8,10},{10,12},{12,14},{14,16},{16,18},{18... | collective-permute-start | bytes 1572872 | tf_op jit(solution)/shard_map/ppermute | solution.py:24
  73.8 19.9 %collective-permute-start.11 = (f32[1,8,128,128]{3,2,1,0:T(8,128)S(1)}, f32[1,8,128,128]{3,2,1,0:T(8,128)S(1)}, u32[]{:S(2)}, u32[]{:S(2)}) collective-permute-start(f32[1,8,128,128]{3,2,1,0:T(8,128)S(1)} %get-tuple-element.16), channel_id=1, source_target_pairs={{2,0},{4,2},{6,4},{8,6},{10,8},{12,10},{14,12},{16,14},{18,16},{20... | collective-permute-start | bytes 1572872 | tf_op jit(solution)/shard_map/ppermute | solution.py:24
  82.0 18.7 %collective-permute-start.10 = (f32[1,8,128,128]{3,2,1,0:T(8,128)S(1)}, f32[1,8,128,128]{3,2,1,0:T(8,128)S(1)}, u32[]{:S(2)}, u32[]{:S(2)}) collective-permute-start(f32[1,8,128,128]{3,2,1,0:T(8,128)S(1)} %get-tuple-element.16), channel_id=1, source_target_pairs={{0,2},{2,4},{4,6},{6,8},{8,10},{10,12},{12,14},{14,16},{16,18},{18... | collective-permute-start | bytes 1572872 | tf_op jit(solution)/shard_map/ppermute | solution.py:24
  91.2 12.1 %collective-permute-start.16 = (f32[1,24,8,128]{3,2,1,0:T(8,128)S(1)}, f32[1,24,8,128]{3,2,1,0:T(8,128)S(1)}, u32[]{:S(2)}, u32[]{:S(2)}) collective-permute-start(f32[1,24,8,128]{3,2,1,0:T(8,128)S(1)} %get-tuple-element.11), channel_id=1, source_target_pairs={{0,1},{2,3},{4,5},{6,7},{8,9},{10,11},{12,13},{14,15},{16,17},{18,... | collective-permute-start | bytes 294920 | tf_op jit(solution)/shard_map/ppermute | solution.py:24
  92.5 10.8 %collective-permute-start.17 = (f32[1,24,8,128]{3,2,1,0:T(8,128)S(1)}, f32[1,24,8,128]{3,2,1,0:T(8,128)S(1)}, u32[]{:S(2)}, u32[]{:S(2)}) collective-permute-start(f32[1,24,8,128]{3,2,1,0:T(8,128)S(1)} %get-tuple-element.12), channel_id=1, source_target_pairs={{1,0},{3,2},{5,4},{7,6},{9,8},{11,10},{13,12},{15,14},{17,16},{19,... | collective-permute-start | bytes 294920 | tf_op jit(solution)/shard_map/ppermute | solution.py:24
  100.7 14.6 %collective-permute-start.12 = (f32[1,24,8,128]{3,2,1,0:T(8,128)S(1)}, f32[1,24,8,128]{3,2,1,0:T(8,128)S(1)}, u32[]{:S(2)}, u32[]{:S(2)}) collective-permute-start(f32[1,24,8,128]{3,2,1,0:T(8,128)S(1)} %get-tuple-element.13), channel_id=1, source_target_pairs={{0,1},{2,3},{4,5},{6,7},{8,9},{10,11},{12,13},{14,15},{16,17},{18,... | collective-permute-start | bytes 294920 | tf_op jit(solution)/shard_map/ppermute | solution.py:24
  102.0 13.3 %collective-permute-start.13 = (f32[1,24,8,128]{3,2,1,0:T(8,128)S(1)}, f32[1,24,8,128]{3,2,1,0:T(8,128)S(1)}, u32[]{:S(2)}, u32[]{:S(2)}) collective-permute-start(f32[1,24,8,128]{3,2,1,0:T(8,128)S(1)} %get-tuple-element.14), channel_id=1, source_target_pairs={{1,0},{3,2},{5,4},{7,6},{9,8},{11,10},{13,12},{15,14},{17,16},{19,... | collective-permute-start | bytes 294920 | tf_op jit(solution)/shard_map/ppermute | solution.py:24

commit v8 on v7

--- a/solution.py
+++ b/solution.py
@@ -45,13 +45,12 @@
     return 0.5 * matmul(identity - cutoff * inverse, identity + signed)
 
 
-def with_halo(pair):
-    up = shifted(pair[:, -HALO:], "rows", 1)
-    down = shifted(pair[:, :HALO], "rows", -1)
-    pair = jnp.concatenate([up, pair, down], axis=1)
-    left = shifted(pair[:, :, -HALO:], "cols", 1)
-    right = shifted(pair[:, :, :HALO], "cols", -1)
-    return jnp.concatenate([left, pair, right], axis=2)
+def halo_pieces(block):
+    left = shifted(block[:, -HALO:], "cols", 1)
+    right = shifted(block[:, :HALO], "cols", -1)
+    up = shifted(jnp.concatenate([left[-HALO:], block[-HALO:], right[-HALO:]], axis=1), "rows", 1)
+    down = shifted(jnp.concatenate([left[:HALO], block[:HALO], right[:HALO]], axis=1), "rows", -1)
+    return up, block, down, left, right
 
 
 def all_sum(x):
@@ -84,8 +83,9 @@
     return jnp.concatenate([top, bottom], axis=0)
 
 
-def tv_kernel(target_ref, kx_ref, ky_ref, fg_ref, dual_ref):
-    t = target_ref[...]
+def tv_kernel(up_ref, mid_ref, down_ref, left_ref, right_ref, kx_ref, ky_ref, fg_ref, dual_ref):
+    t = jnp.concatenate([left_ref[...], mid_ref[...], right_ref[...]], axis=1)
+    t = jnp.concatenate([up_ref[...], t, down_ref[...]], axis=0)
     rows, cols = t.shape[0], t.shape[1]
     kx = kx_ref[...]
     ky = ky_ref[...][None]
@@ -117,25 +117,27 @@
     dual_ref[...] = middle[:, HALO : HALO + width] - fg
 
 
-def tv_local(target, kx, ky, chunk, frames, into=None):
-    rows, cols, lanes = target.shape
-    inner_rows, inner_cols = rows - 2 * HALO, cols - 2 * HALO
+def tv_local(pieces, kx, ky, chunk, frames, into=None):
+    up, mid, down, left, right = pieces
+    inner_rows, inner_cols, lanes = mid.shape
+    rows, cols = inner_rows + 2 * HALO, inner_cols + 2 * HALO
     out = jax.ShapeDtypeStruct((inner_rows, inner_cols, frames), jnp.float32)
-    in_specs = [
-        pl.BlockSpec((rows, cols, lanes), lambda f: (0, 0, 0)),
-        pl.BlockSpec((rows, 1, lanes), lambda f: (0, 0, 0)),
-        pl.BlockSpec((cols, lanes), lambda f: (0, 0)),
-    ]
-    operands = [target, kx, ky]
+
+    def whole(shape):
+        return pl.BlockSpec(shape, lambda f: (0,) * len(shape))
+
+    in_specs = [whole(up.shape), whole(mid.shape), whole(down.shape), whole(left.shape), whole(right.shape)]
+    in_specs += [whole((rows, 1, lanes)), whole((cols, lanes))]
+    operands = [up, mid, down, left, right, kx, ky]
     aliases = {}
     body = tv_kernel
     if into is not None:
         in_specs += [pl.BlockSpec(memory_space=pl.ANY), pl.BlockSpec(memory_space=pl.ANY)]
         operands += list(into)
-        aliases = {3: 0, 4: 1}
+        aliases = {7: 0, 8: 1}
 
-        def body(target_ref, kx_ref, ky_ref, fg_in, dual_in, fg_ref, dual_ref):
-            tv_kernel(target_ref, kx_ref, ky_ref, fg_ref, dual_ref)
+        def body(*refs):
+            tv_kernel(*refs[:7], *refs[9:])
 
     return pl.pallas_call(
         body,
@@ -167,15 +169,15 @@
     first_col = lax.axis_index("cols") * cols_here - HALO
     g = first_row + lax.broadcasted_iota(jnp.int32, (ext_rows, 1, 1), 0)
     h = first_col + lax.broadcasted_iota(jnp.int32, (1, ext_cols, 1), 1)
+    lanes = 128 if frames % 128 == 0 else frames
     keep_x = (g >= 0) & (g <= total_rows - 2)
     keep_y = (h >= 0) & (h <= total_cols - 2)
-    lanes = 128 if frames % 128 == 0 else frames
     kx = jnp.broadcast_to(jnp.where(keep_x, 1.0, 0.0).astype(jnp.float32), (ext_rows, 1, lanes))
     ky = jnp.broadcast_to(jnp.where(keep_y, 1.0, 0.0).astype(jnp.float32)[0], (ext_cols, lanes))
     outs = None
     for chunk in range(frames // lanes):
-        piece = with_halo(target[None, :, :, chunk * lanes : (chunk + 1) * lanes])[0]
-        outs = tv_local(piece, kx, ky, chunk, frames, outs)
+        pieces = halo_pieces(target[:, :, chunk * lanes : (chunk + 1) * lanes])
+        outs = tv_local(pieces, kx, ky, chunk, frames, outs)
     new_foreground, new_dual = outs
     return (background, new_foreground, new_dual)
 

time: 128 us -> 123 us (0.961); the launches traced: 126 us -> 123 us
  waiting for transfers between devices: 39.5 us -> 35.2 us
  other arithmetic: 3.59 us -> 0.92 us
  local copies, waits for them, and re-layouts: 1.71 us -> 4.22 us
  starting transfers between devices: 38.6 us -> 40.3 us
    ppermute x8, waiting for transfers between devices: 14.1 us -> 9.71 us  [shifted(): return lax.ppermute(x, axis, pairs)]
    squeeze x2 -> x0, other arithmetic: 2.73 us -> none  [per_device(): piece = with_halo(target[None, :, :, chunk * lanes:(chunk + 1) * lanes])[0]]
    unnamed x7 -> x27, local copies, waits for them, and re-layouts: 0.17 us -> 2.54 us
    ppermute x8, starting transfers between devices: 25.1 us -> 26.8 us  [shifted(): return lax.ppermute(x, axis, pairs)]
  transfers between devices with their start and end apart: 18 -> 18, of which waited for: 10 -> 10; matrix products, arithmetic and copies ran while one was open for 2% -> 1% of each run, Pallas kernels for 7% -> 7%
where the time goes in v8:
time: 123 us
  starting transfers between devices  40.3 us (33%)
  waiting for transfers between devices  35.2 us (29%)
  matrix products  21.5 us (17%)
  Pallas kernels  18.4 us (15%)
  local copies, waits for them, and re-layouts  4.22 us (3%)
  between operations  2.6 us (2%)
    ppermute x8, starting transfers between devices, shifted(): return lax.ppermute(x, axis, pairs)  26.8 us
    ppermute x9, waiting for transfers between devices, all_sum(): lax.ppermute(x, axis, [(i, i ^ k * step) for i in range(length)])  24 us
    dot_general x39, matrix products, matmul(): jnp.dot(left, right, precision=lax.Precision.HIGHEST, preferred_element_t...  21.5 us
    pallas_call x2, Pallas kernels, tv_local(): pl.pallas_call(body, grid=(1,), in_specs=in_specs, out_specs=[pl.BlockSpe...  18.4 us
    ppermute x9, starting transfers between devices, all_sum(): lax.ppermute(x, axis, [(i, i ^ k * step) for i in range(length)])  13.4 us
    ppermute x8, waiting for transfers between devices, shifted(): return lax.ppermute(x, axis, pairs)  9.71 us
    unnamed x27, local copies, waits for them, and re-layouts  2.54 us
  transfers between devices with their start and end apart: 18, of which 10 were waited for; matrix products, arithmetic and copies ran while one was open for 1% of the time, Pallas kernels for 7%

profile of v8, /device:TPU:8, one launch (start us, length us, event | category | flops | bytes accessed | tf_op | source)
XLA Modules:
  0.0 123.0 jit_solution(16257126376729287083)
XLA Ops:
  0.6 4.5 %convolution_bitcast_fusion = f32[256,256]{0,1:T(8,128)S(1)} fusion(f32[8,128,256]{2,1,0:T(8,128)} %param.5, f32[8,128,256]{2,1,0:T(8,128)} %param.4, bf16[8,128,256]{2,1,0:T(8,128)(2,1)} %param.3), kind=kOutput, calls=%fused_computation.35 | convolution fusion | flops 806092800 | bytes 2883584 | tf_op jit(solution)/shard_map/dot_general | solution.py:28
  5.2 1.4 %collective-permute-done = f32[128,384]{0,1:T(8,128)S(1)} collective-permute-done((f32[128,384]{0,1:T(8,128)S(1)}, f32[128,384]{0,1:T(8,128)S(1)}, u32[]{:S(2)}, u32[]{:S(2)}) %collective-permute-start) | collective-permute-done | bytes 196640 | tf_op jit(solution)/shard_map/ppermute | solution.py:72
  6.7 2.8 %collective-permute-start.3 = (f32[128,384]{0,1:T(8,128)S(1)}, f32[128,384]{0,1:T(8,128)S(1)}, u32[]{:S(2)}, u32[]{:S(2)}) collective-permute-start(f32[128,384]{0,1:T(8,128)S(1)} %fusion.36), channel_id=1, source_target_pairs={{0,6},{2,4},{4,2},{6,0},{8,14},{10,12},{12,10},{14,8},{16,22},{18,... | collective-permute-start | bytes 589832 | tf_op jit(solution)/shard_map/ppermute | solution.py:69
  9.5 0.8 collective-permute-start.2
  10.3 0.5 collective-permute-start.1
  10.9 8.3 %collective-permute-done.3 = f32[128,384]{0,1:T(8,128)S(1)} collective-permute-done((f32[128,384]{0,1:T(8,128)S(1)}, f32[128,384]{0,1:T(8,128)S(1)}, u32[]{:S(2)}, u32[]{:S(2)}) %collective-permute-start.3) | collective-permute-done | bytes 196640 | tf_op jit(solution)/shard_map/ppermute | solution.py:69
  19.2 0.6 collective-permute-done.1
  19.8 4.1 %collective-permute-start.6 = (f32[128,384]{0,1:T(8,128)S(1)}, f32[128,384]{0,1:T(8,128)S(1)}, u32[]{:S(2)}, u32[]{:S(2)}) collective-permute-start(f32[128,384]{0,1:T(8,128)S(1)} %add_add_fusion.2), channel_id=1, source_target_pairs={{0,24},{2,26},{4,28},{6,30},{8,16},{10,18},{12,20},{14,22},{16,8},... | collective-permute-start | bytes 589832 | tf_op jit(solution)/shard_map/ppermute | solution.py:69
  23.9 0.9 collective-permute-start.4
  24.9 6.6 %collective-permute-done.6 = f32[128,384]{0,1:T(8,128)S(1)} collective-permute-done((f32[128,384]{0,1:T(8,128)S(1)}, f32[128,384]{0,1:T(8,128)S(1)}, u32[]{:S(2)}, u32[]{:S(2)}) %collective-permute-start.6) | collective-permute-done | bytes 196640 | tf_op jit(solution)/shard_map/ppermute | solution.py:69
  31.5 1.6 %collective-permute-done.5 = f32[128,384]{0,1:T(8,128)S(1)} collective-permute-done((f32[128,384]{0,1:T(8,128)S(1)}, f32[128,384]{0,1:T(8,128)S(1)}, u32[]{:S(2)}, u32[]{:S(2)}) %collective-permute-start.5) | collective-permute-done | bytes 196640 | tf_op jit(solution)/shard_map/ppermute | solution.py:69
  33.2 1.7 %collective-permute-start.9 = (f32[128,384]{0,1:T(8,128)S(1)}, f32[128,384]{0,1:T(8,128)S(1)}, u32[]{:S(2)}, u32[]{:S(2)}) collective-permute-start(f32[128,384]{0,1:T(8,128)S(1)} %add_add_fusion.1), channel_id=1, source_target_pairs={{0,96},{2,98},{4,100},{6,102},{8,104},{10,106},{12,108},{14,110},{... | collective-permute-start | bytes 589832 | tf_op jit(solution)/shard_map/ppermute | solution.py:69
  34.9 0.9 collective-permute-start.8
  35.8 1.6 %collective-permute-start.7 = (f32[128,384]{0,1:T(8,128)S(1)}, f32[128,384]{0,1:T(8,128)S(1)}, u32[]{:S(2)}, u32[]{:S(2)}) collective-permute-start(f32[128,384]{0,1:T(8,128)S(1)} %add_add_fusion.1), channel_id=1, source_target_pairs={{0,32},{2,34},{4,36},{6,38},{8,40},{10,42},{12,44},{14,46},{16,48}... | collective-permute-start | bytes 589832 | tf_op jit(solution)/shard_map/ppermute | solution.py:69
  37.4 4.5 %collective-permute-done.9 = f32[128,384]{0,1:T(8,128)S(1)} collective-permute-done((f32[128,384]{0,1:T(8,128)S(1)}, f32[128,384]{0,1:T(8,128)S(1)}, u32[]{:S(2)}, u32[]{:S(2)}) %collective-permute-start.9) | collective-permute-done | bytes 196640 | tf_op jit(solution)/shard_map/ppermute | solution.py:69
  41.9 1.2 collective-permute-done.8
  43.1 1.1 collective-permute-done.7
  44.4 0.7 multiply_reduce_fusion
  46.1 0.6 fusion.29
  47.0 0.4 fusion.14
  47.4 0.4 fusion.41
  47.8 0.4 fusion.40
  48.2 0.4 fusion.13
  48.9 0.4 fusion.42
  49.3 0.4 fusion.12
  49.7 0.4 fusion.45
  50.5 0.4 fusion.11
  51.3 0.4 fusion.46
  51.6 0.4 fusion.10
  52.0 0.4 fusion.49
  52.8 0.4 fusion.9
  53.6 0.4 fusion.50
  54.0 0.4 fusion.8
  54.4 1.0 select_reduce_fusion
  56.0 0.4 fusion.7
  56.4 0.4 fusion.20
  56.8 0.4 fusion.6
  57.6 0.4 fusion.5
  58.0 0.4 fusion.53
  58.4 0.4 fusion.4
  59.1 0.4 fusion.3
  59.5 0.6 fusion.55
  60.1 0.4 fusion.2
  60.6 0.4 fusion.56
  60.9 0.4 fusion.16
  61.3 0.4 fusion
  62.1 2.0 %fusion.18 = (f32[8,128,256]{2,1,0:T(8,128)S(1)}, f32[8,128,256]{2,1,0:T(8,128)}) fusion(f32[8,128,256]{2,1,0:T(8,128)S(1)} %copy-done.2, bf16[8,128,256]{2,1,0:T(8,128)(2,1)S(1)} %copy-done.4, f32[256,256,1]{1,0,2:T(8,128)S(1)} %fusion, f32[8,128,256]{2,1,0:T(8,128)S(1)} %copy-done.3), kind=kOutput, calls=%fused_computation.37 | convolution fusion | flops 806879232 | bytes 4980736 | tf_op jit(solution)/shard_map/dot_general | solution.py:28
  64.1 1.3 %collective-permute-start.14 = (f32[8,8,128]{2,1,0:T(8,128)S(1)}, f32[8,8,128]{2,1,0:T(8,128)S(1)}, u32[]{:S(2)}, u32[]{:S(2)}) collective-permute-start(f32[8,8,128]{2,1,0:T(8,128)S(1)} %get-tuple-element.11), channel_id=1, source_target_pairs={{0,1},{2,3},{4,5},{6,7},{8,9},{10,11},{12,13},{14,15},{16,17},{18,... | collective-permute-start | bytes 98312 | tf_op jit(solution)/shard_map/ppermute | solution.py:24
  65.4 1.3 %collective-permute-start.15 = (f32[8,8,128]{2,1,0:T(8,128)S(1)}, f32[8,8,128]{2,1,0:T(8,128)S(1)}, u32[]{:S(2)}, u32[]{:S(2)}) collective-permute-start(f32[8,8,128]{2,1,0:T(8,128)S(1)} %get-tuple-element.12), channel_id=1, source_target_pairs={{1,0},{3,2},{5,4},{7,6},{9,8},{11,10},{13,12},{15,14},{17,16},{19,... | collective-permute-start | bytes 98312 | tf_op jit(solution)/shard_map/ppermute | solution.py:24
  66.9 1.3 %collective-permute-start.11 = (f32[8,8,128]{2,1,0:T(8,128)S(1)}, f32[8,8,128]{2,1,0:T(8,128)S(1)}, u32[]{:S(2)}, u32[]{:S(2)}) collective-permute-start(f32[8,8,128]{2,1,0:T(8,128)S(1)} %get-tuple-element.13), channel_id=1, source_target_pairs={{1,0},{3,2},{5,4},{7,6},{9,8},{11,10},{13,12},{15,14},{17,16},{19,... | collective-permute-start | bytes 98312 | tf_op jit(solution)/shard_map/ppermute | solution.py:24
  68.2 3.0 %collective-permute-start.10 = (f32[8,8,128]{2,1,0:T(8,128)S(1)}, f32[8,8,128]{2,1,0:T(8,128)S(1)}, u32[]{:S(2)}, u32[]{:S(2)}) collective-permute-start(f32[8,8,128]{2,1,0:T(8,128)S(1)} %get-tuple-element.14), channel_id=1, source_target_pairs={{0,1},{2,3},{4,5},{6,7},{8,9},{10,11},{12,13},{14,15},{16,17},{18,... | collective-permute-start | bytes 98312 | tf_op jit(solution)/shard_map/ppermute | solution.py:24
  71.3 0.5 copy-done.11
  71.8 7.9 %collective-permute-start.17 = (f32[8,144,128]{2,1,0:T(8,128)S(1)}, f32[8,144,128]{2,1,0:T(8,128)S(1)}, u32[]{:S(2)}, u32[]{:S(2)}) collective-permute-start(f32[8,144,128]{2,1,0:T(8,128)S(1)} %pad_maximum_fusion.1), channel_id=1, source_target_pairs={{2,0},{4,2},{6,4},{8,6},{10,8},{12,10},{14,12},{16,14},{18,16},{20... | collective-permute-start | bytes 1769480 | tf_op jit(solution)/shard_map/ppermute | solution.py:24
  79.8 1.9 %collective-permute-start.16 = (f32[8,144,128]{2,1,0:T(8,128)S(1)}, f32[8,144,128]{2,1,0:T(8,128)S(1)}, u32[]{:S(2)}, u32[]{:S(2)}) collective-permute-start(f32[8,144,128]{2,1,0:T(8,128)S(1)} %pad_maximum_fusion.1), channel_id=1, source_target_pairs={{0,2},{2,4},{4,6},{6,8},{8,10},{10,12},{12,14},{14,16},{16,18},{18... | collective-permute-start | bytes 1769480 | tf_op jit(solution)/shard_map/ppermute | solution.py:24
  81.8 0.5 copy-done.9
  82.3 8.1 %collective-permute-start.13 = (f32[8,144,128]{2,1,0:T(8,128)S(1)}, f32[8,144,128]{2,1,0:T(8,128)S(1)}, u32[]{:S(2)}, u32[]{:S(2)}) collective-permute-start(f32[8,144,128]{2,1,0:T(8,128)S(1)} %pad_maximum_fusion), channel_id=1, source_target_pairs={{2,0},{4,2},{6,4},{8,6},{10,8},{12,10},{14,12},{16,14},{18,16},{20... | collective-permute-start | bytes 1769480 | tf_op jit(solution)/shard_map/ppermute | solution.py:24
  90.5 1.9 %collective-permute-start.12 = (f32[8,144,128]{2,1,0:T(8,128)S(1)}, f32[8,144,128]{2,1,0:T(8,128)S(1)}, u32[]{:S(2)}, u32[]{:S(2)}) collective-permute-start(f32[8,144,128]{2,1,0:T(8,128)S(1)} %pad_maximum_fusion), channel_id=1, source_target_pairs={{0,2},{2,4},{4,6},{6,8},{8,10},{10,12},{12,14},{14,16},{16,18},{18... | collective-permute-start | bytes 1769480 | tf_op jit(solution)/shard_map/ppermute | solution.py:24
  92.4 1.0 collective-permute-done.17.down_ref
  93.5 8.6 %collective-permute-done.16.up_ref = f32[8,144,128]{2,1,0:T(8,128)S(1)} collective-permute-done((f32[8,144,128]{2,1,0:T(8,128)S(1)}, f32[8,144,128]{2,1,0:T(8,128)S(1)}, u32[]{:S(2)}, u32[]{:S(2)}) %collective-permute-start.16) | collective-permute-done | bytes 589856 | tf_op jit(solution)/shard_map/ppermute | solution.py:24
  102.1 0.8 broadcast_in_dim.30.kx_ref.refs_5_
  102.9 0.7 broadcast_in_dim.33.ky_ref.refs_6_
  103.6 9.2 %shard_map.58 = (f32[8,128,256]{2,1,0:T(8,128)}, f32[8,128,256]{2,1,0:T(8,128)}) custom-call(f32[8,144,128]{2,1,0:T(8,128)} %copy-done.6, f32[8,128,128]{2,1,0:T(8,128)} %copy-done.1, f32[8,144,128]{2,1,0:T(8,128)} %copy-done.5, f32[8,8,128]{2,1,0:T(8,128)} %copy-done.11, f32[8,8,128]{2,1,0:T(8,128)} %copy-done.12, ...), custom_call_target="tpu_custom_call" | custom-call | tf_op jit(solution)/shard_map/pallas_call | solution.py:142
  112.9 0.8 copy-done.7
  113.8 9.2 %shard_map.59 = (f32[8,128,256]{2,1,0:T(8,128)}, f32[8,128,256]{2,1,0:T(8,128)}) custom-call(f32[8,144,128]{2,1,0:T(8,128)} %copy-done.8, f32[8,128,128]{2,1,0:T(8,128)} %copy-done, f32[8,144,128]{2,1,0:T(8,128)} %copy-done.7, f32[8,8,128]{2,1,0:T(8,128)} %copy-done.10, f32[8,8,128]{2,1,0:T(8,128)} %copy-done.9, ...), custom_call_target="tpu_custom_call", output_to_operand_aliasing={{0}: (7, {}), {1}: (8, {})} | custom-call | tf_op jit(solution)/shard_map/pallas_call | solution.py:142
  (58 shorter events, 4.5 us)
Async XLA Ops:
  5.2 1.5 %collective-permute-start = (f32[128,384]{0,1:T(8,128)S(1)}, f32[128,384]{0,1:T(8,128)S(1)}, u32[]{:S(2)}, u32[]{:S(2)}) collective-permute-start(f32[128,384]{0,1:T(8,128)S(1)} %pad_maximum_fusion.2), channel_id=1, source_target_pairs={{0,1},{1,0},{2,3},{3,2},{4,5},{5,4},{6,7},{7,6},{8,9},{9,8},{10,11... | collective-permute-start | bytes 589832 | tf_op jit(solution)/shard_map/ppermute | solution.py:72
  6.7 12.4 %collective-permute-start.3 = (f32[128,384]{0,1:T(8,128)S(1)}, f32[128,384]{0,1:T(8,128)S(1)}, u32[]{:S(2)}, u32[]{:S(2)}) collective-permute-start(f32[128,384]{0,1:T(8,128)S(1)} %fusion.36), channel_id=1, source_target_pairs={{0,6},{2,4},{4,2},{6,0},{8,14},{10,12},{12,10},{14,8},{16,22},{18,... | collective-permute-start | bytes 589832 | tf_op jit(solution)/shard_map/ppermute | solution.py:69
  9.5 9.6 %collective-permute-start.2 = (f32[128,384]{0,1:T(8,128)S(1)}, f32[128,384]{0,1:T(8,128)S(1)}, u32[]{:S(2)}, u32[]{:S(2)}) collective-permute-start(f32[128,384]{0,1:T(8,128)S(1)} %fusion.36), channel_id=1, source_target_pairs={{0,4},{2,6},{4,0},{6,2},{8,12},{10,14},{12,8},{14,10},{16,20},{18,... | collective-permute-start | bytes 589832 | tf_op jit(solution)/shard_map/ppermute | solution.py:69
  10.3 9.4 %collective-permute-start.1 = (f32[128,384]{0,1:T(8,128)S(1)}, f32[128,384]{0,1:T(8,128)S(1)}, u32[]{:S(2)}, u32[]{:S(2)}) collective-permute-start(f32[128,384]{0,1:T(8,128)S(1)} %fusion.36), channel_id=1, source_target_pairs={{0,2},{2,0},{4,6},{6,4},{8,10},{10,8},{12,14},{14,12},{16,18},{18,... | collective-permute-start | bytes 589832 | tf_op jit(solution)/shard_map/ppermute | solution.py:69
  19.8 11.7 %collective-permute-start.6 = (f32[128,384]{0,1:T(8,128)S(1)}, f32[128,384]{0,1:T(8,128)S(1)}, u32[]{:S(2)}, u32[]{:S(2)}) collective-permute-start(f32[128,384]{0,1:T(8,128)S(1)} %add_add_fusion.2), channel_id=1, source_target_pairs={{0,24},{2,26},{4,28},{6,30},{8,16},{10,18},{12,20},{14,22},{16,8},... | collective-permute-start | bytes 589832 | tf_op jit(solution)/shard_map/ppermute | solution.py:69
  23.9 9.2 %collective-permute-start.5 = (f32[128,384]{0,1:T(8,128)S(1)}, f32[128,384]{0,1:T(8,128)S(1)}, u32[]{:S(2)}, u32[]{:S(2)}) collective-permute-start(f32[128,384]{0,1:T(8,128)S(1)} %add_add_fusion.2), channel_id=1, source_target_pairs={{0,16},{2,18},{4,20},{6,22},{8,24},{10,26},{12,28},{14,30},{16,0},... | collective-permute-start | bytes 589832 | tf_op jit(solution)/shard_map/ppermute | solution.py:69
  23.9 9.2 %collective-permute-start.4 = (f32[128,384]{0,1:T(8,128)S(1)}, f32[128,384]{0,1:T(8,128)S(1)}, u32[]{:S(2)}, u32[]{:S(2)}) collective-permute-start(f32[128,384]{0,1:T(8,128)S(1)} %add_add_fusion.2), channel_id=1, source_target_pairs={{0,8},{2,10},{4,12},{6,14},{8,0},{10,2},{12,4},{14,6},{16,24},{18,... | collective-permute-start | bytes 589832 | tf_op jit(solution)/shard_map/ppermute | solution.py:69
  33.2 8.7 %collective-permute-start.9 = (f32[128,384]{0,1:T(8,128)S(1)}, f32[128,384]{0,1:T(8,128)S(1)}, u32[]{:S(2)}, u32[]{:S(2)}) collective-permute-start(f32[128,384]{0,1:T(8,128)S(1)} %add_add_fusion.1), channel_id=1, source_target_pairs={{0,96},{2,98},{4,100},{6,102},{8,104},{10,106},{12,108},{14,110},{... | collective-permute-start | bytes 589832 | tf_op jit(solution)/shard_map/ppermute | solution.py:69
  34.9 8.2 %collective-permute-start.8 = (f32[128,384]{0,1:T(8,128)S(1)}, f32[128,384]{0,1:T(8,128)S(1)}, u32[]{:S(2)}, u32[]{:S(2)}) collective-permute-start(f32[128,384]{0,1:T(8,128)S(1)} %add_add_fusion.1), channel_id=1, source_target_pairs={{0,64},{2,66},{4,68},{6,70},{8,72},{10,74},{12,76},{14,78},{16,80}... | collective-permute-start | bytes 589832 | tf_op jit(solution)/shard_map/ppermute | solution.py:69
  35.8 8.4 %collective-permute-start.7 = (f32[128,384]{0,1:T(8,128)S(1)}, f32[128,384]{0,1:T(8,128)S(1)}, u32[]{:S(2)}, u32[]{:S(2)}) collective-permute-start(f32[128,384]{0,1:T(8,128)S(1)} %add_add_fusion.1), channel_id=1, source_target_pairs={{0,32},{2,34},{4,36},{6,38},{8,40},{10,42},{12,44},{14,46},{16,48}... | collective-permute-start | bytes 589832 | tf_op jit(solution)/shard_map/ppermute | solution.py:69
  60.1 1.6 %copy-start.4 = (bf16[8,128,256]{2,1,0:T(8,128)(2,1)S(1)}, bf16[8,128,256]{2,1,0:T(8,128)(2,1)}, u32[]{:S(2)}) copy-start(bf16[8,128,256]{2,1,0:T(8,128)(2,1)} %param.3) | copy-start | bytes 1572868
  60.5 1.3 %copy-start.2 = (f32[8,128,256]{2,1,0:T(8,128)S(1)}, f32[8,128,256]{2,1,0:T(8,128)}, u32[]{:S(2)}) copy-start(f32[8,128,256]{2,1,0:T(8,128)} %param.5) | copy-start | bytes 3145732
  60.5 1.6 %copy-start.3 = (f32[8,128,256]{2,1,0:T(8,128)S(1)}, f32[8,128,256]{2,1,0:T(8,128)}, u32[]{:S(2)}) copy-start(f32[8,128,256]{2,1,0:T(8,128)} %param.4) | copy-start | bytes 3145732
  64.1 7.1 %collective-permute-start.14 = (f32[8,8,128]{2,1,0:T(8,128)S(1)}, f32[8,8,128]{2,1,0:T(8,128)S(1)}, u32[]{:S(2)}, u32[]{:S(2)}) collective-permute-start(f32[8,8,128]{2,1,0:T(8,128)S(1)} %get-tuple-element.11), channel_id=1, source_target_pairs={{0,1},{2,3},{4,5},{6,7},{8,9},{10,11},{12,13},{14,15},{16,17},{18,... | collective-permute-start | bytes 98312 | tf_op jit(solution)/shard_map/ppermute | solution.py:24
  65.4 5.8 %collective-permute-start.15 = (f32[8,8,128]{2,1,0:T(8,128)S(1)}, f32[8,8,128]{2,1,0:T(8,128)S(1)}, u32[]{:S(2)}, u32[]{:S(2)}) collective-permute-start(f32[8,8,128]{2,1,0:T(8,128)S(1)} %get-tuple-element.12), channel_id=1, source_target_pairs={{1,0},{3,2},{5,4},{7,6},{9,8},{11,10},{13,12},{15,14},{17,16},{19,... | collective-permute-start | bytes 98312 | tf_op jit(solution)/shard_map/ppermute | solution.py:24
  66.8 4.4 %copy-start.1 = (f32[8,128,128]{2,1,0:T(8,128)}, f32[8,128,128]{2,1,0:T(8,128)S(1)}, u32[]{:S(2)}) copy-start(f32[8,128,128]{2,1,0:T(8,128)S(1)} %get-tuple-element.15.mid_ref) | copy-start | bytes 1572868
  66.9 14.9 %copy-start = (f32[8,128,128]{2,1,0:T(8,128)}, f32[8,128,128]{2,1,0:T(8,128)S(1)}, u32[]{:S(2)}) copy-start(f32[8,128,128]{2,1,0:T(8,128)S(1)} %get-tuple-element.16.refs_1_) | copy-start | bytes 1572868
  66.9 14.8 %collective-permute-start.11 = (f32[8,8,128]{2,1,0:T(8,128)S(1)}, f32[8,8,128]{2,1,0:T(8,128)S(1)}, u32[]{:S(2)}, u32[]{:S(2)}) collective-permute-start(f32[8,8,128]{2,1,0:T(8,128)S(1)} %get-tuple-element.13), channel_id=1, source_target_pairs={{1,0},{3,2},{5,4},{7,6},{9,8},{11,10},{13,12},{15,14},{17,16},{19,... | collective-permute-start | bytes 98312 | tf_op jit(solution)/shard_map/ppermute | solution.py:24
  68.2 13.6 %collective-permute-start.10 = (f32[8,8,128]{2,1,0:T(8,128)S(1)}, f32[8,8,128]{2,1,0:T(8,128)S(1)}, u32[]{:S(2)}, u32[]{:S(2)}) collective-permute-start(f32[8,8,128]{2,1,0:T(8,128)S(1)} %get-tuple-element.14), channel_id=1, source_target_pairs={{0,1},{2,3},{4,5},{6,7},{8,9},{10,11},{12,13},{14,15},{16,17},{18,... | collective-permute-start | bytes 98312 | tf_op jit(solution)/shard_map/ppermute | solution.py:24
  71.2 0.6 copy-start.11
  71.2 0.6 copy-start.12
  71.8 21.6 %collective-permute-start.17 = (f32[8,144,128]{2,1,0:T(8,128)S(1)}, f32[8,144,128]{2,1,0:T(8,128)S(1)}, u32[]{:S(2)}, u32[]{:S(2)}) collective-permute-start(f32[8,144,128]{2,1,0:T(8,128)S(1)} %pad_maximum_fusion.1), channel_id=1, source_target_pairs={{2,0},{4,2},{6,4},{8,6},{10,8},{12,10},{14,12},{16,14},{18,16},{20... | collective-permute-start | bytes 1769480 | tf_op jit(solution)/shard_map/ppermute | solution.py:24
  79.8 22.3 %collective-permute-start.16 = (f32[8,144,128]{2,1,0:T(8,128)S(1)}, f32[8,144,128]{2,1,0:T(8,128)S(1)}, u32[]{:S(2)}, u32[]{:S(2)}) collective-permute-start(f32[8,144,128]{2,1,0:T(8,128)S(1)} %pad_maximum_fusion.1), channel_id=1, source_target_pairs={{0,2},{2,4},{4,6},{6,8},{8,10},{10,12},{12,14},{14,16},{16,18},{18... | collective-permute-start | bytes 1769480 | tf_op jit(solution)/shard_map/ppermute | solution.py:24
  81.7 0.6 copy-start.9
  81.7 0.6 copy-start.10
  82.3 30.5 %collective-permute-start.13 = (f32[8,144,128]{2,1,0:T(8,128)S(1)}, f32[8,144,128]{2,1,0:T(8,128)S(1)}, u32[]{:S(2)}, u32[]{:S(2)}) collective-permute-start(f32[8,144,128]{2,1,0:T(8,128)S(1)} %pad_maximum_fusion), channel_id=1, source_target_pairs={{2,0},{4,2},{6,4},{8,6},{10,8},{12,10},{14,12},{16,14},{18,16},{20... | collective-permute-start | bytes 1769480 | tf_op jit(solution)/shard_map/ppermute | solution.py:24
  90.5 22.4 %collective-permute-start.12 = (f32[8,144,128]{2,1,0:T(8,128)S(1)}, f32[8,144,128]{2,1,0:T(8,128)S(1)}, u32[]{:S(2)}, u32[]{:S(2)}) collective-permute-start(f32[8,144,128]{2,1,0:T(8,128)S(1)} %pad_maximum_fusion), channel_id=1, source_target_pairs={{0,2},{2,4},{4,6},{6,8},{8,10},{10,12},{12,14},{14,16},{16,18},{18... | collective-permute-start | bytes 1769480 | tf_op jit(solution)/shard_map/ppermute | solution.py:24
  93.5 10.2 %copy-start.5 = (f32[8,144,128]{2,1,0:T(8,128)}, f32[8,144,128]{2,1,0:T(8,128)S(1)}, u32[]{:S(2)}) copy-start(f32[8,144,128]{2,1,0:T(8,128)S(1)} %collective-permute-done.17.down_ref) | copy-start | bytes 1769476
  102.1 1.5 %copy-start.6 = (f32[8,144,128]{2,1,0:T(8,128)}, f32[8,144,128]{2,1,0:T(8,128)S(1)}, u32[]{:S(2)}) copy-start(f32[8,144,128]{2,1,0:T(8,128)S(1)} %collective-permute-done.16.up_ref) | copy-start | bytes 1769476
  112.8 0.8 copy-start.7
  112.9 1.0 copy-start.8
